TPU v7x, 32 devices: a whole 2x2x4 slice. The times are simulated.
32 devices in a mesh: off: 16 (over z, y, x), dep: 2 (over core).
Axes of the slice: x: 2, y: 2, z: 4, core: 2. Of those that a mesh axis runs over, the one named last changes fastest.
Arguments:
- snapshots: bfloat16 [16, 8, 64, 256], P('off', 'dep'), may hold values from -6 to 6
- reflect: bfloat16 [192, 8, 64, 256], P('off', 'dep'), may hold values from -0.4375 to 0.4375
- courant: float32 [8, 64, 256], P('dep'), may hold values from 0.03 to 0.18
- lags: int32 [192], P('off'), may hold values from -32 to 32, as said below
- owners: int32 [8], replicated, may hold values from 0 to 15, as said below
Outputs:
- scattered: float32 [8, 64, 256], P('dep')
Inputs may be any that keep to these rules, and one draw needn't show every extreme that they name: `lags`: some offset has lag -32 and some offset has lag 32. `owners`: some step uses wavefield 0 and some step uses wavefield 16 - 1.
All inputs are finite; a program needn't handle non-finite values.
Results may differ from a plain program's by a relative error of at most 0.0003.
Values may be sent and summed in bfloat16 or wider, within the bound.
No kernel may reach another device: no remote copies, remote signals or barrier semaphores. Data moves between devices by JAX's collectives and lax.ppermute only.
A program may use at most 64 MiB of HBM per device.

v0:
```python
import jax
import jax.numpy as jnp
from jax import lax
from jax.sharding import PartitionSpec as P

ITERS = 8
LAG = 32


STENCIL_WEIGHTS = (-205.0 / 72.0, 8.0 / 5.0, -1.0 / 5.0, 8.0 / 315.0, -1.0 / 560.0)


def extended(cells, sides, width):
    for axis, dim in sides:
        count = lax.axis_size(axis)
        ends = count - 1
        head = lax.slice_in_dim(cells, 0, width, axis=dim)
        tail = lax.slice_in_dim(cells, cells.shape[dim] - width, cells.shape[dim], axis=dim)
        cells = jnp.concatenate(
            [
                lax.ppermute(tail, axis, [(i, (i + 1) % count) for i in range(ends)]),
                cells,
                lax.ppermute(head, axis, [((i + 1) % count, i) for i in range(ends)]),
            ],
            axis=dim,
        )
    return cells


def broadcast(x, axis, root):
    mine = lax.axis_index(axis) == root
    return lax.psum(jnp.where(mine, x, jnp.zeros_like(x)), axis)


def stencil(padded, depth_cells, row_cells, column_cells):
    center = padded[4 : 4 + depth_cells, 4 : 4 + row_cells, 4 : 4 + column_cells]
    summed = 3.0 * STENCIL_WEIGHTS[0] * center
    for distance in range(1, 5):
        neighbours = (
            padded[
                4 + distance : 4 + distance + depth_cells, 4 : 4 + row_cells, 4 : 4 + column_cells
            ]
            + padded[
                4 - distance : 4 - distance + depth_cells, 4 : 4 + row_cells, 4 : 4 + column_cells
            ]
        )
        neighbours = (
            neighbours
            + padded[
                4 : 4 + depth_cells, 4 + distance : 4 + distance + row_cells, 4 : 4 + column_cells
            ]
            + padded[
                4 : 4 + depth_cells, 4 - distance : 4 - distance + row_cells, 4 : 4 + column_cells
            ]
        )
        neighbours = (
            neighbours
            + padded[
                4 : 4 + depth_cells, 4 : 4 + row_cells, 4 + distance : 4 + distance + column_cells
            ]
            + padded[
                4 : 4 + depth_cells, 4 : 4 + row_cells, 4 - distance : 4 - distance + column_cells
            ]
        )
        summed = summed + STENCIL_WEIGHTS[distance] * neighbours
    return summed


def shifted_sum(reflect, acceleration, lags):
    width_cells = acceleration.shape[2]
    padded = jnp.pad(acceleration, ((0, 0), (0, 0), (LAG, LAG)))

    def add_offset(offset_index, summed):
        lag_now = lags[offset_index]
        window = lax.dynamic_slice_in_dim(padded, LAG - lag_now, width_cells, 2)
        return summed + reflect[offset_index].astype(jnp.float32) * window

    return lax.fori_loop(
        0, reflect.shape[0], add_offset, jnp.zeros(acceleration.shape, jnp.float32)
    )


def accelerate(rimmed, courant):
    padded = jnp.pad(rimmed, ((0, 0), (4, 4), (4, 4))).astype(jnp.float32)
    return courant * stencil(padded, courant.shape[0], courant.shape[1], courant.shape[2])


def per_device(snapshots, reflect, courant, lags, owners):
    depth_cells = courant.shape[0]
    row_cells = courant.shape[1]
    column_cells = courant.shape[2]
    own_layers = extended(snapshots[0], (("dep", 0),), 4)
    own_ready = accelerate(own_layers, courant)
    scattered = jnp.zeros((depth_cells, row_cells, column_cells), jnp.float32)
    previous = jnp.zeros((depth_cells, row_cells, column_cells), jnp.float32)
    for step_now in range(ITERS):
        acceleration = broadcast(own_ready, "off", owners[step_now])
        local_source = shifted_sum(reflect, acceleration, lags)
        source = lax.psum(local_source, "off")
        field_padded = extended(scattered, (("dep", 0),), 4)
        field_padded = jnp.pad(field_padded, ((0, 0), (4, 4), (4, 4)))
        updated = (
            2.0 * scattered
            - previous
            + courant * stencil(field_padded, depth_cells, row_cells, column_cells)
            + source
        )
        previous = scattered
        scattered = updated
    return scattered


def solution(mesh):
    in_specs = (
        P("off", "dep", None, None),
        P("off", "dep", None, None),
        P("dep", None, None),
        P("off"),
        P(),
    )
    out_specs = P("dep", None, None)
    return jax.shard_map(
        per_device, mesh=mesh, in_specs=in_specs, out_specs=out_specs, check_vma=False
    )
```

profile of v0, /device:TPU:0, one launch (start us, length us, event | category | flops | bytes accessed | tf_op | source)
XLA Modules:
  0.0 623.1 jit_solution(5807188864670514048)
XLA Ops:
  6.5 2.5 collective-permute-start.2
  18.4 2.4 broadcast_select_fusion.7
  22.3 130.4 %all-reduce.26.cloned.1.call-done = (f32[4,64,256]{2,1,0:T(8,128)}, f32[4,64,256]{2,1,0:T(8,128)}, f32[4,64,256]{2,1,0:T(8,128)}, f32[4,64,256]{2,1,0:T(8,128)},...) async-done(((f32[4,64,256]{2,1,0:T(8,128)}, f32[4,64,256]{2,1,0:T(8,128)}, f32[4,64,256]{2,1,0:T(8,128)}, ...) | async-done | bytes 2097168 | tf_op jit(solution)/shard_map/psum | solution.py:32
  154.5 47.3 %while.128 = (s32[]{:T(128)}, f32[4,64,256]{2,1,0:T(8,128)}, bf16[12,4,64,256]{3,2,1,0:T(8,128)(2,1)S(1)}, s32[12]{0:T(128)S(1)}, f32[4,64,320]{2,1,0:T(8,128)},...) while((s32[]{:T(128)}, f32[4,64,256]{2,1,0:T(8,128)}, ...), condition=%wide.region_2.3_spmd.clone, body=%wide.region_1.2_spmd.clone.sunk | while | flops 262151 | bytes 917673 | solution.py:78
  203.7 43.8 %while.129 = (s32[]{:T(128)}, f32[4,64,256]{2,1,0:T(8,128)}, bf16[12,4,64,256]{3,2,1,0:T(8,128)(2,1)S(1)}, s32[12]{0:T(128)S(1)}, f32[4,64,320]{2,1,0:T(8,128)},...) while((s32[]{:T(128)}, f32[4,64,256]{2,1,0:T(8,128)}, ...), condition=%wide.region_6.7_spmd.clone, body=%wide.region_5.6_spmd.clone.sunk | while | flops 262151 | bytes 917673 | solution.py:78
  209.0 1.9 fusion.239
  212.6 1.9 fusion.239
  219.9 1.9 fusion.239
  223.6 1.9 fusion.239
  227.3 1.9 fusion.239
  230.9 1.9 fusion.239
  234.6 1.9 fusion.239
  238.2 1.9 fusion.239
  241.9 1.9 fusion.239
  245.6 1.9 fusion.239
  249.4 34.8 %while.130 = (s32[]{:T(128)}, f32[4,64,256]{2,1,0:T(8,128)S(1)}, bf16[12,4,64,256]{3,2,1,0:T(8,128)(2,1)S(1)}, s32[12]{0:T(128)S(1)}, f32[4,64,320]{2,1,0:T(8,12...) while((s32[]{:T(128)}, f32[4,64,256]{2,1,0:T(8,128)S(1)}, ...), condition=%wide.region_10.11_spmd.clone, body=%wide.region_9.10_spmd.clone.sunk | while | flops 262151 | bytes 917673 | solution.py:78
  284.2 2.0 pad.68
  286.1 37.1 %while.131 = (s32[]{:T(128)}, f32[4,64,256]{2,1,0:T(8,128)S(1)}, bf16[12,4,64,256]{3,2,1,0:T(8,128)(2,1)S(1)}, s32[12]{0:T(128)S(1)}, f32[4,64,320]{2,1,0:T(8,12...) while((s32[]{:T(128)}, f32[4,64,256]{2,1,0:T(8,128)S(1)}, ...), condition=%wide.region_14.15_spmd.clone, body=%wide.region_13.14_spmd.clone.sunk | while | flops 262151 | bytes 917673 | solution.py:78
  324.5 27.2 %while.132 = (s32[]{:T(128)}, f32[4,64,256]{2,1,0:T(8,128)S(1)}, bf16[12,4,64,256]{3,2,1,0:T(8,128)(2,1)S(1)}, s32[12]{0:T(128)S(1)}, f32[4,64,320]{2,1,0:T(8,12...) while((s32[]{:T(128)}, f32[4,64,256]{2,1,0:T(8,128)S(1)}, ...), condition=%wide.region_18.19_spmd.clone, body=%wide.region_17.18_spmd.clone.sunk | while | flops 262151 | bytes 917673 | solution.py:78
  353.0 27.2 %while.133 = (s32[]{:T(128)}, f32[4,64,256]{2,1,0:T(8,128)S(1)}, bf16[12,4,64,256]{3,2,1,0:T(8,128)(2,1)S(1)}, s32[12]{0:T(128)S(1)}, f32[4,64,320]{2,1,0:T(8,12...) while((s32[]{:T(128)}, f32[4,64,256]{2,1,0:T(8,128)S(1)}, ...), condition=%wide.region_22.23_spmd.clone, body=%wide.region_21.22_spmd.clone.sunk | while | flops 262151 | bytes 917673 | solution.py:78
  380.9 27.2 %while.134 = (s32[]{:T(128)}, f32[4,64,256]{2,1,0:T(8,128)S(1)}, bf16[12,4,64,256]{3,2,1,0:T(8,128)(2,1)S(1)}, s32[12]{0:T(128)S(1)}, f32[4,64,320]{2,1,0:T(8,12...) while((s32[]{:T(128)}, f32[4,64,256]{2,1,0:T(8,128)S(1)}, ...), condition=%wide.region_26.27_spmd.clone, body=%wide.region_25.26_spmd.clone.sunk | while | flops 262151 | bytes 917673 | solution.py:78
  408.8 27.2 %while.135 = (s32[]{:T(128)}, f32[4,64,256]{2,1,0:T(8,128)S(1)}, bf16[12,4,64,256]{3,2,1,0:T(8,128)(2,1)S(1)}, s32[12]{0:T(128)S(1)}, f32[4,64,320]{2,1,0:T(8,12...) while((s32[]{:T(128)}, f32[4,64,256]{2,1,0:T(8,128)S(1)}, ...), condition=%wide.region_30.31_spmd.clone, body=%wide.region_29.30_spmd.clone.sunk | while | flops 262151 | bytes 917673 | solution.py:78
  438.1 3.1 collective-permute-start.1
  442.7 120.5 %all-reduce.24.cloned.1.call-done = (f32[4,64,256]{2,1,0:T(8,128)}, f32[4,64,256]{2,1,0:T(8,128)}, f32[4,64,256]{2,1,0:T(8,128)}, f32[4,64,256]{2,1,0:T(8,128)},...) async-done(((f32[4,64,256]{2,1,0:T(8,128)}, f32[4,64,256]{2,1,0:T(8,128)}, f32[4,64,256]{2,1,0:T(8,128)}, ...) | async-done | bytes 2097168 | tf_op jit(solution)/shard_map/psum | solution.py:99
  563.3 2.0 fusion.184
  566.8 3.1 collective-permute-start.5
  573.9 3.1 collective-permute-start.7
  581.1 3.2 collective-permute-start.9
  588.3 3.1 collective-permute-start.11
  595.5 3.1 collective-permute-start.13
  602.6 3.1 collective-permute-start.15
  609.8 3.1 collective-permute-start.17
  (283 shorter events, 173.9 us)
Async XLA Ops:
  6.5 11.9 %copy-start = (f32[4,64,256]{2,1,0:T(8,128)S(1)}, f32[4,64,256]{2,1,0:T(8,128)}, u32[]{:S(2)}) copy-start(f32[4,64,256]{2,1,0:T(8,128)} %param.23) | copy-start | bytes 786436
  6.5 146.1 %all-reduce.26.cloned.1.call-start = ((), (), s32[]{:S(2)}) async-start(), calls=%async_computation.1 | async-start | bytes 4194304 | tf_op jit(solution)/shard_map/psum | solution.py:32
  6.5 10.5 %collective-permute-start.2 = (bf16[4,64,256]{2,1,0:T(8,128)(2,1)}, bf16[4,64,256]{2,1,0:T(8,128)(2,1)S(1)}, u32[]{:S(2)}, u32[]{:S(2)}) collective-permute-start(bf16[4,64,256]{2,1,0:T(8,128)(2,1)} %bitcast.97), channel_id=1, source_target_pairs={{0,1},{2,3},{4,5},{6,7},{8,9},{10,11},{12,13},{14,15},{16,17},{18,... | collective-permute-start | bytes 393224 | tf_op jit(solution)/shard_map/ppermute | solution.py:21
  9.1 8.0 %collective-permute-start.3 = (bf16[4,64,256]{2,1,0:T(8,128)(2,1)}, bf16[4,64,256]{2,1,0:T(8,128)(2,1)S(1)}, u32[]{:S(2)}, u32[]{:S(2)}) collective-permute-start(bf16[4,64,256]{2,1,0:T(8,128)(2,1)} %bitcast.98), channel_id=1, source_target_pairs={{1,0},{3,2},{5,4},{7,6},{9,8},{11,10},{13,12},{15,14},{17,16},{19,... | collective-permute-start | bytes 393224 | tf_op jit(solution)/shard_map/ppermute | solution.py:23
  22.1 132.4 %copy-start.1 = (bf16[12,4,64,256]{3,2,1,0:T(8,128)(2,1)S(1)}, bf16[12,4,64,256]{3,2,1,0:T(8,128)(2,1)}, u32[]{:S(2)}) copy-start(bf16[12,4,64,256]{3,2,1,0:T(8,128)(2,1)} %param.22) | copy-start | bytes 4718596
  22.1 132.4 %copy-start.17 = (s32[12]{0:T(128)S(1)}, s32[12]{0:T(128)}, u32[]{:S(2)}) copy-start(s32[12]{0:T(128)} %param.24) | copy-start | bytes 148
  22.2 541.1 %all-reduce.24.cloned.1.call-start = ((), (), s32[]{:S(2)}) async-start(), calls=%async_computation | async-start | bytes 4194304 | tf_op jit(solution)/shard_map/psum | solution.py:99
  352.9 27.3 %copy-start.16 = (f32[4,64,256]{2,1,0:T(8,128)S(1)}, f32[4,64,256]{2,1,0:T(8,128)}, u32[]{:S(2)}) copy-start(f32[4,64,256]{2,1,0:T(8,128)} %get-tuple-element.1302) | copy-start | bytes 786436
  380.4 27.7 %copy-start.15 = (f32[4,64,256]{2,1,0:T(8,128)S(1)}, f32[4,64,256]{2,1,0:T(8,128)}, u32[]{:S(2)}) copy-start(f32[4,64,256]{2,1,0:T(8,128)} %get-tuple-element.1301) | copy-start | bytes 786436
  436.8 4.4 collective-permute-start
  438.1 4.2 collective-permute-start.1
  565.3 6.1 copy-start.14
  565.3 4.5 collective-permute-start.4
  566.8 4.2 collective-permute-start.5
  572.5 6.1 copy-start.13
  572.5 4.5 collective-permute-start.6
  573.9 4.2 collective-permute-start.7
  579.7 6.1 copy-start.12
  579.7 4.7 collective-permute-start.8
  581.1 4.2 collective-permute-start.9
  586.8 6.1 copy-start.11
  586.9 4.5 collective-permute-start.10
  588.3 4.2 collective-permute-start.11
  594.0 6.1 copy-start.10
  594.0 4.5 collective-permute-start.12
  595.5 4.2 collective-permute-start.13
  601.2 6.1 copy-start.9
  601.2 4.5 collective-permute-start.14
  602.6 4.2 collective-permute-start.15
  608.4 6.1 copy-start.8
  608.4 4.5 collective-permute-start.16
  609.8 4.2 collective-permute-start.17
  (6 other events, 6.5 us)
Sparse Core Ops, SparseCore 0:
  22.3 130.3 all-reduce.25
  436.9 126.3 all-reduce.23
where the time goes:
time: 627 us; the launch traced here: 623 us
  waiting for transfers between devices  260 us (41%)
  loops' own time  126 us (20%)
  other arithmetic  105 us (17%)
  local copies, waits for them, and re-layouts  73.7 us (12%)
  starting transfers between devices  39.8 us (6%)
  between operations  19.1 us (3%)
    psum x1, waiting for transfers between devices, broadcast(): return lax.psum(jnp.where(mine, x, jnp.zeros_like(x)), axis)  130 us
    another operation x8, loops' own time, shifted_sum(): lax.fori_loop(0, reflect.shape[0], add_offset, jnp.zeros(acceleration.sha...  126 us
    psum x1, waiting for transfers between devices, per_device(): source = lax.psum(local_source, 'off')  121 us
    add x96, other arithmetic, add_offset(): return summed + reflect[offset_index].astype(jnp.float32) * window  85.7 us
    dynamic_slice x96, local copies, waits for them, and re-layouts, add_offset(): lag_now = lags[offset_index]  60 us
    ppermute x9, starting transfers between devices, extended(): lax.ppermute(tail, axis, [(i, (i + 1) % count) for i in range(ends)])  27.2 us
    ppermute x9, starting transfers between devices, extended(): lax.ppermute(head, axis, [((i + 1) % count, i) for i in range(ends)])  12.6 us
  transfers between devices with their start and end apart: 20, of which 10 were waited for; matrix products, arithmetic and copies ran while one was open for 0% of the time, Pallas kernels for 0%

commit v1 on v0

v1 whole, which is shorter than its diff:
```python
import functools

import jax
import jax.numpy as jnp
from jax import lax
from jax.experimental import pallas as pl
from jax.experimental.pallas import tpu as pltpu
from jax.sharding import PartitionSpec as P


ITERS = 8
LAG = 32
REACH = 4

STENCIL_WEIGHTS = (-205.0 / 72.0, 8.0 / 5.0, -1.0 / 5.0, 8.0 / 315.0, -1.0 / 560.0)


BF16 = jnp.bfloat16
F32 = jnp.float32


def extended(cells, sides, width):
    for axis, dim in sides:
        count = lax.axis_size(axis)
        ends = count - 1
        head = lax.slice_in_dim(cells, 0, width, axis=dim)
        tail = lax.slice_in_dim(cells, cells.shape[dim] - width, cells.shape[dim], axis=dim)
        cells = jnp.concatenate(
            [
                lax.ppermute(tail, axis, [(i, (i + 1) % count) for i in range(ends)]),
                cells,
                lax.ppermute(head, axis, [((i + 1) % count, i) for i in range(ends)]),
            ],
            axis=dim,
        )
    return cells


def broadcast(x, axis, root):
    mine = lax.axis_index(axis) == root
    return lax.psum(jnp.where(mine, x, jnp.zeros_like(x)), axis)


def stencil(padded, depth_cells, row_cells, column_cells):
    def part(dz, dy, dx):
        return padded[
            4 + dz : 4 + dz + depth_cells, 4 + dy : 4 + dy + row_cells, 4 + dx : 4 + dx + column_cells
        ]

    summed = 3.0 * STENCIL_WEIGHTS[0] * part(0, 0, 0)
    for k in range(1, 5):
        neighbours = part(k, 0, 0) + part(-k, 0, 0)
        neighbours = neighbours + part(0, k, 0) + part(0, -k, 0)
        neighbours = neighbours + part(0, 0, k) + part(0, 0, -k)
        summed = summed + STENCIL_WEIGHTS[k] * neighbours
    return summed


def shifted_sum(reflect, acceleration, lags):
    width_cells = acceleration.shape[2]
    padded = jnp.pad(acceleration, ((0, 0), (0, 0), (LAG, LAG)))

    def add_offset(offset_index, summed):
        lag_now = lags[offset_index]
        window = lax.dynamic_slice_in_dim(padded, LAG - lag_now, width_cells, 2)
        return summed + reflect[offset_index].astype(F32) * window

    return lax.fori_loop(0, reflect.shape[0], add_offset, jnp.zeros(acceleration.shape, F32))


def halo_steps(snapshots, reflect, courant, lags, owners):
    own_layers = extended(snapshots[0], (("dep", 0),), 4)
    own_ready = courant * stencil(
        jnp.pad(own_layers, ((0, 0), (4, 4), (4, 4))).astype(F32), *courant.shape
    )
    scattered = jnp.zeros(courant.shape, F32)
    previous = jnp.zeros(courant.shape, F32)
    for step_now in range(ITERS):
        acceleration = broadcast(own_ready, "off", owners[step_now])
        source = shifted_sum(reflect, acceleration, lags)
        field = jnp.pad(extended(scattered, (("dep", 0),), 4), ((0, 0), (4, 4), (4, 4)))
        updated = 2.0 * scattered - previous + courant * stencil(field, *courant.shape) + source
        previous = scattered
        scattered = updated
    return lax.psum(scattered, "off")


def split(v):
    high = v.astype(BF16)
    return high, (v - high.astype(F32)).astype(BF16)


def band(rows, columns, block):
    i = lax.broadcasted_iota(jnp.int32, (rows, columns), 0)
    j = lax.broadcasted_iota(jnp.int32, (rows, columns), 1)
    apart = jnp.where(i // block == j // block, jnp.abs(i - j), 0)
    full = jnp.zeros((rows, columns), F32)
    for k in range(1, REACH + 1):
        full = jnp.where(apart == k, STENCIL_WEIGHTS[k], full)
    return split(full)


def copy(source, target, sem):
    return pltpu.make_async_copy(source, target, sem)


def prepare_kernel(core_ref, own_reflect, far_reflect, own_courant, far_courant, rt, cour, across, down, refl, sems):
    core = core_ref[0]
    half = own_courant.shape[0]
    rows, columns = cour.shape[1:]
    offsets, blocks = rt.shape[:2]
    stack = 128 // rows
    here, there = pl.ds(core * half, half), pl.ds((1 - core) * half, half)
    moves = [
        copy(own_courant, cour.at[here], sems.at[0]),
        copy(far_courant, cour.at[there], sems.at[1]),
        copy(own_reflect.at[pl.ds(core * offsets, offsets)], refl.at[:, here], sems.at[2]),
        copy(far_reflect, refl.at[:, there], sems.at[3]),
    ]
    for move in moves:
        move.start()
    high, low = band(columns, columns, columns)
    for i, part in enumerate((high, low, high)):
        across[i * columns : (i + 1) * columns] = part
    group = down.shape[0]
    high, low = band(group, group, rows)
    for i, part in enumerate((high, low, high)):
        down[:, i * group : (i + 1) * group] = part
    for move in moves:
        move.wait()

    def turn(h, carry):
        for b in range(blocks):
            tile = jnp.concatenate([refl[h, stack * b + i] for i in range(stack)], 0)
            rt[h, b] = tile.astype(F32).T.astype(BF16)
        return carry

    lax.fori_loop(0, offsets, turn, 0)


def vertical(plane_of, z, depth):
    total = (3.0 * STENCIL_WEIGHTS[0]) * plane_of(z)
    for k in range(1, REACH + 1):
        near = [plane_of(n) for n in (z - k, z + k) if 0 <= n < depth]
        if near:
            total = total + STENCIL_WEIGHTS[k] * functools.reduce(jnp.add, near)
    return total


def sideways(terms, across, down):
    n = len(terms)
    group, columns = terms[0].shape
    x_part = jnp.dot(jnp.concatenate(terms, 1), across[0 : n * columns], preferred_element_type=F32)
    y_part = jnp.dot(down[:, 0 : n * group], jnp.concatenate(terms, 0), preferred_element_type=F32)
    return x_part + y_part


def source_of(field, lag_of, rt, cour, across, down, plain, shifted, turned, source):
    depth, rows, columns = cour.shape
    offsets, blocks = rt.shape[:2]
    group = down.shape[0]
    planes, tiles, stack = group // rows, group // 128, 128 // rows
    for z in range(depth):
        plain[z] = field[z].astype(F32)
    for g in range(depth // planes):
        high = jnp.concatenate([field[g * planes + p] for p in range(planes)], 0)
        both = sideways([high, high], across, down)
        for b in range(tiles):
            pieces = []
            for i in range(stack):
                p = b * stack + i
                z = g * planes + p
                upright = vertical(lambda n: plain[n], z, depth)
                pieces.append(cour[z] * (both[p * rows : (p + 1) * rows] + upright))
            shifted[g * tiles + b, LAG : LAG + columns] = jnp.concatenate(pieces, 0).T
    chunk = 64
    for b in range(blocks):
        for r in range(0, columns, chunk):
            total = jnp.zeros((chunk, 128), F32)
            for h in range(offsets):
                image = rt[h, b, r : r + chunk].astype(F32)
                total = total + image * shifted[b, pl.ds(LAG + r - lag_of(h), chunk)]
            turned[b, r : r + chunk] = total
    for b in range(blocks):
        tile = turned[b].T
        for i in range(stack):
            source[stack * b + i] = tile[i * rows : (i + 1) * rows]


def clear_rims(shifted, columns):
    for b in range(shifted.shape[0]):
        shifted[b, 0:LAG] = jnp.zeros((LAG, 128), F32)
        shifted[b, LAG + columns : 2 * LAG + columns] = jnp.zeros((LAG, 128), F32)


def fetch_fields(where_ref, owners_ref, choose, fields, sems, half):
    place, core = where_ref[0], where_ref[1]
    here, there = pl.ds(core * half, half), pl.ds((1 - core) * half, half)
    for t in range(ITERS):
        for test, at, own, far in choose(owners_ref[t] ^ place):

            @pl.when(test)
            def _(at=at, own=own, far=far, t=t):
                copy(own.at[at], fields.at[t, here], sems.at[t, 0]).start()
                copy(far.at[at], fields.at[t, there], sems.at[t, 1]).start()


def held(where_ref, owners_ref, choose, t):
    tests = [test for test, *_ in choose(owners_ref[t] ^ where_ref[0])]
    return functools.reduce(jnp.logical_or, tests)


def wait_fields(fields, sems, t, half):
    for i in range(2):
        part = fields.at[t, pl.ds(i * half, half)]
        copy(part, part, sems.at[t, i]).wait()


def sums_kernel(
    choose, where_ref, owners_ref, lags_ref, rt, cour, across, down, sums,
    fields, plain, shifted, turned, field_sems,
):
    depth = cour.shape[0]
    first = where_ref[1] * rt.shape[0]
    fetch_fields(where_ref, owners_ref, choose, fields, field_sems, depth // 2)
    clear_rims(shifted, cour.shape[2])

    def step(t, carry):
        @pl.when(held(where_ref, owners_ref, choose, t))
        def _():
            wait_fields(fields, field_sems, t, depth // 2)
            source_of(
                fields.at[t], lambda h: lags_ref[first + h], rt, cour, across, down, plain, shifted, turned, sums.at[t]
            )

        return carry

    lax.fori_loop(0, ITERS, step, 0)


def steps_kernel(
    choose, where_ref, owners_ref, lags_ref, rt, cour, across, down, kept_ref, given_ref, sums,
    fields, plain, shifted, turned, field_sems, wave_a, wave_b,
):
    sums_kernel(
        choose, where_ref, owners_ref, lags_ref, rt, cour, across, down, sums,
        fields, plain, shifted, turned, field_sems,
    )
    depth, rows, _ = cour.shape
    half = depth // 2
    group = down.shape[0]
    planes = group // rows

    def grow(t, now, before):
        for g in range(depth // planes):
            high, low = split(jnp.concatenate([now[g * planes + p] for p in range(planes)], 0))
            both = sideways([high, high, low], across, down)
            for p in range(planes):
                z = g * planes + p
                laplace = both[p * rows : (p + 1) * rows] + vertical(lambda n: now[n], z, depth)
                before[z] = (2.0 * now[z] - before[z]) + (cour[z] * laplace + sums[t, z])

    wave_a[...] = sums[0]
    wave_b[...] = jnp.zeros(wave_b.shape, F32)

    def pair(i, carry):
        grow(2 * i + 1, wave_a, wave_b)
        grow(2 * i + 2, wave_b, wave_a)
        return carry

    lax.fori_loop(0, (ITERS - 1) // 2, pair, 0)
    last = wave_a
    if ITERS % 2 == 0:
        grow(ITERS - 1, wave_a, wave_b)
        last = wave_b
    core = where_ref[1]
    kept_ref[...] = last[pl.ds(core * half, half)]
    given_ref[...] = last[pl.ds((1 - core) * half, half)]


def swapped(x):
    return lax.ppermute(x, "dep", [(0, 1), (1, 0)])


def flip(x, bits):
    count = lax.axis_size("off")
    return lax.ppermute(x, "off", [(i, i ^ bits) for i in range(count)])


def core_pair(snapshots, reflect, courant, lags, owners):
    count = lax.axis_size("off")
    core = lax.axis_index("dep")
    mine = reflect.shape[0] // 2
    half, rows, columns = courant.shape
    depth = 2 * half
    blocks = depth * rows // 128
    group = 256
    wing = 4
    lines = count // wing
    cut = 2 * (lines - 1) // 3

    z_parts = [flip(snapshots, wing * j) for j in range(1, lines)]
    o_x, o_y = flip(snapshots, 1), flip(snapshots, 2)
    o_d = flip(o_x, 2)
    sent = lax.dynamic_slice_in_dim(reflect, (1 - core) * mine, mine, 0)
    far_reflect = swapped(sent)
    far_courant = swapped(courant)
    z_all = jnp.concatenate(z_parts, 0)
    z_x, z_y = flip(z_all, 1), flip(z_all, 2)
    d_x = flip(z_x[:cut], 2)
    d_y = flip(z_y[cut:], 1)

    smem = pl.BlockSpec(memory_space=pltpu.SMEM)
    anyspace = pl.BlockSpec(memory_space=pl.ANY)
    vmem = pl.BlockSpec(memory_space=pltpu.VMEM)
    where = jnp.stack([lax.axis_index("off"), core]).astype(jnp.int32)
    tables = [
        jax.ShapeDtypeStruct((mine, blocks, columns, 128), BF16),
        jax.ShapeDtypeStruct((depth, rows, columns), F32),
        jax.ShapeDtypeStruct((3 * columns, columns), BF16),
        jax.ShapeDtypeStruct((group, 3 * group), BF16),
    ]
    prepare = pl.pallas_call(
        prepare_kernel,
        out_shape=tables,
        in_specs=[smem] + [anyspace] * 4,
        out_specs=[vmem] * 4,
        scratch_shapes=[pltpu.VMEM((mine, depth, rows, columns), BF16), pltpu.SemaphoreType.DMA((4,))],
        compiler_params=pltpu.CompilerParams(vmem_limit_bytes=16 << 20),
        cost_estimate=pl.CostEstimate(flops=10**7, bytes_accessed=6 << 20, transcendentals=0),
    )
    prepared = prepare(where[1:], reflect, far_reflect, courant, far_courant)

    scratch = [
        pltpu.VMEM((ITERS, depth, rows, columns), BF16),
        pltpu.VMEM((depth, rows, columns), F32),
        pltpu.VMEM((blocks, columns + 2 * LAG, 128), F32),
        pltpu.VMEM((blocks, columns, 128), F32),
        pltpu.SemaphoreType.DMA((ITERS, 2)),
    ]
    waves = [pltpu.VMEM((depth, rows, columns), F32)] * 2
    params = pltpu.CompilerParams(vmem_limit_bytes=32 << 20)
    cost = pl.CostEstimate(flops=10**9, bytes_accessed=10 << 20, transcendentals=0)
    sums_shape = jax.ShapeDtypeStruct((ITERS, depth, rows, columns), F32)

    def near_banks(owns, fars):
        def choose(apart):
            low, line = apart % wing, apart // wing
            own_line = [((line == 0) & (low == i), 0, owns[i], fars[i]) for i in range(wing)]
            return own_line + [((line > 0) & (low == 0), line - 1, owns[wing], fars[wing])]

        return choose

    def side_banks(owns, fars):
        def choose(apart):
            low, line = apart % wing, apart // wing
            return [((line > 0) & (low == 1 + i), line - 1, owns[i], fars[i]) for i in range(2)]

        return choose

    def far_banks(owns, fars):
        def choose(apart):
            low, line = apart % wing, apart // wing
            return [
                ((low == 3) & (line > 0) & (line <= cut), line - 1, owns[0], fars[0]),
                ((low == 3) & (line > cut), line - 1 - cut, owns[1], fars[1]),
            ]

        return choose

    def run(body, banks, own_parts, extra, out_shape, more_scratch=()):
        far_parts = [swapped(v) for v in own_parts]
        n = len(own_parts)

        def kernel(where_ref, owners_ref, lags_ref, *refs):
            rest = refs[2 * n : 2 * n + 4] + refs[2 * n + 4 + len(extra) :]
            body(banks(refs[:n], refs[n : 2 * n]), where_ref, owners_ref, lags_ref, *rest)

        return pl.pallas_call(
            kernel,
            in_specs=[smem] * 3 + [anyspace] * (2 * n) + [vmem] * (4 + len(extra)),
            out_shape=out_shape,
            out_specs=[vmem] * len(out_shape),
            scratch_shapes=scratch + list(more_scratch),
            input_output_aliases={3 + 2 * n + 4: len(out_shape) - 1} if extra else {},
            compiler_params=params,
            cost_estimate=cost,
        )(where, owners, lags, *own_parts, *far_parts, *prepared, *extra)

    out_half = jax.ShapeDtypeStruct((half, rows, columns), F32)
    sums = run(sums_kernel, near_banks, [snapshots, o_x, o_y, o_d, z_all], [], [sums_shape])
    sums = run(sums_kernel, side_banks, [z_x, z_y], sums, [sums_shape])
    kept, given, _ = run(steps_kernel, far_banks, [d_x, d_y], sums, [out_half, out_half, sums_shape], waves)

    total = kept + swapped(given)
    pieces = total.reshape(count, half * rows // count, columns)
    summed = lax.all_to_all(pieces, "off", 0, 0).sum(0)
    spread = jnp.broadcast_to(summed[None], pieces.shape)
    return lax.all_to_all(spread, "off", 0, 0).reshape(half, rows, columns)


def solution(mesh):
    offs, deps = mesh.shape["off"], mesh.shape["dep"]

    def per_device(snapshots, reflect, courant, lags, owners):
        fits = (
            deps == 2
            and snapshots.shape[0] == 1
            and offs >= 16
            and offs & (offs - 1) == 0
            and reflect.shape[0] % 2 == 0
            and courant.shape[2] % 128 == 0
            and (courant.shape[0] * courant.shape[1]) % (8 * offs) == 0
            and (courant.shape[0] * courant.shape[1]) % 128 == 0
            and courant.shape[1] % 16 == 0
            and 128 % courant.shape[1] == 0
        )
        body = core_pair if fits else halo_steps
        return body(snapshots, reflect, courant, lags, owners)

    in_specs = (
        P("off", "dep", None, None),
        P("off", "dep", None, None),
        P("dep", None, None),
        P("off"),
        P(),
    )
    return jax.shard_map(
        per_device, mesh=mesh, in_specs=in_specs, out_specs=P("dep", None, None), check_vma=False
    )
```

time: 627 us -> 109 us (0.17)
  waiting for transfers between devices: 260 us -> 24.3 us
  loops' own time: 126 us -> 0 us
  other arithmetic: 105 us -> 0.13 us
  local copies, waits for them, and re-layouts: 73.7 us -> 17.4 us
  blocking collectives: 0 us -> 27.6 us
  starting transfers between devices: 39.8 us -> 17.3 us
  Pallas kernels: 0 us -> 21.7 us
  between operations: 19.1 us -> 0.19 us
    psum x2 -> x0, waiting for transfers between devices: 251 us -> none  [the longest x1 130 us: broadcast(): return lax.psum(jnp.where(mine, x, jnp.zeros_like(x)), axis)]
    another operation x8 -> x0, loops' own time: 126 us -> none  [shifted_sum(): lax.fori_loop(0, reflect.shape[0], add_offset, jnp.zeros(acceleration.sha...]
    add x104 -> x1, other arithmetic: 96.2 us -> 0.03 us  [core_pair(): total = kept + swapped(given)]
    dynamic_slice x96 -> x1, local copies, waits for them, and re-layouts: 60 us -> 2.12 us  [core_pair(): sent = lax.dynamic_slice_in_dim(reflect, (1 - core) * mine, mine, 0)]
    all_to_all x0 -> x2, blocking collectives: none -> 27.6 us  [the longest x1 14.8 us: core_pair(): summed = lax.all_to_all(pieces, 'off', 0, 0).sum(0)]
    ppermute x18 -> x22, starting transfers between devices: 39.7 us -> 17.3 us  [the longest x10 14.8 us: flip(): return lax.ppermute(x, 'off', [(i, i ^ bits) for i in range(count)])]
    pallas_call x0 -> x4, Pallas kernels: none -> 21.7 us  [the longest x3 20.4 us: run(): pl.pallas_call(kernel, in_specs=[smem] * 3 + [anyspace] * (2 * n) + [vmem...]
    ppermute x18 -> x22, waiting for transfers between devices: 8.79 us -> 24.3 us  [the longest x10 23.1 us: flip(): return lax.ppermute(x, 'off', [(i, i ^ bits) for i in range(count)])]
  transfers between devices with their start and end apart: 20 -> 22, of which waited for: 10 -> 6; matrix products, arithmetic and copies ran while one was open for 0% -> 3% of each run, Pallas kernels for 0% -> 13%
where the time goes in v1:
time: 109 us
  blocking collectives  27.6 us (25%)
  waiting for transfers between devices  24.3 us (22%)
  Pallas kernels  21.7 us (20%)
  local copies, waits for them, and re-layouts  17.4 us (16%)
  starting transfers between devices  17.3 us (16%)
    ppermute x10, waiting for transfers between devices, flip(): return lax.ppermute(x, 'off', [(i, i ^ bits) for i in range(count)])  23.1 us
    pallas_call x3, Pallas kernels, run(): pl.pallas_call(kernel, in_specs=[smem] * 3 + [anyspace] * (2 * n) + [vmem...  20.4 us
    ppermute x10, starting transfers between devices, flip(): return lax.ppermute(x, 'off', [(i, i ^ bits) for i in range(count)])  14.8 us
    all_to_all x1, blocking collectives, core_pair(): summed = lax.all_to_all(pieces, 'off', 0, 0).sum(0)  14.8 us
    unnamed x45, local copies, waits for them, and re-layouts  14.6 us
    all_to_all x1, blocking collectives, core_pair(): return lax.all_to_all(spread, 'off', 0, 0).reshape(half, rows, columns)  12.8 us
    ppermute x12, starting transfers between devices, swapped(): return lax.ppermute(x, 'dep', [(0, 1), (1, 0)])  2.44 us
  transfers between devices with their start and end apart: 22, of which 6 were waited for; matrix products, arithmetic and copies ran while one was open for 3% of the time, Pallas kernels for 13%

profile of v1, /device:TPU:0, one launch (start us, length us, event | category | flops | bytes accessed | tf_op | source)
XLA Modules:
  0.0 108.7 jit_solution(6772259436229017593)
XLA Ops:
  0.0 3.1 %collective-permute-start = (bf16[1,4,64,256]{3,2,1,0:T(8,128)(2,1)}, bf16[1,4,64,256]{3,2,1,0:T(8,128)(2,1)S(1)}, u32[]{:S(2)}, u32[]{:S(2)}) collective-permute-start(bf16[1,4,64,256]{3,2,1,0:T(8,128)(2,1)} %refs_0_.1), channel_id=1, source_target_pairs={{0,8},{2,10},{4,12},{6,14},{8,0},{10,2},{12,4},{14,6},{16,24},{18,... | collective-permute-start | bytes 393224 | tf_op jit(solution)/shard_map/ppermute | solution.py:287
  3.1 2.6 %collective-permute-start.1 = (bf16[1,4,64,256]{3,2,1,0:T(8,128)(2,1)}, bf16[1,4,64,256]{3,2,1,0:T(8,128)(2,1)S(1)}, u32[]{:S(2)}, u32[]{:S(2)}) collective-permute-start(bf16[1,4,64,256]{3,2,1,0:T(8,128)(2,1)} %refs_0_.1), channel_id=1, source_target_pairs={{0,16},{2,18},{4,20},{6,22},{8,24},{10,26},{12,28},{14,30},{16,0},... | collective-permute-start | bytes 393224 | tf_op jit(solution)/shard_map/ppermute | solution.py:287
  5.7 1.7 %collective-permute-start.13 = (bf16[1,4,64,256]{3,2,1,0:T(8,128)(2,1)}, bf16[1,4,64,256]{3,2,1,0:T(8,128)(2,1)S(1)}, u32[]{:S(2)}, u32[]{:S(2)}) collective-permute-start(bf16[1,4,64,256]{3,2,1,0:T(8,128)(2,1)} %refs_0_.1), channel_id=1, source_target_pairs={{0,2},{2,0},{4,6},{6,4},{8,10},{10,8},{12,14},{14,12},{16,18},{18,... | collective-permute-start | bytes 393224 | tf_op jit(solution)/shard_map/ppermute | solution.py:287
  7.4 2.1 %constant_dynamic-slice_fusion = bf16[6,4,64,256]{3,2,1,0:T(8,128)(2,1)} fusion(bf16[12,4,64,256]{3,2,1,0:T(8,128)(2,1)} %own_reflect.1, s32[]{:T(128)S(6)} %select_n.3), kind=kLoop, calls=%fused_computation.4 | loop fusion | bytes 1572868 | tf_op jit(solution)/shard_map/dynamic_slice | solution.py:305
  9.6 6.7 %collective-permute-done.1 = bf16[1,4,64,256]{3,2,1,0:T(8,128)(2,1)S(1)} collective-permute-done((bf16[1,4,64,256]{3,2,1,0:T(8,128)(2,1)}, bf16[1,4,64,256]{3,2,1,0:T(8,128)(2,1)S(1)}, u32[]{:S(2)}, u32[]{:S(2)}) %collective-permute-start.1) | collective-permute-done | bytes 131104 | tf_op jit(solution)/shard_map/ppermute | solution.py:287
  16.3 1.6 %collective-permute-start.3 = (bf16[3,4,64,256]{3,2,1,0:T(8,128)(2,1)S(1)}, bf16[3,4,64,256]{3,2,1,0:T(8,128)(2,1)S(1)}, u32[]{:S(2)}, u32[]{:S(2)}) collective-permute-start(bf16[3,4,64,256]{3,2,1,0:T(8,128)(2,1)S(1)} %constant_dynamic-update-slice_fusion.refs_4_), channel_id=1, source_target_pairs={{0,2},{2,0},{4,6},{6,4},{8,10},{10,8},{12,14},{14,12},{16,18},{18,... | collective-permute-start | bytes 1179656 | tf_op jit(solution)/shard_map/ppermute | solution.py:287
  17.8 1.5 %collective-permute-start.14 = (bf16[1,4,64,256]{3,2,1,0:T(8,128)(2,1)}, bf16[1,4,64,256]{3,2,1,0:T(8,128)(2,1)S(1)}, u32[]{:S(2)}, u32[]{:S(2)}) collective-permute-start(bf16[1,4,64,256]{3,2,1,0:T(8,128)(2,1)} %refs_0_.1), channel_id=1, source_target_pairs={{0,4},{2,6},{4,0},{6,2},{8,12},{10,14},{12,8},{14,10},{16,20},{18,... | collective-permute-start | bytes 393224 | tf_op jit(solution)/shard_map/ppermute | solution.py:287
  20.0 3.0 %collective-permute-done.14.refs_2_ = bf16[1,4,64,256]{3,2,1,0:T(8,128)(2,1)S(1)} collective-permute-done((bf16[1,4,64,256]{3,2,1,0:T(8,128)(2,1)}, bf16[1,4,64,256]{3,2,1,0:T(8,128)(2,1)S(1)}, u32[]{:S(2)}, u32[]{:S(2)}) %collective-permute-start.14) | collective-permute-done | bytes 131104 | tf_op jit(solution)/shard_map/ppermute | solution.py:287
  23.0 2.4 %collective-permute-start.5 = (bf16[3,4,64,256]{3,2,1,0:T(8,128)(2,1)S(1)}, bf16[3,4,64,256]{3,2,1,0:T(8,128)(2,1)S(1)}, u32[]{:S(2)}, u32[]{:S(2)}) collective-permute-start(bf16[3,4,64,256]{3,2,1,0:T(8,128)(2,1)S(1)} %constant_dynamic-update-slice_fusion.refs_4_), channel_id=1, source_target_pairs={{0,4},{2,6},{4,0},{6,2},{8,12},{10,14},{12,8},{14,10},{16,20},{18,... | collective-permute-start | bytes 1179656 | tf_op jit(solution)/shard_map/ppermute | solution.py:287
  26.8 7.6 %collective-permute-done.15.refs_3_ = bf16[1,4,64,256]{3,2,1,0:T(8,128)(2,1)S(1)} collective-permute-done((bf16[1,4,64,256]{3,2,1,0:T(8,128)(2,1)}, bf16[1,4,64,256]{3,2,1,0:T(8,128)(2,1)S(1)}, u32[]{:S(2)}, u32[]{:S(2)}) %collective-permute-start.15) | collective-permute-done | bytes 131104 | tf_op jit(solution)/shard_map/ppermute | solution.py:287
  36.9 1.4 %collective-permute-start.4 = (bf16[2,4,64,256]{3,2,1,0:T(8,128)(2,1)S(1)}, bf16[2,4,64,256]{3,2,1,0:T(8,128)(2,1)}, u32[]{:S(2)}, u32[]{:S(2)}) collective-permute-start(bf16[2,4,64,256]{3,2,1,0:T(8,128)(2,1)S(1)} %slice.8), channel_id=1, source_target_pairs={{0,4},{2,6},{4,0},{6,2},{8,12},{10,14},{12,8},{14,10},{16,20},{18,... | collective-permute-start | bytes 786440 | tf_op jit(solution)/shard_map/ppermute | solution.py:287
  40.8 4.4 %collective-permute-done.4.refs_0_ = bf16[2,4,64,256]{3,2,1,0:T(8,128)(2,1)} collective-permute-done((bf16[2,4,64,256]{3,2,1,0:T(8,128)(2,1)S(1)}, bf16[2,4,64,256]{3,2,1,0:T(8,128)(2,1)}, u32[]{:S(2)}, u32[]{:S(2)}) %collective-permute-start.4) | collective-permute-done | bytes 262176 | tf_op jit(solution)/shard_map/ppermute | solution.py:287
  45.8 0.9 copy-done.1
  46.7 0.9 copy-done.3
  47.7 1.3 %shard_map.55 = (bf16[6,4,256,128]{3,2,1,0:T(8,128)(2,1)S(1)}, f32[8,64,256]{2,1,0:T(8,128)S(1)}, bf16[768,256]{1,0:T(8,128)(2,1)S(1)}, bf16[256,768]{1,0:T(8,128)(2,1)S(1)}) custom-call(s32[1]{0:T(128)} %bitcast.1.core_ref, bf16[12,4,64,256]{3,2,1,0:T(8,128)(2,1)S(1)} %copy-done, bf16[6,4,64,256]{3,2,1,0:T(8,128)(2,1)S(1)} %collective-permute-done.9.far_reflect, ...), custom_call_target="tpu_custom_call" | custom-call | flops 10000000 | bytes 6291456 | tf_op jit(solution)/shard_map/pallas_call | solution.py:332
  49.0 1.5 %collective-permute-done.6.refs_1_ = bf16[1,4,64,256]{3,2,1,0:T(8,128)(2,1)} collective-permute-done((bf16[1,4,64,256]{3,2,1,0:T(8,128)(2,1)}, bf16[1,4,64,256]{3,2,1,0:T(8,128)(2,1)}, u32[]{:S(2)}, u32[]{:S(2)}) %collective-permute-start.6) | collective-permute-done | bytes 131104 | tf_op jit(solution)/shard_map/ppermute | solution.py:287
  50.5 0.9 copy-done.4
  51.4 0.9 copy-done.6
  52.3 0.9 copy-done.8
  53.2 0.9 copy-done.10
  54.1 0.9 copy-done.12
  55.0 0.9 copy-done.14
  55.9 0.9 copy-done.16
  56.8 0.9 copy-done.18
  57.7 9.5 %shard_map.56.refs_8_ = f32[8,8,64,256]{3,2,1,0:T(8,128)S(1)} custom-call(s32[2]{0:T(128)S(1)} %pad_add_fusion.where_ref, s32[8]{0:T(128)S(1)} %copy-done.19, s32[12]{0:T(128)S(1)} %copy-done.20, bf16[1,4,64,256]{3,2,1,0:T(8,128)(2,1)S(1)} %copy-done.4, bf16[1,4,64,256]{3,2,1,0:T(8,128)(2,1)S(1)} %copy-done.6, bf16[1,4,64,256]{3,2,1,0:T(8,128)(2,1)S(1)} %copy-done.8, ...), custom_call_target="tpu_custom_call" | custom-call | flops 1000000000 | bytes 10485760 | tf_op jit(solution)/shard_map/pallas_call | solution.py:379
  67.3 3.1 %shard_map.57.refs_8_ = f32[8,8,64,256]{3,2,1,0:T(8,128)S(1)} custom-call(s32[2]{0:T(128)S(1)} %pad_add_fusion.where_ref, s32[8]{0:T(128)S(1)} %copy-done.19, s32[12]{0:T(128)S(1)} %copy-done.20, bf16[3,4,64,256]{3,2,1,0:T(8,128)(2,1)S(1)} %collective-permute-done.3.refs_0_, ...), custom_call_target="tpu_custom_call", output_to_operand_aliasing={{}: (11, {})} | custom-call | flops 1000000000 | bytes 10485760 | tf_op jit(solution)/shard_map/pallas_call | solution.py:379
  70.4 7.8 %shard_map.58 = (f32[4,64,256]{2,1,0:T(8,128)S(1)}, f32[4,64,256]{2,1,0:T(8,128)S(1)}, f32[8,8,64,256]{3,2,1,0:T(8,128)S(1)}) custom-call(s32[2]{0:T(128)S(1)} %pad_add_fusion.where_ref, s32[8]{0:T(128)S(1)} %copy-done.19, s32[12]{0:T(128)S(1)} %copy-done.20, ...), custom_call_target="tpu_custom_call", output_to_operand_aliasing={{2}: (11, {})} | custom-call | flops 1000000000 | bytes 10485760 | tf_op jit(solution)/shard_map/pallas_call | solution.py:379
  78.2 0.9 collective-permute-start.21
  79.1 1.2 %collective-permute-done.21 = f32[4,64,256]{2,1,0:T(8,128)S(1)} collective-permute-done((f32[4,64,256]{2,1,0:T(8,128)S(1)}, f32[4,64,256]{2,1,0:T(8,128)S(1)}, u32[]{:S(2)}, u32[]{:S(2)}) %collective-permute-start.21) | collective-permute-done | bytes 262176 | tf_op jit(solution)/shard_map/ppermute | solution.py:282
  80.3 14.8 %all_to_all.10 = f32[16,16,256]{2,1,0:T(8,128)S(1)} all-to-all(f32[16,16,256]{2,1,0:T(8,128)S(1)} %bitcast.4), channel_id=1, replica_groups=mesh['off'=16,'dep'=2] {'off'}, dimensions={0} | all-to-all | bytes 524288 | tf_op jit(solution)/shard_map/all_to_all | solution.py:397
  95.1 12.8 %all_to_all.11 = f32[16,16,256]{2,1,0:T(8,128)S(1)} all-to-all(f32[16,16,256]{2,1,0:T(8,128)S(1)} %broadcast_in_dim.2), channel_id=1, replica_groups=mesh['off'=16,'dep'=2] {'off'}, dimensions={0} | all-to-all | bytes 524288 | tf_op jit(solution)/shard_map/all_to_all | solution.py:399
  108.0 0.7 copy.13
  (71 shorter events, 7.8 us)
Async XLA Ops:
  0.0 45.8 %copy-start = (bf16[12,4,64,256]{3,2,1,0:T(8,128)(2,1)S(1)}, bf16[12,4,64,256]{3,2,1,0:T(8,128)(2,1)}, u32[]{:S(2)}) copy-start(bf16[12,4,64,256]{3,2,1,0:T(8,128)(2,1)} %own_reflect.1) | copy-start | bytes 4718596
  0.0 50.5 %copy-start.20 = (s32[12]{0:T(128)S(1)}, s32[12]{0:T(128)}, u32[]{:S(2)}) copy-start(s32[12]{0:T(128)} %lags_ref.5) | copy-start | bytes 148
  0.0 50.5 %copy-start.19 = (s32[8]{0:T(128)S(1)}, s32[8]{0:T(128)}, u32[]{:S(2)}) copy-start(s32[8]{0:T(128)} %owners_ref.5) | copy-start | bytes 100
  0.0 9.5 %collective-permute-start = (bf16[1,4,64,256]{3,2,1,0:T(8,128)(2,1)}, bf16[1,4,64,256]{3,2,1,0:T(8,128)(2,1)S(1)}, u32[]{:S(2)}, u32[]{:S(2)}) collective-permute-start(bf16[1,4,64,256]{3,2,1,0:T(8,128)(2,1)} %refs_0_.1), channel_id=1, source_target_pairs={{0,8},{2,10},{4,12},{6,14},{8,0},{10,2},{12,4},{14,6},{16,24},{18,... | collective-permute-start | bytes 393224 | tf_op jit(solution)/shard_map/ppermute | solution.py:287
  3.1 13.1 %collective-permute-start.1 = (bf16[1,4,64,256]{3,2,1,0:T(8,128)(2,1)}, bf16[1,4,64,256]{3,2,1,0:T(8,128)(2,1)S(1)}, u32[]{:S(2)}, u32[]{:S(2)}) collective-permute-start(bf16[1,4,64,256]{3,2,1,0:T(8,128)(2,1)} %refs_0_.1), channel_id=1, source_target_pairs={{0,16},{2,18},{4,20},{6,22},{8,24},{10,26},{12,28},{14,30},{16,0},... | collective-permute-start | bytes 393224 | tf_op jit(solution)/shard_map/ppermute | solution.py:287
  5.7 10.5 %collective-permute-start.2 = (bf16[1,4,64,256]{3,2,1,0:T(8,128)(2,1)}, bf16[1,4,64,256]{3,2,1,0:T(8,128)(2,1)S(1)}, u32[]{:S(2)}, u32[]{:S(2)}) collective-permute-start(bf16[1,4,64,256]{3,2,1,0:T(8,128)(2,1)} %refs_0_.1), channel_id=1, source_target_pairs={{0,24},{2,26},{4,28},{6,30},{8,16},{10,18},{12,20},{14,22},{16,8},... | collective-permute-start | bytes 393224 | tf_op jit(solution)/shard_map/ppermute | solution.py:287
  5.7 13.6 %collective-permute-start.13 = (bf16[1,4,64,256]{3,2,1,0:T(8,128)(2,1)}, bf16[1,4,64,256]{3,2,1,0:T(8,128)(2,1)S(1)}, u32[]{:S(2)}, u32[]{:S(2)}) collective-permute-start(bf16[1,4,64,256]{3,2,1,0:T(8,128)(2,1)} %refs_0_.1), channel_id=1, source_target_pairs={{0,2},{2,0},{4,6},{6,4},{8,10},{10,8},{12,14},{14,12},{16,18},{18,... | collective-permute-start | bytes 393224 | tf_op jit(solution)/shard_map/ppermute | solution.py:287
  9.5 36.2 %collective-permute-start.9 = (bf16[6,4,64,256]{3,2,1,0:T(8,128)(2,1)}, bf16[6,4,64,256]{3,2,1,0:T(8,128)(2,1)S(1)}, u32[]{:S(2)}, u32[]{:S(2)}) collective-permute-start(bf16[6,4,64,256]{3,2,1,0:T(8,128)(2,1)} %constant_dynamic-slice_fusion), channel_id=1, source_target_pairs={{0,1},{1,0},{2,3},{3,2},{4,5},{5,4},{6,7},{7,6},{8,9},{9,8},{10,11... | collective-permute-start | bytes 2359304 | tf_op jit(solution)/shard_map/ppermute | solution.py:282
  16.3 18.7 %collective-permute-start.3 = (bf16[3,4,64,256]{3,2,1,0:T(8,128)(2,1)S(1)}, bf16[3,4,64,256]{3,2,1,0:T(8,128)(2,1)S(1)}, u32[]{:S(2)}, u32[]{:S(2)}) collective-permute-start(bf16[3,4,64,256]{3,2,1,0:T(8,128)(2,1)S(1)} %constant_dynamic-update-slice_fusion.refs_4_), channel_id=1, source_target_pairs={{0,2},{2,0},{4,6},{6,4},{8,10},{10,8},{12,14},{14,12},{16,18},{18,... | collective-permute-start | bytes 1179656 | tf_op jit(solution)/shard_map/ppermute | solution.py:287
  17.8 5.2 %collective-permute-start.14 = (bf16[1,4,64,256]{3,2,1,0:T(8,128)(2,1)}, bf16[1,4,64,256]{3,2,1,0:T(8,128)(2,1)S(1)}, u32[]{:S(2)}, u32[]{:S(2)}) collective-permute-start(bf16[1,4,64,256]{3,2,1,0:T(8,128)(2,1)} %refs_0_.1), channel_id=1, source_target_pairs={{0,4},{2,6},{4,0},{6,2},{8,12},{10,14},{12,8},{14,10},{16,20},{18,... | collective-permute-start | bytes 393224 | tf_op jit(solution)/shard_map/ppermute | solution.py:287
  19.3 6.7 %collective-permute-start.10 = (f32[4,64,256]{2,1,0:T(8,128)}, f32[4,64,256]{2,1,0:T(8,128)S(1)}, u32[]{:S(2)}, u32[]{:S(2)}) collective-permute-start(f32[4,64,256]{2,1,0:T(8,128)} %own_courant.1), channel_id=1, source_target_pairs={{0,1},{1,0},{2,3},{3,2},{4,5},{5,4},{6,7},{7,6},{8,9},{9,8},{10,11... | collective-permute-start | bytes 786440 | tf_op jit(solution)/shard_map/ppermute | solution.py:282
  19.4 6.1 %collective-permute-start.16 = (bf16[1,4,64,256]{3,2,1,0:T(8,128)(2,1)}, bf16[1,4,64,256]{3,2,1,0:T(8,128)(2,1)S(1)}, u32[]{:S(2)}, u32[]{:S(2)}) collective-permute-start(bf16[1,4,64,256]{3,2,1,0:T(8,128)(2,1)} %refs_0_.1), channel_id=1, source_target_pairs={{0,1},{1,0},{2,3},{3,2},{4,5},{5,4},{6,7},{7,6},{8,9},{9,8},{10,11... | collective-permute-start | bytes 393224 | tf_op jit(solution)/shard_map/ppermute | solution.py:282
  23.0 17.0 %collective-permute-start.5 = (bf16[3,4,64,256]{3,2,1,0:T(8,128)(2,1)S(1)}, bf16[3,4,64,256]{3,2,1,0:T(8,128)(2,1)S(1)}, u32[]{:S(2)}, u32[]{:S(2)}) collective-permute-start(bf16[3,4,64,256]{3,2,1,0:T(8,128)(2,1)S(1)} %constant_dynamic-update-slice_fusion.refs_4_), channel_id=1, source_target_pairs={{0,4},{2,6},{4,0},{6,2},{8,12},{10,14},{12,8},{14,10},{16,20},{18,... | collective-permute-start | bytes 1179656 | tf_op jit(solution)/shard_map/ppermute | solution.py:287
  26.1 8.3 %collective-permute-start.15 = (bf16[1,4,64,256]{3,2,1,0:T(8,128)(2,1)}, bf16[1,4,64,256]{3,2,1,0:T(8,128)(2,1)S(1)}, u32[]{:S(2)}, u32[]{:S(2)}) collective-permute-start(bf16[1,4,64,256]{3,2,1,0:T(8,128)(2,1)} %copy-done.5), channel_id=1, source_target_pairs={{0,4},{2,6},{4,0},{6,2},{8,12},{10,14},{12,8},{14,10},{16,20},{18,... | collective-permute-start | bytes 393224 | tf_op jit(solution)/shard_map/ppermute | solution.py:287
  26.8 9.4 %collective-permute-start.17 = (bf16[1,4,64,256]{3,2,1,0:T(8,128)(2,1)}, bf16[1,4,64,256]{3,2,1,0:T(8,128)(2,1)S(1)}, u32[]{:S(2)}, u32[]{:S(2)}) collective-permute-start(bf16[1,4,64,256]{3,2,1,0:T(8,128)(2,1)} %copy-done.5), channel_id=1, source_target_pairs={{0,1},{1,0},{2,3},{3,2},{4,5},{5,4},{6,7},{7,6},{8,9},{9,8},{10,11... | collective-permute-start | bytes 393224 | tf_op jit(solution)/shard_map/ppermute | solution.py:282
  34.4 3.9 %collective-permute-start.18 = (bf16[1,4,64,256]{3,2,1,0:T(8,128)(2,1)S(1)}, bf16[1,4,64,256]{3,2,1,0:T(8,128)(2,1)S(1)}, u32[]{:S(2)}, u32[]{:S(2)}) collective-permute-start(bf16[1,4,64,256]{3,2,1,0:T(8,128)(2,1)S(1)} %collective-permute-done.14.refs_2_), channel_id=1, source_target_pairs={{0,1},{1,0},{2,3},{3,2},{4,5},{5,4},{6,7},{7,6},{8,9},{9,8},{10,11... | collective-permute-start | bytes 393224 | tf_op jit(solution)/shard_map/ppermute | solution.py:282
  35.0 3.9 %collective-permute-start.19 = (bf16[1,4,64,256]{3,2,1,0:T(8,128)(2,1)S(1)}, bf16[1,4,64,256]{3,2,1,0:T(8,128)(2,1)S(1)}, u32[]{:S(2)}, u32[]{:S(2)}) collective-permute-start(bf16[1,4,64,256]{3,2,1,0:T(8,128)(2,1)S(1)} %collective-permute-done.15.refs_3_), channel_id=1, source_target_pairs={{0,1},{1,0},{2,3},{3,2},{4,5},{5,4},{6,7},{7,6},{8,9},{9,8},{10,11... | collective-permute-start | bytes 393224 | tf_op jit(solution)/shard_map/ppermute | solution.py:282
  36.9 8.3 %collective-permute-start.4 = (bf16[2,4,64,256]{3,2,1,0:T(8,128)(2,1)S(1)}, bf16[2,4,64,256]{3,2,1,0:T(8,128)(2,1)}, u32[]{:S(2)}, u32[]{:S(2)}) collective-permute-start(bf16[2,4,64,256]{3,2,1,0:T(8,128)(2,1)S(1)} %slice.8), channel_id=1, source_target_pairs={{0,4},{2,6},{4,0},{6,2},{8,12},{10,14},{12,8},{14,10},{16,20},{18,... | collective-permute-start | bytes 786440 | tf_op jit(solution)/shard_map/ppermute | solution.py:287
  38.9 11.5 %collective-permute-start.20 = (bf16[3,4,64,256]{3,2,1,0:T(8,128)(2,1)S(1)}, bf16[3,4,64,256]{3,2,1,0:T(8,128)(2,1)}, u32[]{:S(2)}, u32[]{:S(2)}) collective-permute-start(bf16[3,4,64,256]{3,2,1,0:T(8,128)(2,1)S(1)} %constant_dynamic-update-slice_fusion.refs_4_), channel_id=1, source_target_pairs={{0,1},{1,0},{2,3},{3,2},{4,5},{5,4},{6,7},{7,6},{8,9},{9,8},{10,11... | collective-permute-start | bytes 1179656 | tf_op jit(solution)/shard_map/ppermute | solution.py:282
  39.6 27.7 %collective-permute-start.11 = (bf16[3,4,64,256]{3,2,1,0:T(8,128)(2,1)S(1)}, bf16[3,4,64,256]{3,2,1,0:T(8,128)(2,1)}, u32[]{:S(2)}, u32[]{:S(2)}) collective-permute-start(bf16[3,4,64,256]{3,2,1,0:T(8,128)(2,1)S(1)} %collective-permute-done.3.refs_0_), channel_id=1, source_target_pairs={{0,1},{1,0},{2,3},{3,2},{4,5},{5,4},{6,7},{7,6},{8,9},{9,8},{10,11... | collective-permute-start | bytes 1179656 | tf_op jit(solution)/shard_map/ppermute | solution.py:282
  40.1 27.2 %collective-permute-start.12 = (bf16[3,4,64,256]{3,2,1,0:T(8,128)(2,1)S(1)}, bf16[3,4,64,256]{3,2,1,0:T(8,128)(2,1)}, u32[]{:S(2)}, u32[]{:S(2)}) collective-permute-start(bf16[3,4,64,256]{3,2,1,0:T(8,128)(2,1)S(1)} %collective-permute-done.5.refs_1_), channel_id=1, source_target_pairs={{0,1},{1,0},{2,3},{3,2},{4,5},{5,4},{6,7},{7,6},{8,9},{9,8},{10,11... | collective-permute-start | bytes 1179656 | tf_op jit(solution)/shard_map/ppermute | solution.py:282
  45.2 5.3 %collective-permute-start.6 = (bf16[1,4,64,256]{3,2,1,0:T(8,128)(2,1)}, bf16[1,4,64,256]{3,2,1,0:T(8,128)(2,1)}, u32[]{:S(2)}, u32[]{:S(2)}) collective-permute-start(bf16[1,4,64,256]{3,2,1,0:T(8,128)(2,1)} %slice.9), channel_id=1, source_target_pairs={{0,2},{2,0},{4,6},{6,4},{8,10},{10,8},{12,14},{14,12},{16,18},{18,... | collective-permute-start | bytes 393224 | tf_op jit(solution)/shard_map/ppermute | solution.py:287
  45.7 24.6 %collective-permute-start.7 = (bf16[2,4,64,256]{3,2,1,0:T(8,128)(2,1)}, bf16[2,4,64,256]{3,2,1,0:T(8,128)(2,1)S(1)}, u32[]{:S(2)}, u32[]{:S(2)}) collective-permute-start(bf16[2,4,64,256]{3,2,1,0:T(8,128)(2,1)} %collective-permute-done.4.refs_0_), channel_id=1, source_target_pairs={{0,1},{1,0},{2,3},{3,2},{4,5},{5,4},{6,7},{7,6},{8,9},{9,8},{10,11... | collective-permute-start | bytes 786440 | tf_op jit(solution)/shard_map/ppermute | solution.py:282
  45.8 1.0 copy-start.1
  46.7 0.9 copy-start.3
  50.5 19.9 %collective-permute-start.8 = (bf16[1,4,64,256]{3,2,1,0:T(8,128)(2,1)}, bf16[1,4,64,256]{3,2,1,0:T(8,128)(2,1)S(1)}, u32[]{:S(2)}, u32[]{:S(2)}) collective-permute-start(bf16[1,4,64,256]{3,2,1,0:T(8,128)(2,1)} %collective-permute-done.6.refs_1_), channel_id=1, source_target_pairs={{0,1},{1,0},{2,3},{3,2},{4,5},{5,4},{6,7},{7,6},{8,9},{9,8},{10,11... | collective-permute-start | bytes 393224 | tf_op jit(solution)/shard_map/ppermute | solution.py:282
  50.5 0.9 copy-start.4
  51.4 0.9 copy-start.6
  52.3 0.9 copy-start.8
  55.9 0.9 copy-start.16
  56.8 0.9 copy-start.18
  78.2 2.1 %collective-permute-start.21 = (f32[4,64,256]{2,1,0:T(8,128)S(1)}, f32[4,64,256]{2,1,0:T(8,128)S(1)}, u32[]{:S(2)}, u32[]{:S(2)}) collective-permute-start(f32[4,64,256]{2,1,0:T(8,128)S(1)} %get-tuple-element.16), channel_id=1, source_target_pairs={{0,1},{1,0},{2,3},{3,2},{4,5},{5,4},{6,7},{7,6},{8,9},{9,8},{10,11... | collective-permute-start | bytes 786440 | tf_op jit(solution)/shard_map/ppermute | solution.py:282
  (11 other events, 8.0 us)

commit v2 on v1

--- a/solution.py
+++ b/solution.py
@@ -90,14 +90,18 @@
     return high, (v - high.astype(F32)).astype(BF16)
 
 
+EXACT_WEIGHTS = tuple(w / 4096.0 for w in (-43050.0, 8064.0, -1008.0, 128.0, -9.0))
+SCALE = 4096.0 / 5040.0
+
+
 def band(rows, columns, block):
     i = lax.broadcasted_iota(jnp.int32, (rows, columns), 0)
     j = lax.broadcasted_iota(jnp.int32, (rows, columns), 1)
     apart = jnp.where(i // block == j // block, jnp.abs(i - j), 0)
     full = jnp.zeros((rows, columns), F32)
     for k in range(1, REACH + 1):
-        full = jnp.where(apart == k, STENCIL_WEIGHTS[k], full)
-    return split(full)
+        full = jnp.where(apart == k, EXACT_WEIGHTS[k], full)
+    return full.astype(BF16)
 
 
 def copy(source, target, sem):
@@ -111,23 +115,24 @@
     offsets, blocks = rt.shape[:2]
     stack = 128 // rows
     here, there = pl.ds(core * half, half), pl.ds((1 - core) * half, half)
+    mine = pl.ds(core * offsets, offsets)
     moves = [
-        copy(own_courant, cour.at[here], sems.at[0]),
-        copy(far_courant, cour.at[there], sems.at[1]),
-        copy(own_reflect.at[pl.ds(core * offsets, offsets)], refl.at[:, here], sems.at[2]),
-        copy(far_reflect, refl.at[:, there], sems.at[3]),
+        copy(own_reflect.at[mine], refl.at[:, here], sems.at[0]),
+        copy(far_reflect, refl.at[:, there], sems.at[1]),
+        copy(own_courant, cour.at[here], sems.at[2]),
+        copy(far_courant, cour.at[there], sems.at[3]),
     ]
     for move in moves:
         move.start()
-    high, low = band(columns, columns, columns)
-    for i, part in enumerate((high, low, high)):
-        across[i * columns : (i + 1) * columns] = part
+    wide = band(columns, columns, columns)
     group = down.shape[0]
-    high, low = band(group, group, rows)
-    for i, part in enumerate((high, low, high)):
-        down[:, i * group : (i + 1) * group] = part
+    tall = band(group, group, rows)
+    for i in range(2):
+        across[i * columns : (i + 1) * columns] = wide
+        down[:, i * group : (i + 1) * group] = tall
     for move in moves:
         move.wait()
+    cour[...] = cour[...] * SCALE
 
     def turn(h, carry):
         for b in range(blocks):
@@ -139,11 +144,11 @@
 
 
 def vertical(plane_of, z, depth):
-    total = (3.0 * STENCIL_WEIGHTS[0]) * plane_of(z)
+    total = EXACT_WEIGHTS[0] * plane_of(z)
     for k in range(1, REACH + 1):
         near = [plane_of(n) for n in (z - k, z + k) if 0 <= n < depth]
         if near:
-            total = total + STENCIL_WEIGHTS[k] * functools.reduce(jnp.add, near)
+            total = total + EXACT_WEIGHTS[k] * functools.reduce(jnp.add, near)
     return total
 
 
@@ -155,16 +160,14 @@
     return x_part + y_part
 
 
-def source_of(field, lag_of, rt, cour, across, down, plain, shifted, turned, source):
+def source_of(lag_of, rt, cour, across, down, plain, shifted, turned, source):
     depth, rows, columns = cour.shape
     offsets, blocks = rt.shape[:2]
     group = down.shape[0]
     planes, tiles, stack = group // rows, group // 128, 128 // rows
-    for z in range(depth):
-        plain[z] = field[z].astype(F32)
     for g in range(depth // planes):
-        high = jnp.concatenate([field[g * planes + p] for p in range(planes)], 0)
-        both = sideways([high, high], across, down)
+        high = jnp.concatenate([plain[g * planes + p].astype(BF16) for p in range(planes)], 0)
+        both = sideways([high], across, down)
         for b in range(tiles):
             pieces = []
             for i in range(stack):
@@ -193,45 +196,30 @@
         shifted[b, LAG + columns : 2 * LAG + columns] = jnp.zeros((LAG, 128), F32)
 
 
-def fetch_fields(where_ref, owners_ref, choose, fields, sems, half):
-    place, core = where_ref[0], where_ref[1]
-    here, there = pl.ds(core * half, half), pl.ds((1 - core) * half, half)
-    for t in range(ITERS):
-        for test, at, own, far in choose(owners_ref[t] ^ place):
-
-            @pl.when(test)
-            def _(at=at, own=own, far=far, t=t):
-                copy(own.at[at], fields.at[t, here], sems.at[t, 0]).start()
-                copy(far.at[at], fields.at[t, there], sems.at[t, 1]).start()
-
-
-def held(where_ref, owners_ref, choose, t):
-    tests = [test for test, *_ in choose(owners_ref[t] ^ where_ref[0])]
-    return functools.reduce(jnp.logical_or, tests)
-
-
-def wait_fields(fields, sems, t, half):
-    for i in range(2):
-        part = fields.at[t, pl.ds(i * half, half)]
-        copy(part, part, sems.at[t, i]).wait()
+def take_field(tests, core, plain):
+    for test, at, own, far in tests:
+        half = own.shape[1]
+
+        @pl.when(test)
+        def _(at=at, own=own, far=far, half=half):
+            for z in range(half):
+                plain[core * half + z] = own[at, z].astype(F32)
+                plain[(1 - core) * half + z] = far[at, z].astype(F32)
 
 
 def sums_kernel(
-    choose, where_ref, owners_ref, lags_ref, rt, cour, across, down, sums,
-    fields, plain, shifted, turned, field_sems,
+    choose, where_ref, owners_ref, lags_ref, rt, cour, across, down, sums, plain, shifted, turned,
 ):
-    depth = cour.shape[0]
     first = where_ref[1] * rt.shape[0]
-    fetch_fields(where_ref, owners_ref, choose, fields, field_sems, depth // 2)
     clear_rims(shifted, cour.shape[2])
 
     def step(t, carry):
-        @pl.when(held(where_ref, owners_ref, choose, t))
+        tests = choose(owners_ref[t] ^ where_ref[0])
+
+        @pl.when(functools.reduce(jnp.logical_or, [test for test, *_ in tests]))
         def _():
-            wait_fields(fields, field_sems, t, depth // 2)
-            source_of(
-                fields.at[t], lambda h: lags_ref[first + h], rt, cour, across, down, plain, shifted, turned, sums.at[t]
-            )
+            take_field(tests, where_ref[1], plain)
+            source_of(lambda h: lags_ref[first + h], rt, cour, across, down, plain, shifted, turned, sums.at[t])
 
         return carry
 
@@ -240,11 +228,10 @@
 
 def steps_kernel(
     choose, where_ref, owners_ref, lags_ref, rt, cour, across, down, kept_ref, given_ref, sums,
-    fields, plain, shifted, turned, field_sems, wave_a, wave_b,
+    plain, shifted, turned, wave_a, wave_b,
 ):
     sums_kernel(
-        choose, where_ref, owners_ref, lags_ref, rt, cour, across, down, sums,
-        fields, plain, shifted, turned, field_sems,
+        choose, where_ref, owners_ref, lags_ref, rt, cour, across, down, sums, plain, shifted, turned
     )
     depth, rows, _ = cour.shape
     half = depth // 2
@@ -254,7 +241,7 @@
     def grow(t, now, before):
         for g in range(depth // planes):
             high, low = split(jnp.concatenate([now[g * planes + p] for p in range(planes)], 0))
-            both = sideways([high, high, low], across, down)
+            both = sideways([high, low], across, down)
             for p in range(planes):
                 z = g * planes + p
                 laplace = both[p * rows : (p + 1) * rows] + vertical(lambda n: now[n], z, depth)
@@ -305,10 +292,6 @@
     sent = lax.dynamic_slice_in_dim(reflect, (1 - core) * mine, mine, 0)
     far_reflect = swapped(sent)
     far_courant = swapped(courant)
-    z_all = jnp.concatenate(z_parts, 0)
-    z_x, z_y = flip(z_all, 1), flip(z_all, 2)
-    d_x = flip(z_x[:cut], 2)
-    d_y = flip(z_y[cut:], 1)
 
     smem = pl.BlockSpec(memory_space=pltpu.SMEM)
     anyspace = pl.BlockSpec(memory_space=pl.ANY)
@@ -317,29 +300,34 @@
     tables = [
         jax.ShapeDtypeStruct((mine, blocks, columns, 128), BF16),
         jax.ShapeDtypeStruct((depth, rows, columns), F32),
-        jax.ShapeDtypeStruct((3 * columns, columns), BF16),
-        jax.ShapeDtypeStruct((group, 3 * group), BF16),
+        jax.ShapeDtypeStruct((2 * columns, columns), BF16),
+        jax.ShapeDtypeStruct((group, 2 * group), BF16),
     ]
     prepare = pl.pallas_call(
         prepare_kernel,
         out_shape=tables,
         in_specs=[smem] + [anyspace] * 4,
         out_specs=[vmem] * 4,
-        scratch_shapes=[pltpu.VMEM((mine, depth, rows, columns), BF16), pltpu.SemaphoreType.DMA((4,))],
-        compiler_params=pltpu.CompilerParams(vmem_limit_bytes=16 << 20),
+        scratch_shapes=[
+            pltpu.VMEM((mine, depth, rows, columns), BF16),
+            pltpu.SemaphoreType.DMA((4,)),
+        ],
+        compiler_params=pltpu.CompilerParams(vmem_limit_bytes=8 << 20),
         cost_estimate=pl.CostEstimate(flops=10**7, bytes_accessed=6 << 20, transcendentals=0),
     )
     prepared = prepare(where[1:], reflect, far_reflect, courant, far_courant)
+    z_all = jnp.concatenate(z_parts, 0)
+    z_x, z_y = flip(z_all, 1), flip(z_all, 2)
+    d_x = flip(z_x[:cut], 2)
+    d_y = flip(z_y[cut:], 1)
 
     scratch = [
-        pltpu.VMEM((ITERS, depth, rows, columns), BF16),
         pltpu.VMEM((depth, rows, columns), F32),
         pltpu.VMEM((blocks, columns + 2 * LAG, 128), F32),
         pltpu.VMEM((blocks, columns, 128), F32),
-        pltpu.SemaphoreType.DMA((ITERS, 2)),
     ]
     waves = [pltpu.VMEM((depth, rows, columns), F32)] * 2
-    params = pltpu.CompilerParams(vmem_limit_bytes=32 << 20)
+    params = pltpu.CompilerParams(vmem_limit_bytes=12 << 20)
     cost = pl.CostEstimate(flops=10**9, bytes_accessed=10 << 20, transcendentals=0)
     sums_shape = jax.ShapeDtypeStruct((ITERS, depth, rows, columns), F32)
 
@@ -378,7 +366,7 @@
 
         return pl.pallas_call(
             kernel,
-            in_specs=[smem] * 3 + [anyspace] * (2 * n) + [vmem] * (4 + len(extra)),
+            in_specs=[smem] * 3 + [vmem] * (2 * n + 4 + len(extra)),
             out_shape=out_shape,
             out_specs=[vmem] * len(out_shape),
             scratch_shapes=scratch + list(more_scratch),

time: 109 us -> 106 us (0.972)
  Pallas kernels: 21.7 us -> 16.9 us
  blocking collectives: 27.6 us -> 28.7 us
    pallas_call x3, Pallas kernels: 20.4 us -> 15.6 us  [run(): pl.pallas_call(kernel, in_specs=[smem] * 3 + [vmem] * (2 * n + 4 + len(ex...]
  transfers between devices with their start and end apart: 22 -> 22, of which waited for: 6 -> 6; matrix products, arithmetic and copies ran while one was open for 3% -> 3% of each run, Pallas kernels for 13% -> 10%
where the time goes in v2:
time: 106 us; the launch traced here: 105 us
  blocking collectives  28.7 us (27%)
  waiting for transfers between devices  24.3 us (23%)
  local copies, waits for them, and re-layouts  17.4 us (16%)
  starting transfers between devices  17.3 us (16%)
  Pallas kernels  16.9 us (16%)
    ppermute x10, waiting for transfers between devices, flip(): return lax.ppermute(x, 'off', [(i, i ^ bits) for i in range(count)])  23.1 us
    all_to_all x1, blocking collectives, core_pair(): summed = lax.all_to_all(pieces, 'off', 0, 0).sum(0)  15.9 us
    pallas_call x3, Pallas kernels, run(): pl.pallas_call(kernel, in_specs=[smem] * 3 + [vmem] * (2 * n + 4 + len(ex...  15.6 us
    ppermute x10, starting transfers between devices, flip(): return lax.ppermute(x, 'off', [(i, i ^ bits) for i in range(count)])  14.8 us
    unnamed x45, local copies, waits for them, and re-layouts  14.6 us
    all_to_all x1, blocking collectives, core_pair(): return lax.all_to_all(spread, 'off', 0, 0).reshape(half, rows, columns)  12.8 us
    ppermute x12, starting transfers between devices, swapped(): return lax.ppermute(x, 'dep', [(0, 1), (1, 0)])  2.46 us
  transfers between devices with their start and end apart: 22, of which 6 were waited for; matrix products, arithmetic and copies ran while one was open for 3% of the time, Pallas kernels for 10%

profile of v2, /device:TPU:0, one launch (start us, length us, event | category | flops | bytes accessed | tf_op | source)
XLA Modules:
  0.0 105.0 jit_solution(9400311720150264358)
XLA Ops:
  0.0 3.1 %collective-permute-start = (bf16[1,4,64,256]{3,2,1,0:T(8,128)(2,1)}, bf16[1,4,64,256]{3,2,1,0:T(8,128)(2,1)S(1)}, u32[]{:S(2)}, u32[]{:S(2)}) collective-permute-start(bf16[1,4,64,256]{3,2,1,0:T(8,128)(2,1)} %refs_0_.1), channel_id=1, source_target_pairs={{0,8},{2,10},{4,12},{6,14},{8,0},{10,2},{12,4},{14,6},{16,24},{18,... | collective-permute-start | bytes 393224 | tf_op jit(solution)/shard_map/ppermute | solution.py:274
  3.1 2.6 %collective-permute-start.1 = (bf16[1,4,64,256]{3,2,1,0:T(8,128)(2,1)}, bf16[1,4,64,256]{3,2,1,0:T(8,128)(2,1)S(1)}, u32[]{:S(2)}, u32[]{:S(2)}) collective-permute-start(bf16[1,4,64,256]{3,2,1,0:T(8,128)(2,1)} %refs_0_.1), channel_id=1, source_target_pairs={{0,16},{2,18},{4,20},{6,22},{8,24},{10,26},{12,28},{14,30},{16,0},... | collective-permute-start | bytes 393224 | tf_op jit(solution)/shard_map/ppermute | solution.py:274
  5.7 1.7 %collective-permute-start.13 = (bf16[1,4,64,256]{3,2,1,0:T(8,128)(2,1)}, bf16[1,4,64,256]{3,2,1,0:T(8,128)(2,1)S(1)}, u32[]{:S(2)}, u32[]{:S(2)}) collective-permute-start(bf16[1,4,64,256]{3,2,1,0:T(8,128)(2,1)} %refs_0_.1), channel_id=1, source_target_pairs={{0,2},{2,0},{4,6},{6,4},{8,10},{10,8},{12,14},{14,12},{16,18},{18,... | collective-permute-start | bytes 393224 | tf_op jit(solution)/shard_map/ppermute | solution.py:274
  7.4 2.1 %constant_dynamic-slice_fusion = bf16[6,4,64,256]{3,2,1,0:T(8,128)(2,1)} fusion(bf16[12,4,64,256]{3,2,1,0:T(8,128)(2,1)} %own_reflect.1, s32[]{:T(128)S(6)} %select_n.3), kind=kLoop, calls=%fused_computation.4 | loop fusion | bytes 1572868 | tf_op jit(solution)/shard_map/dynamic_slice | solution.py:292
  9.6 6.7 %collective-permute-done.1 = bf16[1,4,64,256]{3,2,1,0:T(8,128)(2,1)S(1)} collective-permute-done((bf16[1,4,64,256]{3,2,1,0:T(8,128)(2,1)}, bf16[1,4,64,256]{3,2,1,0:T(8,128)(2,1)S(1)}, u32[]{:S(2)}, u32[]{:S(2)}) %collective-permute-start.1) | collective-permute-done | bytes 131104 | tf_op jit(solution)/shard_map/ppermute | solution.py:274
  16.3 1.6 %collective-permute-start.3 = (bf16[3,4,64,256]{3,2,1,0:T(8,128)(2,1)S(1)}, bf16[3,4,64,256]{3,2,1,0:T(8,128)(2,1)S(1)}, u32[]{:S(2)}, u32[]{:S(2)}) collective-permute-start(bf16[3,4,64,256]{3,2,1,0:T(8,128)(2,1)S(1)} %constant_dynamic-update-slice_fusion.refs_4_), channel_id=1, source_target_pairs={{0,2},{2,0},{4,6},{6,4},{8,10},{10,8},{12,14},{14,12},{16,18},{18,... | collective-permute-start | bytes 1179656 | tf_op jit(solution)/shard_map/ppermute | solution.py:274
  17.8 1.5 %collective-permute-start.14 = (bf16[1,4,64,256]{3,2,1,0:T(8,128)(2,1)}, bf16[1,4,64,256]{3,2,1,0:T(8,128)(2,1)S(1)}, u32[]{:S(2)}, u32[]{:S(2)}) collective-permute-start(bf16[1,4,64,256]{3,2,1,0:T(8,128)(2,1)} %refs_0_.1), channel_id=1, source_target_pairs={{0,4},{2,6},{4,0},{6,2},{8,12},{10,14},{12,8},{14,10},{16,20},{18,... | collective-permute-start | bytes 393224 | tf_op jit(solution)/shard_map/ppermute | solution.py:274
  20.0 3.0 %collective-permute-done.14.refs_2_ = bf16[1,4,64,256]{3,2,1,0:T(8,128)(2,1)S(1)} collective-permute-done((bf16[1,4,64,256]{3,2,1,0:T(8,128)(2,1)}, bf16[1,4,64,256]{3,2,1,0:T(8,128)(2,1)S(1)}, u32[]{:S(2)}, u32[]{:S(2)}) %collective-permute-start.14) | collective-permute-done | bytes 131104 | tf_op jit(solution)/shard_map/ppermute | solution.py:274
  23.0 2.4 %collective-permute-start.5 = (bf16[3,4,64,256]{3,2,1,0:T(8,128)(2,1)S(1)}, bf16[3,4,64,256]{3,2,1,0:T(8,128)(2,1)S(1)}, u32[]{:S(2)}, u32[]{:S(2)}) collective-permute-start(bf16[3,4,64,256]{3,2,1,0:T(8,128)(2,1)S(1)} %constant_dynamic-update-slice_fusion.refs_4_), channel_id=1, source_target_pairs={{0,4},{2,6},{4,0},{6,2},{8,12},{10,14},{12,8},{14,10},{16,20},{18,... | collective-permute-start | bytes 1179656 | tf_op jit(solution)/shard_map/ppermute | solution.py:274
  26.8 7.6 %collective-permute-done.15.refs_3_ = bf16[1,4,64,256]{3,2,1,0:T(8,128)(2,1)S(1)} collective-permute-done((bf16[1,4,64,256]{3,2,1,0:T(8,128)(2,1)}, bf16[1,4,64,256]{3,2,1,0:T(8,128)(2,1)S(1)}, u32[]{:S(2)}, u32[]{:S(2)}) %collective-permute-start.15) | collective-permute-done | bytes 131104 | tf_op jit(solution)/shard_map/ppermute | solution.py:274
  36.9 1.4 %collective-permute-start.4 = (bf16[2,4,64,256]{3,2,1,0:T(8,128)(2,1)S(1)}, bf16[2,4,64,256]{3,2,1,0:T(8,128)(2,1)}, u32[]{:S(2)}, u32[]{:S(2)}) collective-permute-start(bf16[2,4,64,256]{3,2,1,0:T(8,128)(2,1)S(1)} %slice.8), channel_id=1, source_target_pairs={{0,4},{2,6},{4,0},{6,2},{8,12},{10,14},{12,8},{14,10},{16,20},{18,... | collective-permute-start | bytes 786440 | tf_op jit(solution)/shard_map/ppermute | solution.py:274
  40.8 4.4 %collective-permute-done.4.refs_0_ = bf16[2,4,64,256]{3,2,1,0:T(8,128)(2,1)} collective-permute-done((bf16[2,4,64,256]{3,2,1,0:T(8,128)(2,1)S(1)}, bf16[2,4,64,256]{3,2,1,0:T(8,128)(2,1)}, u32[]{:S(2)}, u32[]{:S(2)}) %collective-permute-start.4) | collective-permute-done | bytes 262176 | tf_op jit(solution)/shard_map/ppermute | solution.py:274
  45.8 0.9 copy-done.1
  46.7 0.9 copy-done.3
  47.7 1.3 %shard_map.55 = (bf16[6,4,256,128]{3,2,1,0:T(8,128)(2,1)S(1)}, f32[8,64,256]{2,1,0:T(8,128)S(1)}, bf16[512,256]{1,0:T(8,128)(2,1)S(1)}, bf16[256,512]{1,0:T(8,128)(2,1)S(1)}) custom-call(s32[1]{0:T(128)} %bitcast.1.core_ref, bf16[12,4,64,256]{3,2,1,0:T(8,128)(2,1)S(1)} %copy-done, bf16[6,4,64,256]{3,2,1,0:T(8,128)(2,1)S(1)} %collective-permute-done.9.far_reflect, ...), custom_call_target="tpu_custom_call" | custom-call | flops 10000000 | bytes 6291456 | tf_op jit(solution)/shard_map/pallas_call | solution.py:318
  49.0 1.5 %collective-permute-done.6.refs_1_ = bf16[1,4,64,256]{3,2,1,0:T(8,128)(2,1)} collective-permute-done((bf16[1,4,64,256]{3,2,1,0:T(8,128)(2,1)}, bf16[1,4,64,256]{3,2,1,0:T(8,128)(2,1)}, u32[]{:S(2)}, u32[]{:S(2)}) %collective-permute-start.6) | collective-permute-done | bytes 131104 | tf_op jit(solution)/shard_map/ppermute | solution.py:274
  50.5 0.9 copy-done.4
  51.4 0.9 copy-done.6
  52.3 0.9 copy-done.8
  53.2 0.9 copy-done.10
  54.1 0.9 copy-done.12
  55.0 0.9 copy-done.14
  55.9 0.9 copy-done.16
  56.8 0.9 copy-done.18
  57.7 7.3 %shard_map.56.refs_8_ = f32[8,8,64,256]{3,2,1,0:T(8,128)S(1)} custom-call(s32[2]{0:T(128)S(1)} %pad_add_fusion.where_ref, s32[8]{0:T(128)S(1)} %copy-done.19, s32[12]{0:T(128)S(1)} %copy-done.20, bf16[1,4,64,256]{3,2,1,0:T(8,128)(2,1)S(1)} %copy-done.4, bf16[1,4,64,256]{3,2,1,0:T(8,128)(2,1)S(1)} %copy-done.6, bf16[1,4,64,256]{3,2,1,0:T(8,128)(2,1)S(1)} %copy-done.8, ...), custom_call_target="tpu_custom_call" | custom-call | flops 1000000000 | bytes 10485760 | tf_op jit(solution)/shard_map/pallas_call | solution.py:367
  65.0 2.3 %shard_map.57.refs_8_ = f32[8,8,64,256]{3,2,1,0:T(8,128)S(1)} custom-call(s32[2]{0:T(128)S(1)} %pad_add_fusion.where_ref, s32[8]{0:T(128)S(1)} %copy-done.19, s32[12]{0:T(128)S(1)} %copy-done.20, bf16[3,4,64,256]{3,2,1,0:T(8,128)(2,1)S(1)} %collective-permute-done.3.refs_0_, ...), custom_call_target="tpu_custom_call", output_to_operand_aliasing={{}: (11, {})} | custom-call | flops 1000000000 | bytes 10485760 | tf_op jit(solution)/shard_map/pallas_call | solution.py:367
  67.4 6.1 %shard_map.58 = (f32[4,64,256]{2,1,0:T(8,128)S(1)}, f32[4,64,256]{2,1,0:T(8,128)S(1)}, f32[8,8,64,256]{3,2,1,0:T(8,128)S(1)}) custom-call(s32[2]{0:T(128)S(1)} %pad_add_fusion.where_ref, s32[8]{0:T(128)S(1)} %copy-done.19, s32[12]{0:T(128)S(1)} %copy-done.20, ...), custom_call_target="tpu_custom_call", output_to_operand_aliasing={{2}: (11, {})} | custom-call | flops 1000000000 | bytes 10485760 | tf_op jit(solution)/shard_map/pallas_call | solution.py:367
  73.4 0.9 collective-permute-start.21
  74.4 1.2 %collective-permute-done.21 = f32[4,64,256]{2,1,0:T(8,128)S(1)} collective-permute-done((f32[4,64,256]{2,1,0:T(8,128)S(1)}, f32[4,64,256]{2,1,0:T(8,128)S(1)}, u32[]{:S(2)}, u32[]{:S(2)}) %collective-permute-start.21) | collective-permute-done | bytes 262176 | tf_op jit(solution)/shard_map/ppermute | solution.py:269
  75.6 15.9 %all_to_all.10 = f32[16,16,256]{2,1,0:T(8,128)S(1)} all-to-all(f32[16,16,256]{2,1,0:T(8,128)S(1)} %bitcast.4), channel_id=1, replica_groups=mesh['off'=16,'dep'=2] {'off'}, dimensions={0} | all-to-all | bytes 524288 | tf_op jit(solution)/shard_map/all_to_all | solution.py:385
  91.5 12.8 %all_to_all.11 = f32[16,16,256]{2,1,0:T(8,128)S(1)} all-to-all(f32[16,16,256]{2,1,0:T(8,128)S(1)} %broadcast_in_dim.2), channel_id=1, replica_groups=mesh['off'=16,'dep'=2] {'off'}, dimensions={0} | all-to-all | bytes 524288 | tf_op jit(solution)/shard_map/all_to_all | solution.py:387
  104.3 0.7 copy.13
  (71 shorter events, 7.8 us)
Async XLA Ops:
  0.0 45.8 %copy-start = (bf16[12,4,64,256]{3,2,1,0:T(8,128)(2,1)S(1)}, bf16[12,4,64,256]{3,2,1,0:T(8,128)(2,1)}, u32[]{:S(2)}) copy-start(bf16[12,4,64,256]{3,2,1,0:T(8,128)(2,1)} %own_reflect.1) | copy-start | bytes 4718596
  0.0 50.5 %copy-start.20 = (s32[12]{0:T(128)S(1)}, s32[12]{0:T(128)}, u32[]{:S(2)}) copy-start(s32[12]{0:T(128)} %lags_ref.5) | copy-start | bytes 148
  0.0 50.5 %copy-start.19 = (s32[8]{0:T(128)S(1)}, s32[8]{0:T(128)}, u32[]{:S(2)}) copy-start(s32[8]{0:T(128)} %owners_ref.5) | copy-start | bytes 100
  0.0 9.5 %collective-permute-start = (bf16[1,4,64,256]{3,2,1,0:T(8,128)(2,1)}, bf16[1,4,64,256]{3,2,1,0:T(8,128)(2,1)S(1)}, u32[]{:S(2)}, u32[]{:S(2)}) collective-permute-start(bf16[1,4,64,256]{3,2,1,0:T(8,128)(2,1)} %refs_0_.1), channel_id=1, source_target_pairs={{0,8},{2,10},{4,12},{6,14},{8,0},{10,2},{12,4},{14,6},{16,24},{18,... | collective-permute-start | bytes 393224 | tf_op jit(solution)/shard_map/ppermute | solution.py:274
  3.1 13.1 %collective-permute-start.1 = (bf16[1,4,64,256]{3,2,1,0:T(8,128)(2,1)}, bf16[1,4,64,256]{3,2,1,0:T(8,128)(2,1)S(1)}, u32[]{:S(2)}, u32[]{:S(2)}) collective-permute-start(bf16[1,4,64,256]{3,2,1,0:T(8,128)(2,1)} %refs_0_.1), channel_id=1, source_target_pairs={{0,16},{2,18},{4,20},{6,22},{8,24},{10,26},{12,28},{14,30},{16,0},... | collective-permute-start | bytes 393224 | tf_op jit(solution)/shard_map/ppermute | solution.py:274
  5.7 10.5 %collective-permute-start.2 = (bf16[1,4,64,256]{3,2,1,0:T(8,128)(2,1)}, bf16[1,4,64,256]{3,2,1,0:T(8,128)(2,1)S(1)}, u32[]{:S(2)}, u32[]{:S(2)}) collective-permute-start(bf16[1,4,64,256]{3,2,1,0:T(8,128)(2,1)} %refs_0_.1), channel_id=1, source_target_pairs={{0,24},{2,26},{4,28},{6,30},{8,16},{10,18},{12,20},{14,22},{16,8},... | collective-permute-start | bytes 393224 | tf_op jit(solution)/shard_map/ppermute | solution.py:274
  5.7 13.6 %collective-permute-start.13 = (bf16[1,4,64,256]{3,2,1,0:T(8,128)(2,1)}, bf16[1,4,64,256]{3,2,1,0:T(8,128)(2,1)S(1)}, u32[]{:S(2)}, u32[]{:S(2)}) collective-permute-start(bf16[1,4,64,256]{3,2,1,0:T(8,128)(2,1)} %refs_0_.1), channel_id=1, source_target_pairs={{0,2},{2,0},{4,6},{6,4},{8,10},{10,8},{12,14},{14,12},{16,18},{18,... | collective-permute-start | bytes 393224 | tf_op jit(solution)/shard_map/ppermute | solution.py:274
  9.5 36.2 %collective-permute-start.9 = (bf16[6,4,64,256]{3,2,1,0:T(8,128)(2,1)}, bf16[6,4,64,256]{3,2,1,0:T(8,128)(2,1)S(1)}, u32[]{:S(2)}, u32[]{:S(2)}) collective-permute-start(bf16[6,4,64,256]{3,2,1,0:T(8,128)(2,1)} %constant_dynamic-slice_fusion), channel_id=1, source_target_pairs={{0,1},{1,0},{2,3},{3,2},{4,5},{5,4},{6,7},{7,6},{8,9},{9,8},{10,11... | collective-permute-start | bytes 2359304 | tf_op jit(solution)/shard_map/ppermute | solution.py:269
  16.3 18.7 %collective-permute-start.3 = (bf16[3,4,64,256]{3,2,1,0:T(8,128)(2,1)S(1)}, bf16[3,4,64,256]{3,2,1,0:T(8,128)(2,1)S(1)}, u32[]{:S(2)}, u32[]{:S(2)}) collective-permute-start(bf16[3,4,64,256]{3,2,1,0:T(8,128)(2,1)S(1)} %constant_dynamic-update-slice_fusion.refs_4_), channel_id=1, source_target_pairs={{0,2},{2,0},{4,6},{6,4},{8,10},{10,8},{12,14},{14,12},{16,18},{18,... | collective-permute-start | bytes 1179656 | tf_op jit(solution)/shard_map/ppermute | solution.py:274
  17.8 5.2 %collective-permute-start.14 = (bf16[1,4,64,256]{3,2,1,0:T(8,128)(2,1)}, bf16[1,4,64,256]{3,2,1,0:T(8,128)(2,1)S(1)}, u32[]{:S(2)}, u32[]{:S(2)}) collective-permute-start(bf16[1,4,64,256]{3,2,1,0:T(8,128)(2,1)} %refs_0_.1), channel_id=1, source_target_pairs={{0,4},{2,6},{4,0},{6,2},{8,12},{10,14},{12,8},{14,10},{16,20},{18,... | collective-permute-start | bytes 393224 | tf_op jit(solution)/shard_map/ppermute | solution.py:274
  19.3 6.7 %collective-permute-start.10 = (f32[4,64,256]{2,1,0:T(8,128)}, f32[4,64,256]{2,1,0:T(8,128)S(1)}, u32[]{:S(2)}, u32[]{:S(2)}) collective-permute-start(f32[4,64,256]{2,1,0:T(8,128)} %own_courant.1), channel_id=1, source_target_pairs={{0,1},{1,0},{2,3},{3,2},{4,5},{5,4},{6,7},{7,6},{8,9},{9,8},{10,11... | collective-permute-start | bytes 786440 | tf_op jit(solution)/shard_map/ppermute | solution.py:269
  19.4 6.1 %collective-permute-start.16 = (bf16[1,4,64,256]{3,2,1,0:T(8,128)(2,1)}, bf16[1,4,64,256]{3,2,1,0:T(8,128)(2,1)S(1)}, u32[]{:S(2)}, u32[]{:S(2)}) collective-permute-start(bf16[1,4,64,256]{3,2,1,0:T(8,128)(2,1)} %refs_0_.1), channel_id=1, source_target_pairs={{0,1},{1,0},{2,3},{3,2},{4,5},{5,4},{6,7},{7,6},{8,9},{9,8},{10,11... | collective-permute-start | bytes 393224 | tf_op jit(solution)/shard_map/ppermute | solution.py:269
  23.0 17.0 %collective-permute-start.5 = (bf16[3,4,64,256]{3,2,1,0:T(8,128)(2,1)S(1)}, bf16[3,4,64,256]{3,2,1,0:T(8,128)(2,1)S(1)}, u32[]{:S(2)}, u32[]{:S(2)}) collective-permute-start(bf16[3,4,64,256]{3,2,1,0:T(8,128)(2,1)S(1)} %constant_dynamic-update-slice_fusion.refs_4_), channel_id=1, source_target_pairs={{0,4},{2,6},{4,0},{6,2},{8,12},{10,14},{12,8},{14,10},{16,20},{18,... | collective-permute-start | bytes 1179656 | tf_op jit(solution)/shard_map/ppermute | solution.py:274
  26.1 8.3 %collective-permute-start.15 = (bf16[1,4,64,256]{3,2,1,0:T(8,128)(2,1)}, bf16[1,4,64,256]{3,2,1,0:T(8,128)(2,1)S(1)}, u32[]{:S(2)}, u32[]{:S(2)}) collective-permute-start(bf16[1,4,64,256]{3,2,1,0:T(8,128)(2,1)} %copy-done.5), channel_id=1, source_target_pairs={{0,4},{2,6},{4,0},{6,2},{8,12},{10,14},{12,8},{14,10},{16,20},{18,... | collective-permute-start | bytes 393224 | tf_op jit(solution)/shard_map/ppermute | solution.py:274
  26.8 9.4 %collective-permute-start.17 = (bf16[1,4,64,256]{3,2,1,0:T(8,128)(2,1)}, bf16[1,4,64,256]{3,2,1,0:T(8,128)(2,1)S(1)}, u32[]{:S(2)}, u32[]{:S(2)}) collective-permute-start(bf16[1,4,64,256]{3,2,1,0:T(8,128)(2,1)} %copy-done.5), channel_id=1, source_target_pairs={{0,1},{1,0},{2,3},{3,2},{4,5},{5,4},{6,7},{7,6},{8,9},{9,8},{10,11... | collective-permute-start | bytes 393224 | tf_op jit(solution)/shard_map/ppermute | solution.py:269
  34.4 3.9 %collective-permute-start.18 = (bf16[1,4,64,256]{3,2,1,0:T(8,128)(2,1)S(1)}, bf16[1,4,64,256]{3,2,1,0:T(8,128)(2,1)S(1)}, u32[]{:S(2)}, u32[]{:S(2)}) collective-permute-start(bf16[1,4,64,256]{3,2,1,0:T(8,128)(2,1)S(1)} %collective-permute-done.14.refs_2_), channel_id=1, source_target_pairs={{0,1},{1,0},{2,3},{3,2},{4,5},{5,4},{6,7},{7,6},{8,9},{9,8},{10,11... | collective-permute-start | bytes 393224 | tf_op jit(solution)/shard_map/ppermute | solution.py:269
  35.0 3.9 %collective-permute-start.19 = (bf16[1,4,64,256]{3,2,1,0:T(8,128)(2,1)S(1)}, bf16[1,4,64,256]{3,2,1,0:T(8,128)(2,1)S(1)}, u32[]{:S(2)}, u32[]{:S(2)}) collective-permute-start(bf16[1,4,64,256]{3,2,1,0:T(8,128)(2,1)S(1)} %collective-permute-done.15.refs_3_), channel_id=1, source_target_pairs={{0,1},{1,0},{2,3},{3,2},{4,5},{5,4},{6,7},{7,6},{8,9},{9,8},{10,11... | collective-permute-start | bytes 393224 | tf_op jit(solution)/shard_map/ppermute | solution.py:269
  36.9 8.3 %collective-permute-start.4 = (bf16[2,4,64,256]{3,2,1,0:T(8,128)(2,1)S(1)}, bf16[2,4,64,256]{3,2,1,0:T(8,128)(2,1)}, u32[]{:S(2)}, u32[]{:S(2)}) collective-permute-start(bf16[2,4,64,256]{3,2,1,0:T(8,128)(2,1)S(1)} %slice.8), channel_id=1, source_target_pairs={{0,4},{2,6},{4,0},{6,2},{8,12},{10,14},{12,8},{14,10},{16,20},{18,... | collective-permute-start | bytes 786440 | tf_op jit(solution)/shard_map/ppermute | solution.py:274
  38.9 11.5 %collective-permute-start.20 = (bf16[3,4,64,256]{3,2,1,0:T(8,128)(2,1)S(1)}, bf16[3,4,64,256]{3,2,1,0:T(8,128)(2,1)}, u32[]{:S(2)}, u32[]{:S(2)}) collective-permute-start(bf16[3,4,64,256]{3,2,1,0:T(8,128)(2,1)S(1)} %constant_dynamic-update-slice_fusion.refs_4_), channel_id=1, source_target_pairs={{0,1},{1,0},{2,3},{3,2},{4,5},{5,4},{6,7},{7,6},{8,9},{9,8},{10,11... | collective-permute-start | bytes 1179656 | tf_op jit(solution)/shard_map/ppermute | solution.py:269
  39.6 25.4 %collective-permute-start.11 = (bf16[3,4,64,256]{3,2,1,0:T(8,128)(2,1)S(1)}, bf16[3,4,64,256]{3,2,1,0:T(8,128)(2,1)}, u32[]{:S(2)}, u32[]{:S(2)}) collective-permute-start(bf16[3,4,64,256]{3,2,1,0:T(8,128)(2,1)S(1)} %collective-permute-done.3.refs_0_), channel_id=1, source_target_pairs={{0,1},{1,0},{2,3},{3,2},{4,5},{5,4},{6,7},{7,6},{8,9},{9,8},{10,11... | collective-permute-start | bytes 1179656 | tf_op jit(solution)/shard_map/ppermute | solution.py:269
  40.1 24.9 %collective-permute-start.12 = (bf16[3,4,64,256]{3,2,1,0:T(8,128)(2,1)S(1)}, bf16[3,4,64,256]{3,2,1,0:T(8,128)(2,1)}, u32[]{:S(2)}, u32[]{:S(2)}) collective-permute-start(bf16[3,4,64,256]{3,2,1,0:T(8,128)(2,1)S(1)} %collective-permute-done.5.refs_1_), channel_id=1, source_target_pairs={{0,1},{1,0},{2,3},{3,2},{4,5},{5,4},{6,7},{7,6},{8,9},{9,8},{10,11... | collective-permute-start | bytes 1179656 | tf_op jit(solution)/shard_map/ppermute | solution.py:269
  45.2 5.3 %collective-permute-start.6 = (bf16[1,4,64,256]{3,2,1,0:T(8,128)(2,1)}, bf16[1,4,64,256]{3,2,1,0:T(8,128)(2,1)}, u32[]{:S(2)}, u32[]{:S(2)}) collective-permute-start(bf16[1,4,64,256]{3,2,1,0:T(8,128)(2,1)} %slice.9), channel_id=1, source_target_pairs={{0,2},{2,0},{4,6},{6,4},{8,10},{10,8},{12,14},{14,12},{16,18},{18,... | collective-permute-start | bytes 393224 | tf_op jit(solution)/shard_map/ppermute | solution.py:274
  45.7 21.7 %collective-permute-start.7 = (bf16[2,4,64,256]{3,2,1,0:T(8,128)(2,1)}, bf16[2,4,64,256]{3,2,1,0:T(8,128)(2,1)S(1)}, u32[]{:S(2)}, u32[]{:S(2)}) collective-permute-start(bf16[2,4,64,256]{3,2,1,0:T(8,128)(2,1)} %collective-permute-done.4.refs_0_), channel_id=1, source_target_pairs={{0,1},{1,0},{2,3},{3,2},{4,5},{5,4},{6,7},{7,6},{8,9},{9,8},{10,11... | collective-permute-start | bytes 786440 | tf_op jit(solution)/shard_map/ppermute | solution.py:269
  45.8 1.0 copy-start.1
  46.7 0.9 copy-start.3
  50.5 16.9 %collective-permute-start.8 = (bf16[1,4,64,256]{3,2,1,0:T(8,128)(2,1)}, bf16[1,4,64,256]{3,2,1,0:T(8,128)(2,1)S(1)}, u32[]{:S(2)}, u32[]{:S(2)}) collective-permute-start(bf16[1,4,64,256]{3,2,1,0:T(8,128)(2,1)} %collective-permute-done.6.refs_1_), channel_id=1, source_target_pairs={{0,1},{1,0},{2,3},{3,2},{4,5},{5,4},{6,7},{7,6},{8,9},{9,8},{10,11... | collective-permute-start | bytes 393224 | tf_op jit(solution)/shard_map/ppermute | solution.py:269
  50.5 0.9 copy-start.4
  51.4 0.9 copy-start.6
  52.3 0.9 copy-start.8
  55.9 0.9 copy-start.16
  56.8 0.9 copy-start.18
  73.4 2.1 %collective-permute-start.21 = (f32[4,64,256]{2,1,0:T(8,128)S(1)}, f32[4,64,256]{2,1,0:T(8,128)S(1)}, u32[]{:S(2)}, u32[]{:S(2)}) collective-permute-start(f32[4,64,256]{2,1,0:T(8,128)S(1)} %get-tuple-element.16), channel_id=1, source_target_pairs={{0,1},{1,0},{2,3},{3,2},{4,5},{5,4},{6,7},{7,6},{8,9},{9,8},{10,11... | collective-permute-start | bytes 786440 | tf_op jit(solution)/shard_map/ppermute | solution.py:269
  (11 other events, 8.0 us)

commit v3 on v2

--- a/solution.py
+++ b/solution.py
@@ -104,40 +104,26 @@
     return full.astype(BF16)
 
 
-def copy(source, target, sem):
-    return pltpu.make_async_copy(source, target, sem)
-
-
-def prepare_kernel(core_ref, own_reflect, far_reflect, own_courant, far_courant, rt, cour, across, down, refl, sems):
+def prepare_kernel(core_ref, own_reflect, far_reflect, own_courant, far_courant, rt, cour, across, down):
     core = core_ref[0]
-    half = own_courant.shape[0]
-    rows, columns = cour.shape[1:]
+    half, rows, columns = own_courant.shape
     offsets, blocks = rt.shape[:2]
     stack = 128 // rows
-    here, there = pl.ds(core * half, half), pl.ds((1 - core) * half, half)
-    mine = pl.ds(core * offsets, offsets)
-    moves = [
-        copy(own_reflect.at[mine], refl.at[:, here], sems.at[0]),
-        copy(far_reflect, refl.at[:, there], sems.at[1]),
-        copy(own_courant, cour.at[here], sems.at[2]),
-        copy(far_courant, cour.at[there], sems.at[3]),
-    ]
-    for move in moves:
-        move.start()
+    here, there = core * half, (1 - core) * half
     wide = band(columns, columns, columns)
     group = down.shape[0]
     tall = band(group, group, rows)
     for i in range(2):
         across[i * columns : (i + 1) * columns] = wide
         down[:, i * group : (i + 1) * group] = tall
-    for move in moves:
-        move.wait()
-    cour[...] = cour[...] * SCALE
+    cour[pl.ds(here, half)] = own_courant[...]
+    cour[pl.ds(there, half)] = far_courant[...]
 
     def turn(h, carry):
-        for b in range(blocks):
-            tile = jnp.concatenate([refl[h, stack * b + i] for i in range(stack)], 0)
-            rt[h, b] = tile.astype(F32).T.astype(BF16)
+        for source, start in ((own_reflect, here // stack), (far_reflect, there // stack)):
+            for b in range(blocks // 2):
+                tile = jnp.concatenate([source[h, stack * b + i] for i in range(stack)], 0)
+                rt[h, start + b] = tile.astype(F32).T.astype(BF16)
         return carry
 
     lax.fori_loop(0, offsets, turn, 0)
@@ -196,6 +182,20 @@
         shifted[b, LAG + columns : 2 * LAG + columns] = jnp.zeros((LAG, 128), F32)
 
 
+def join_kernel(*refs):
+    *parts, out = refs
+    for i, part in enumerate(parts):
+        out[i] = part[0]
+
+
+def pick_kernel(core_ref, first, second, out):
+    for i, part in enumerate((first, second)):
+
+        @pl.when(core_ref[0] == i)
+        def _(part=part):
+            out[...] = part[...]
+
+
 def take_field(tests, core, plain):
     for test, at, own, far in tests:
         half = own.shape[1]
@@ -272,6 +272,12 @@
 def flip(x, bits):
     count = lax.axis_size("off")
     return lax.ppermute(x, "off", [(i, i ^ bits) for i in range(count)])
+
+
+def cross(x):
+    count = lax.axis_size("off")
+    pairs = [(2 * i + c, 2 * (i ^ (2 - c)) + c) for i in range(count) for c in range(2)]
+    return lax.ppermute(x, ("off", "dep"), pairs)
 
 
 def core_pair(snapshots, reflect, courant, lags, owners):
@@ -284,14 +290,15 @@
     group = 256
     wing = 4
     lines = count // wing
-    cut = 2 * (lines - 1) // 3
 
     z_parts = [flip(snapshots, wing * j) for j in range(1, lines)]
     o_x, o_y = flip(snapshots, 1), flip(snapshots, 2)
     o_d = flip(o_x, 2)
     sent = lax.dynamic_slice_in_dim(reflect, (1 - core) * mine, mine, 0)
     far_reflect = swapped(sent)
-    far_courant = swapped(courant)
+    own_reflect = lax.dynamic_slice_in_dim(reflect, core * mine, mine, 0)
+    own_courant = courant * SCALE
+    far_courant = swapped(own_courant)
 
     smem = pl.BlockSpec(memory_space=pltpu.SMEM)
     anyspace = pl.BlockSpec(memory_space=pl.ANY)
@@ -306,20 +313,34 @@
     prepare = pl.pallas_call(
         prepare_kernel,
         out_shape=tables,
-        in_specs=[smem] + [anyspace] * 4,
+        in_specs=[smem] + [vmem] * 4,
         out_specs=[vmem] * 4,
-        scratch_shapes=[
-            pltpu.VMEM((mine, depth, rows, columns), BF16),
-            pltpu.SemaphoreType.DMA((4,)),
-        ],
         compiler_params=pltpu.CompilerParams(vmem_limit_bytes=8 << 20),
         cost_estimate=pl.CostEstimate(flops=10**7, bytes_accessed=6 << 20, transcendentals=0),
     )
-    prepared = prepare(where[1:], reflect, far_reflect, courant, far_courant)
-    z_all = jnp.concatenate(z_parts, 0)
+    prepared = prepare(where[1:], own_reflect, far_reflect, own_courant, far_courant)
+    z_shape = jax.ShapeDtypeStruct((lines - 1, half, rows, columns), BF16)
+    small = pl.CostEstimate(flops=0, bytes_accessed=1 << 20, transcendentals=0)
+    join = pl.pallas_call(
+        join_kernel,
+        out_shape=z_shape,
+        in_specs=[vmem] * (lines - 1),
+        out_specs=vmem,
+        compiler_params=pltpu.CompilerParams(vmem_limit_bytes=4 << 20),
+        cost_estimate=small,
+    )
+    pick = pl.pallas_call(
+        pick_kernel,
+        out_shape=z_shape,
+        in_specs=[smem, vmem, vmem],
+        out_specs=vmem,
+        compiler_params=pltpu.CompilerParams(vmem_limit_bytes=4 << 20),
+        cost_estimate=small,
+    )
+    z_all = join(*z_parts)
     z_x, z_y = flip(z_all, 1), flip(z_all, 2)
-    d_x = flip(z_x[:cut], 2)
-    d_y = flip(z_y[cut:], 1)
+    picked = pick(where[1:], z_x, z_y)
+    diagonal = cross(picked)
 
     scratch = [
         pltpu.VMEM((depth, rows, columns), F32),
@@ -349,10 +370,7 @@
     def far_banks(owns, fars):
         def choose(apart):
             low, line = apart % wing, apart // wing
-            return [
-                ((low == 3) & (line > 0) & (line <= cut), line - 1, owns[0], fars[0]),
-                ((low == 3) & (line > cut), line - 1 - cut, owns[1], fars[1]),
-            ]
+            return [((low == 3) & (line > 0), line - 1, owns[0], fars[0])]
 
         return choose
 
@@ -378,7 +396,7 @@
     out_half = jax.ShapeDtypeStruct((half, rows, columns), F32)
     sums = run(sums_kernel, near_banks, [snapshots, o_x, o_y, o_d, z_all], [], [sums_shape])
     sums = run(sums_kernel, side_banks, [z_x, z_y], sums, [sums_shape])
-    kept, given, _ = run(steps_kernel, far_banks, [d_x, d_y], sums, [out_half, out_half, sums_shape], waves)
+    kept, given, _ = run(steps_kernel, far_banks, [diagonal], sums, [out_half, out_half, sums_shape], waves)
 
     total = kept + swapped(given)
     pieces = total.reshape(count, half * rows // count, columns)

time: 106 us -> 95.7 us (0.903)
  local copies, waits for them, and re-layouts: 17.4 us -> 10.1 us
  waiting for transfers between devices: 24.3 us -> 18.3 us
  blocking collectives: 28.7 us -> 30 us
    unnamed x45 -> x27, local copies, waits for them, and re-layouts: 14.6 us -> 8.58 us
    ppermute x10 -> x8, waiting for transfers between devices: 23.1 us -> 17.2 us  [flip(): return lax.ppermute(x, 'off', [(i, i ^ bits) for i in range(count)])]
    all_to_all x1, blocking collectives: 15.9 us -> 17.2 us  [core_pair(): summed = lax.all_to_all(pieces, 'off', 0, 0).sum(0)]
    ppermute x12 -> x11, starting transfers between devices: 2.46 us -> 3.09 us  [swapped(): return lax.ppermute(x, 'dep', [(0, 1), (1, 0)])]
    ppermute x10 -> x8, starting transfers between devices: 14.8 us -> 14.7 us  [flip(): return lax.ppermute(x, 'off', [(i, i ^ bits) for i in range(count)])]
  transfers between devices with their start and end apart: 22 -> 20, of which waited for: 6 -> 6; matrix products, arithmetic and copies ran while one was open for 3% -> 3% of each run, Pallas kernels for 10% -> 12%
where the time goes in v3:
time: 95.7 us; the launch traced here: 95.3 us
  blocking collectives  30 us (31%)
  waiting for transfers between devices  18.3 us (19%)
  starting transfers between devices  17.8 us (19%)
  Pallas kernels  17.7 us (18%)
  local copies, waits for them, and re-layouts  10.1 us (11%)
  other arithmetic  1.11 us (1%)
    all_to_all x1, blocking collectives, core_pair(): summed = lax.all_to_all(pieces, 'off', 0, 0).sum(0)  17.2 us
    ppermute x8, waiting for transfers between devices, flip(): return lax.ppermute(x, 'off', [(i, i ^ bits) for i in range(count)])  17.2 us
    pallas_call x3, Pallas kernels, run(): pl.pallas_call(kernel, in_specs=[smem] * 3 + [vmem] * (2 * n + 4 + len(ex...  16.6 us
    ppermute x8, starting transfers between devices, flip(): return lax.ppermute(x, 'off', [(i, i ^ bits) for i in range(count)])  14.7 us
    all_to_all x1, blocking collectives, core_pair(): return lax.all_to_all(spread, 'off', 0, 0).reshape(half, rows, columns)  12.8 us
    unnamed x27, local copies, waits for them, and re-layouts  8.58 us
    ppermute x11, starting transfers between devices, swapped(): return lax.ppermute(x, 'dep', [(0, 1), (1, 0)])  3.09 us
  transfers between devices with their start and end apart: 20, of which 6 were waited for; matrix products, arithmetic and copies ran while one was open for 3% of the time, Pallas kernels for 12%

profile of v3, /device:TPU:0, one launch (start us, length us, event | category | flops | bytes accessed | tf_op | source)
XLA Modules:
  0.0 95.3 jit_solution(50951392087976984)
XLA Ops:
  0.0 3.1 %collective-permute-start = (bf16[1,4,64,256]{3,2,1,0:T(8,128)(2,1)}, bf16[1,4,64,256]{3,2,1,0:T(8,128)(2,1)S(1)}, u32[]{:S(2)}, u32[]{:S(2)}) collective-permute-start(bf16[1,4,64,256]{3,2,1,0:T(8,128)(2,1)} %refs_0_.1), channel_id=1, source_target_pairs={{0,8},{2,10},{4,12},{6,14},{8,0},{10,2},{12,4},{14,6},{16,24},{18,... | collective-permute-start | bytes 393224 | tf_op jit(solution)/shard_map/ppermute | solution.py:274
  3.1 2.6 %collective-permute-start.1 = (bf16[1,4,64,256]{3,2,1,0:T(8,128)(2,1)}, bf16[1,4,64,256]{3,2,1,0:T(8,128)(2,1)S(1)}, u32[]{:S(2)}, u32[]{:S(2)}) collective-permute-start(bf16[1,4,64,256]{3,2,1,0:T(8,128)(2,1)} %refs_0_.1), channel_id=1, source_target_pairs={{0,16},{2,18},{4,20},{6,22},{8,24},{10,26},{12,28},{14,30},{16,0},... | collective-permute-start | bytes 393224 | tf_op jit(solution)/shard_map/ppermute | solution.py:274
  5.7 1.7 %collective-permute-start.11 = (bf16[1,4,64,256]{3,2,1,0:T(8,128)(2,1)}, bf16[1,4,64,256]{3,2,1,0:T(8,128)(2,1)}, u32[]{:S(2)}, u32[]{:S(2)}) collective-permute-start(bf16[1,4,64,256]{3,2,1,0:T(8,128)(2,1)} %refs_0_.1), channel_id=1, source_target_pairs={{0,2},{2,0},{4,6},{6,4},{8,10},{10,8},{12,14},{14,12},{16,18},{18,... | collective-permute-start | bytes 393224 | tf_op jit(solution)/shard_map/ppermute | solution.py:274
  7.4 1.0 %collective-permute-done.refs_0_ = bf16[1,4,64,256]{3,2,1,0:T(8,128)(2,1)S(1)} collective-permute-done((bf16[1,4,64,256]{3,2,1,0:T(8,128)(2,1)}, bf16[1,4,64,256]{3,2,1,0:T(8,128)(2,1)S(1)}, u32[]{:S(2)}, u32[]{:S(2)}) %collective-permute-start) | collective-permute-done | bytes 131104 | tf_op jit(solution)/shard_map/ppermute | solution.py:274
  8.4 7.8 %collective-permute-done.1.refs_1_ = bf16[1,4,64,256]{3,2,1,0:T(8,128)(2,1)S(1)} collective-permute-done((bf16[1,4,64,256]{3,2,1,0:T(8,128)(2,1)}, bf16[1,4,64,256]{3,2,1,0:T(8,128)(2,1)S(1)}, u32[]{:S(2)}, u32[]{:S(2)}) %collective-permute-start.1) | collective-permute-done | bytes 131104 | tf_op jit(solution)/shard_map/ppermute | solution.py:274
  16.3 1.6 %collective-permute-start.4 = (bf16[3,4,64,256]{3,2,1,0:T(8,128)(2,1)S(1)}, bf16[3,4,64,256]{3,2,1,0:T(8,128)(2,1)S(1)}, u32[]{:S(2)}, u32[]{:S(2)}) collective-permute-start(bf16[3,4,64,256]{3,2,1,0:T(8,128)(2,1)S(1)} %shard_map.55.refs_4_), channel_id=1, source_target_pairs={{0,4},{2,6},{4,0},{6,2},{8,12},{10,14},{12,8},{14,10},{16,20},{18,... | collective-permute-start | bytes 1179656 | tf_op jit(solution)/shard_map/ppermute | solution.py:274
  17.8 1.5 %collective-permute-start.3 = (bf16[3,4,64,256]{3,2,1,0:T(8,128)(2,1)S(1)}, bf16[3,4,64,256]{3,2,1,0:T(8,128)(2,1)S(1)}, u32[]{:S(2)}, u32[]{:S(2)}) collective-permute-start(bf16[3,4,64,256]{3,2,1,0:T(8,128)(2,1)S(1)} %shard_map.55.refs_4_), channel_id=1, source_target_pairs={{0,2},{2,0},{4,6},{6,4},{8,10},{10,8},{12,14},{14,12},{16,18},{18,... | collective-permute-start | bytes 1179656 | tf_op jit(solution)/shard_map/ppermute | solution.py:274
  19.3 1.5 %constant_dynamic-slice_fusion = (bf16[6,4,64,256]{3,2,1,0:T(8,128)(2,1)S(1)}, bf16[6,4,64,256]{3,2,1,0:T(8,128)(2,1)S(1)}) fusion(bf16[12,4,64,256]{3,2,1,0:T(8,128)(2,1)} %param.6, s32[]{:T(128)S(6)} %select_n.7, s32[]{:T(128)S(6)} %select_n.6), kind=kLoop, calls=%fused_computation.2 | loop fusion | bytes 3145736 | tf_op jit(solution)/shard_map/dynamic_slice | solution.py:297
  20.9 1.0 %broadcast_multiply_fusion.own_courant = f32[4,64,256]{2,1,0:T(8,128)S(1)} fusion(f32[4,64,256]{2,1,0:T(8,128)} %param.7), kind=kLoop, calls=%fused_computation | loop fusion | flops 65536 | bytes 524288 | tf_op jit(solution)/shard_map/mul | solution.py:300
  22.5 2.3 %collective-permute-done.4.second.refs_1_ = bf16[3,4,64,256]{3,2,1,0:T(8,128)(2,1)S(1)} collective-permute-done((bf16[3,4,64,256]{3,2,1,0:T(8,128)(2,1)S(1)}, bf16[3,4,64,256]{3,2,1,0:T(8,128)(2,1)S(1)}, u32[]{:S(2)}, u32[]{:S(2)}) %collective-permute-start.4) | collective-permute-done | bytes 393248 | tf_op jit(solution)/shard_map/ppermute | solution.py:274
  24.8 2.2 %collective-permute-start.12 = (bf16[1,4,64,256]{3,2,1,0:T(8,128)(2,1)S(1)}, bf16[1,4,64,256]{3,2,1,0:T(8,128)(2,1)S(1)}, u32[]{:S(2)}, u32[]{:S(2)}) collective-permute-start(bf16[1,4,64,256]{3,2,1,0:T(8,128)(2,1)S(1)} %copy-done.2), channel_id=1, source_target_pairs={{0,4},{2,6},{4,0},{6,2},{8,12},{10,14},{12,8},{14,10},{16,20},{18,... | collective-permute-start | bytes 393224 | tf_op jit(solution)/shard_map/ppermute | solution.py:274
  27.2 2.7 %collective-permute-done.12.refs_2_ = bf16[1,4,64,256]{3,2,1,0:T(8,128)(2,1)S(1)} collective-permute-done((bf16[1,4,64,256]{3,2,1,0:T(8,128)(2,1)S(1)}, bf16[1,4,64,256]{3,2,1,0:T(8,128)(2,1)S(1)}, u32[]{:S(2)}, u32[]{:S(2)}) %collective-permute-start.12) | collective-permute-done | bytes 131104 | tf_op jit(solution)/shard_map/ppermute | solution.py:274
  29.9 2.0 %collective-permute-start.13 = (bf16[1,4,64,256]{3,2,1,0:T(8,128)(2,1)}, bf16[1,4,64,256]{3,2,1,0:T(8,128)(2,1)}, u32[]{:S(2)}, u32[]{:S(2)}) collective-permute-start(bf16[1,4,64,256]{3,2,1,0:T(8,128)(2,1)} %collective-permute-done.11.refs_1_), channel_id=1, source_target_pairs={{0,4},{2,6},{4,0},{6,2},{8,12},{10,14},{12,8},{14,10},{16,20},{18,... | collective-permute-start | bytes 393224 | tf_op jit(solution)/shard_map/ppermute | solution.py:274
  31.9 0.6 copy-done.5
  32.6 0.7 copy-done
  33.8 0.7 copy-done.3
  34.4 3.3 %collective-permute-done.13.refs_3_ = bf16[1,4,64,256]{3,2,1,0:T(8,128)(2,1)} collective-permute-done((bf16[1,4,64,256]{3,2,1,0:T(8,128)(2,1)}, bf16[1,4,64,256]{3,2,1,0:T(8,128)(2,1)}, u32[]{:S(2)}, u32[]{:S(2)}) %collective-permute-start.13) | collective-permute-done | bytes 131104 | tf_op jit(solution)/shard_map/ppermute | solution.py:274
  38.9 0.7 copy-done.9
  40.2 0.9 copy-done.1
  41.2 1.0 %shard_map.57 = (bf16[6,4,256,128]{3,2,1,0:T(8,128)(2,1)S(1)}, f32[8,64,256]{2,1,0:T(8,128)S(1)}, bf16[512,256]{1,0:T(8,128)(2,1)S(1)}, bf16[256,512]{1,0:T(8,128)(2,1)S(1)}) custom-call(s32[1]{0:T(128)} %bitcast.1.core_ref, bf16[6,4,64,256]{3,2,1,0:T(8,128)(2,1)S(1)} %get-tuple-element.18.own_reflect, ...), custom_call_target="tpu_custom_call" | custom-call | flops 10000000 | bytes 6291456 | tf_op jit(solution)/shard_map/pallas_call | solution.py:321
  42.2 0.9 copy-done.4
  43.1 0.9 copy-done.6
  44.0 0.9 copy-done.8
  45.0 0.9 copy-done.10
  45.9 7.7 %shard_map.58.refs_8_ = f32[8,8,64,256]{3,2,1,0:T(8,128)S(1)} custom-call(s32[2]{0:T(128)S(1)} %pad_add_fusion.where_ref, s32[8]{0:T(128)S(1)} %copy-done.11, s32[12]{0:T(128)S(1)} %copy-done.12, bf16[1,4,64,256]{3,2,1,0:T(8,128)(2,1)S(1)} %copy-done.2, bf16[1,4,64,256]{3,2,1,0:T(8,128)(2,1)} %collective-permute-done.11.refs_1_, ...), custom_call_target="tpu_custom_call" | custom-call | flops 1000000000 | bytes 10485760 | tf_op jit(solution)/shard_map/pallas_call | solution.py:385
  53.6 2.4 %shard_map.59.refs_6_ = f32[8,8,64,256]{3,2,1,0:T(8,128)S(1)} custom-call(s32[2]{0:T(128)S(1)} %pad_add_fusion.where_ref, s32[8]{0:T(128)S(1)} %copy-done.11, s32[12]{0:T(128)S(1)} %copy-done.12, bf16[3,4,64,256]{3,2,1,0:T(8,128)(2,1)S(1)} %collective-permute-done.3.first.refs_0_, ...), custom_call_target="tpu_custom_call", output_to_operand_aliasing={{}: (11, {})} | custom-call | flops 1000000000 | bytes 10485760 | tf_op jit(solution)/shard_map/pallas_call | solution.py:385
  56.0 6.6 %shard_map.60 = (f32[4,64,256]{2,1,0:T(8,128)S(1)}, f32[4,64,256]{2,1,0:T(8,128)S(1)}, f32[8,8,64,256]{3,2,1,0:T(8,128)S(1)}) custom-call(s32[2]{0:T(128)S(1)} %pad_add_fusion.where_ref, s32[8]{0:T(128)S(1)} %copy-done.11, s32[12]{0:T(128)S(1)} %copy-done.12, ...), custom_call_target="tpu_custom_call", output_to_operand_aliasing={{2}: (9, {})} | custom-call | flops 1000000000 | bytes 10485760 | tf_op jit(solution)/shard_map/pallas_call | solution.py:385
  62.5 0.8 collective-permute-start.19
  63.3 1.2 %collective-permute-done.19 = f32[4,64,256]{2,1,0:T(8,128)S(1)} collective-permute-done((f32[4,64,256]{2,1,0:T(8,128)S(1)}, f32[4,64,256]{2,1,0:T(8,128)S(1)}, u32[]{:S(2)}, u32[]{:S(2)}) %collective-permute-start.19) | collective-permute-done | bytes 262176 | tf_op jit(solution)/shard_map/ppermute | solution.py:269
  64.5 17.2 %all_to_all.10 = f32[16,16,256]{2,1,0:T(8,128)S(1)} all-to-all(f32[16,16,256]{2,1,0:T(8,128)S(1)} %bitcast.4), channel_id=1, replica_groups=mesh['off'=16,'dep'=2] {'off'}, dimensions={0} | all-to-all | bytes 524288 | tf_op jit(solution)/shard_map/all_to_all | solution.py:403
  81.8 12.8 %all_to_all.11 = f32[16,16,256]{2,1,0:T(8,128)S(1)} all-to-all(f32[16,16,256]{2,1,0:T(8,128)S(1)} %broadcast_in_dim.2), channel_id=1, replica_groups=mesh['off'=16,'dep'=2] {'off'}, dimensions={0} | all-to-all | bytes 524288 | tf_op jit(solution)/shard_map/all_to_all | solution.py:405
  94.6 0.7 copy.11
  (49 shorter events, 3.3 us)
Async XLA Ops:
  0.0 24.8 %copy-start.2 = (bf16[1,4,64,256]{3,2,1,0:T(8,128)(2,1)S(1)}, bf16[1,4,64,256]{3,2,1,0:T(8,128)(2,1)}, u32[]{:S(2)}) copy-start(bf16[1,4,64,256]{3,2,1,0:T(8,128)(2,1)} %refs_0_.1) | copy-start | bytes 393220
  0.0 42.2 %copy-start.12 = (s32[12]{0:T(128)S(1)}, s32[12]{0:T(128)}, u32[]{:S(2)}) copy-start(s32[12]{0:T(128)} %lags_ref.5) | copy-start | bytes 148
  0.0 42.2 %copy-start.11 = (s32[8]{0:T(128)S(1)}, s32[8]{0:T(128)}, u32[]{:S(2)}) copy-start(s32[8]{0:T(128)} %owners_ref.5) | copy-start | bytes 100
  0.0 8.4 %collective-permute-start = (bf16[1,4,64,256]{3,2,1,0:T(8,128)(2,1)}, bf16[1,4,64,256]{3,2,1,0:T(8,128)(2,1)S(1)}, u32[]{:S(2)}, u32[]{:S(2)}) collective-permute-start(bf16[1,4,64,256]{3,2,1,0:T(8,128)(2,1)} %refs_0_.1), channel_id=1, source_target_pairs={{0,8},{2,10},{4,12},{6,14},{8,0},{10,2},{12,4},{14,6},{16,24},{18,... | collective-permute-start | bytes 393224 | tf_op jit(solution)/shard_map/ppermute | solution.py:274
  3.1 13.1 %collective-permute-start.1 = (bf16[1,4,64,256]{3,2,1,0:T(8,128)(2,1)}, bf16[1,4,64,256]{3,2,1,0:T(8,128)(2,1)S(1)}, u32[]{:S(2)}, u32[]{:S(2)}) collective-permute-start(bf16[1,4,64,256]{3,2,1,0:T(8,128)(2,1)} %refs_0_.1), channel_id=1, source_target_pairs={{0,16},{2,18},{4,20},{6,22},{8,24},{10,26},{12,28},{14,30},{16,0},... | collective-permute-start | bytes 393224 | tf_op jit(solution)/shard_map/ppermute | solution.py:274
  5.7 10.5 %collective-permute-start.2 = (bf16[1,4,64,256]{3,2,1,0:T(8,128)(2,1)}, bf16[1,4,64,256]{3,2,1,0:T(8,128)(2,1)S(1)}, u32[]{:S(2)}, u32[]{:S(2)}) collective-permute-start(bf16[1,4,64,256]{3,2,1,0:T(8,128)(2,1)} %refs_0_.1), channel_id=1, source_target_pairs={{0,24},{2,26},{4,28},{6,30},{8,16},{10,18},{12,20},{14,22},{16,8},... | collective-permute-start | bytes 393224 | tf_op jit(solution)/shard_map/ppermute | solution.py:274
  5.7 21.3 %collective-permute-start.11 = (bf16[1,4,64,256]{3,2,1,0:T(8,128)(2,1)}, bf16[1,4,64,256]{3,2,1,0:T(8,128)(2,1)}, u32[]{:S(2)}, u32[]{:S(2)}) collective-permute-start(bf16[1,4,64,256]{3,2,1,0:T(8,128)(2,1)} %refs_0_.1), channel_id=1, source_target_pairs={{0,2},{2,0},{4,6},{6,4},{8,10},{10,8},{12,14},{14,12},{16,18},{18,... | collective-permute-start | bytes 393224 | tf_op jit(solution)/shard_map/ppermute | solution.py:274
  16.3 8.5 %collective-permute-start.4 = (bf16[3,4,64,256]{3,2,1,0:T(8,128)(2,1)S(1)}, bf16[3,4,64,256]{3,2,1,0:T(8,128)(2,1)S(1)}, u32[]{:S(2)}, u32[]{:S(2)}) collective-permute-start(bf16[3,4,64,256]{3,2,1,0:T(8,128)(2,1)S(1)} %shard_map.55.refs_4_), channel_id=1, source_target_pairs={{0,4},{2,6},{4,0},{6,2},{8,12},{10,14},{12,8},{14,10},{16,20},{18,... | collective-permute-start | bytes 1179656 | tf_op jit(solution)/shard_map/ppermute | solution.py:274
  17.8 9.1 %collective-permute-start.3 = (bf16[3,4,64,256]{3,2,1,0:T(8,128)(2,1)S(1)}, bf16[3,4,64,256]{3,2,1,0:T(8,128)(2,1)S(1)}, u32[]{:S(2)}, u32[]{:S(2)}) collective-permute-start(bf16[3,4,64,256]{3,2,1,0:T(8,128)(2,1)S(1)} %shard_map.55.refs_4_), channel_id=1, source_target_pairs={{0,2},{2,0},{4,6},{6,4},{8,10},{10,8},{12,14},{14,12},{16,18},{18,... | collective-permute-start | bytes 1179656 | tf_op jit(solution)/shard_map/ppermute | solution.py:274
  20.8 19.2 %collective-permute-start.7 = (bf16[6,4,64,256]{3,2,1,0:T(8,128)(2,1)S(1)}, bf16[6,4,64,256]{3,2,1,0:T(8,128)(2,1)S(1)}, u32[]{:S(2)}, u32[]{:S(2)}) collective-permute-start(bf16[6,4,64,256]{3,2,1,0:T(8,128)(2,1)S(1)} %get-tuple-element.17), channel_id=1, source_target_pairs={{0,1},{1,0},{2,3},{3,2},{4,5},{5,4},{6,7},{7,6},{8,9},{9,8},{10,11... | collective-permute-start | bytes 2359304 | tf_op jit(solution)/shard_map/ppermute | solution.py:269
  21.9 10.7 %collective-permute-start.8 = (f32[4,64,256]{2,1,0:T(8,128)S(1)}, f32[4,64,256]{2,1,0:T(8,128)S(1)}, u32[]{:S(2)}, u32[]{:S(2)}) collective-permute-start(f32[4,64,256]{2,1,0:T(8,128)S(1)} %broadcast_multiply_fusion.own_courant), channel_id=1, source_target_pairs={{0,1},{1,0},{2,3},{3,2},{4,5},{5,4},{6,7},{7,6},{8,9},{9,8},{10,11... | collective-permute-start | bytes 786440 | tf_op jit(solution)/shard_map/ppermute | solution.py:269
  24.8 5.1 %collective-permute-start.12 = (bf16[1,4,64,256]{3,2,1,0:T(8,128)(2,1)S(1)}, bf16[1,4,64,256]{3,2,1,0:T(8,128)(2,1)S(1)}, u32[]{:S(2)}, u32[]{:S(2)}) collective-permute-start(bf16[1,4,64,256]{3,2,1,0:T(8,128)(2,1)S(1)} %copy-done.2), channel_id=1, source_target_pairs={{0,4},{2,6},{4,0},{6,2},{8,12},{10,14},{12,8},{14,10},{16,20},{18,... | collective-permute-start | bytes 393224 | tf_op jit(solution)/shard_map/ppermute | solution.py:274
  27.0 12.6 %collective-permute-start.5 = (bf16[3,4,64,256]{3,2,1,0:T(8,128)(2,1)S(1)}, bf16[3,4,64,256]{3,2,1,0:T(8,128)(2,1)S(1)}, u32[]{:S(2)}, u32[]{:S(2)}) collective-permute-start(bf16[3,4,64,256]{3,2,1,0:T(8,128)(2,1)S(1)} %shard_map.56), channel_id=1, source_target_pairs={{0,4},{1,3},{2,6},{3,1},{4,0},{5,7},{6,2},{7,5},{8,12},{9,11},{10,... | collective-permute-start | bytes 1179656 | tf_op jit(solution)/shard_map/ppermute | solution.py:280
  27.1 4.8 %collective-permute-start.14 = (bf16[1,4,64,256]{3,2,1,0:T(8,128)(2,1)S(1)}, bf16[1,4,64,256]{3,2,1,0:T(8,128)(2,1)S(1)}, u32[]{:S(2)}, u32[]{:S(2)}) collective-permute-start(bf16[1,4,64,256]{3,2,1,0:T(8,128)(2,1)S(1)} %copy-done.2), channel_id=1, source_target_pairs={{0,1},{1,0},{2,3},{3,2},{4,5},{5,4},{6,7},{7,6},{8,9},{9,8},{10,11... | collective-permute-start | bytes 393224 | tf_op jit(solution)/shard_map/ppermute | solution.py:269
  29.9 7.9 %collective-permute-start.13 = (bf16[1,4,64,256]{3,2,1,0:T(8,128)(2,1)}, bf16[1,4,64,256]{3,2,1,0:T(8,128)(2,1)}, u32[]{:S(2)}, u32[]{:S(2)}) collective-permute-start(bf16[1,4,64,256]{3,2,1,0:T(8,128)(2,1)} %collective-permute-done.11.refs_1_), channel_id=1, source_target_pairs={{0,4},{2,6},{4,0},{6,2},{8,12},{10,14},{12,8},{14,10},{16,20},{18,... | collective-permute-start | bytes 393224 | tf_op jit(solution)/shard_map/ppermute | solution.py:274
  31.9 0.7 copy-start.5
  32.6 5.2 %collective-permute-start.15 = (bf16[1,4,64,256]{3,2,1,0:T(8,128)(2,1)}, bf16[1,4,64,256]{3,2,1,0:T(8,128)(2,1)S(1)}, u32[]{:S(2)}, u32[]{:S(2)}) collective-permute-start(bf16[1,4,64,256]{3,2,1,0:T(8,128)(2,1)} %collective-permute-done.11.refs_1_), channel_id=1, source_target_pairs={{0,1},{1,0},{2,3},{3,2},{4,5},{5,4},{6,7},{7,6},{8,9},{9,8},{10,11... | collective-permute-start | bytes 393224 | tf_op jit(solution)/shard_map/ppermute | solution.py:269
  32.6 0.7 copy-start
  33.3 5.6 %collective-permute-start.16 = (bf16[1,4,64,256]{3,2,1,0:T(8,128)(2,1)S(1)}, bf16[1,4,64,256]{3,2,1,0:T(8,128)(2,1)S(1)}, u32[]{:S(2)}, u32[]{:S(2)}) collective-permute-start(bf16[1,4,64,256]{3,2,1,0:T(8,128)(2,1)S(1)} %collective-permute-done.12.refs_2_), channel_id=1, source_target_pairs={{0,1},{1,0},{2,3},{3,2},{4,5},{5,4},{6,7},{7,6},{8,9},{9,8},{10,11... | collective-permute-start | bytes 393224 | tf_op jit(solution)/shard_map/ppermute | solution.py:269
  33.8 0.7 copy-start.3
  37.7 4.5 %collective-permute-start.18 = (bf16[3,4,64,256]{3,2,1,0:T(8,128)(2,1)S(1)}, bf16[3,4,64,256]{3,2,1,0:T(8,128)(2,1)}, u32[]{:S(2)}, u32[]{:S(2)}) collective-permute-start(bf16[3,4,64,256]{3,2,1,0:T(8,128)(2,1)S(1)} %shard_map.55.refs_4_), channel_id=1, source_target_pairs={{0,1},{1,0},{2,3},{3,2},{4,5},{5,4},{6,7},{7,6},{8,9},{9,8},{10,11... | collective-permute-start | bytes 1179656 | tf_op jit(solution)/shard_map/ppermute | solution.py:269
  38.4 15.2 %collective-permute-start.10 = (bf16[3,4,64,256]{3,2,1,0:T(8,128)(2,1)S(1)}, bf16[3,4,64,256]{3,2,1,0:T(8,128)(2,1)}, u32[]{:S(2)}, u32[]{:S(2)}) collective-permute-start(bf16[3,4,64,256]{3,2,1,0:T(8,128)(2,1)S(1)} %collective-permute-done.4.second.refs_1_), channel_id=1, source_target_pairs={{0,1},{1,0},{2,3},{3,2},{4,5},{5,4},{6,7},{7,6},{8,9},{9,8},{10,11... | collective-permute-start | bytes 1179656 | tf_op jit(solution)/shard_map/ppermute | solution.py:269
  38.9 0.7 copy-start.9
  39.6 14.0 %collective-permute-start.9 = (bf16[3,4,64,256]{3,2,1,0:T(8,128)(2,1)S(1)}, bf16[3,4,64,256]{3,2,1,0:T(8,128)(2,1)}, u32[]{:S(2)}, u32[]{:S(2)}) collective-permute-start(bf16[3,4,64,256]{3,2,1,0:T(8,128)(2,1)S(1)} %collective-permute-done.3.first.refs_0_), channel_id=1, source_target_pairs={{0,1},{1,0},{2,3},{3,2},{4,5},{5,4},{6,7},{7,6},{8,9},{9,8},{10,11... | collective-permute-start | bytes 1179656 | tf_op jit(solution)/shard_map/ppermute | solution.py:269
  39.6 16.4 %collective-permute-start.6 = (bf16[3,4,64,256]{3,2,1,0:T(8,128)(2,1)S(1)}, bf16[3,4,64,256]{3,2,1,0:T(8,128)(2,1)}, u32[]{:S(2)}, u32[]{:S(2)}) collective-permute-start(bf16[3,4,64,256]{3,2,1,0:T(8,128)(2,1)S(1)} %collective-permute-done.5.refs_0_), channel_id=1, source_target_pairs={{0,1},{1,0},{2,3},{3,2},{4,5},{5,4},{6,7},{7,6},{8,9},{9,8},{10,11... | collective-permute-start | bytes 1179656 | tf_op jit(solution)/shard_map/ppermute | solution.py:269
  40.1 2.1 %collective-permute-start.17 = (bf16[1,4,64,256]{3,2,1,0:T(8,128)(2,1)}, bf16[1,4,64,256]{3,2,1,0:T(8,128)(2,1)}, u32[]{:S(2)}, u32[]{:S(2)}) collective-permute-start(bf16[1,4,64,256]{3,2,1,0:T(8,128)(2,1)} %collective-permute-done.13.refs_3_), channel_id=1, source_target_pairs={{0,1},{1,0},{2,3},{3,2},{4,5},{5,4},{6,7},{7,6},{8,9},{9,8},{10,11... | collective-permute-start | bytes 393224 | tf_op jit(solution)/shard_map/ppermute | solution.py:269
  40.2 0.9 copy-start.1
  42.2 0.9 copy-start.4
  43.1 0.9 copy-start.6
  44.0 0.9 copy-start.8
  44.9 0.9 copy-start.10
  62.5 1.9 %collective-permute-start.19 = (f32[4,64,256]{2,1,0:T(8,128)S(1)}, f32[4,64,256]{2,1,0:T(8,128)S(1)}, u32[]{:S(2)}, u32[]{:S(2)}) collective-permute-start(f32[4,64,256]{2,1,0:T(8,128)S(1)} %get-tuple-element.16), channel_id=1, source_target_pairs={{0,1},{1,0},{2,3},{3,2},{4,5},{5,4},{6,7},{7,6},{8,9},{9,8},{10,11... | collective-permute-start | bytes 786440 | tf_op jit(solution)/shard_map/ppermute | solution.py:269
  (1 other events, 0.6 us)

commit v4 on v3

--- a/solution.py
+++ b/solution.py
@@ -104,8 +104,8 @@
     return full.astype(BF16)
 
 
-def prepare_kernel(core_ref, own_reflect, far_reflect, own_courant, far_courant, rt, cour, across, down):
-    core = core_ref[0]
+def prepare_kernel(own_reflect, far_reflect, own_courant, far_courant, rt, cour, across, down):
+    core = lax.axis_index("dep")
     half, rows, columns = own_courant.shape
     offsets, blocks = rt.shape[:2]
     stack = 128 // rows
@@ -188,14 +188,6 @@
         out[i] = part[0]
 
 
-def pick_kernel(core_ref, first, second, out):
-    for i, part in enumerate((first, second)):
-
-        @pl.when(core_ref[0] == i)
-        def _(part=part):
-            out[...] = part[...]
-
-
 def take_field(tests, core, plain):
     for test, at, own, far in tests:
         half = own.shape[1]
@@ -207,31 +199,37 @@
                 plain[(1 - core) * half + z] = far[at, z].astype(F32)
 
 
-def sums_kernel(
-    choose, where_ref, owners_ref, lags_ref, rt, cour, across, down, sums, plain, shifted, turned,
-):
-    first = where_ref[1] * rt.shape[0]
+def sums_kernel(groups, where_now, owners_ref, lags_ref, rt, cour, across, down, sums, plain, shifted, turned):
+    first = where_now[1] * rt.shape[0]
     clear_rims(shifted, cour.shape[2])
 
-    def step(t, carry):
-        tests = choose(owners_ref[t] ^ where_ref[0])
-
-        @pl.when(functools.reduce(jnp.logical_or, [test for test, *_ in tests]))
+    def any_of(tests):
+        return functools.reduce(jnp.logical_or, [test for test, *_ in tests])
+
+    def step(t, counts):
+        taken, after = [], []
+        for (choose, low, high), count in zip(groups, counts, strict=True):
+            tests = choose(owners_ref[t] ^ where_now[0])
+            due = (count >= low) & (count < high)
+            taken += [(test & due, *bank) for test, *bank in tests]
+            after.append(count + any_of(tests).astype(jnp.int32))
+
+        @pl.when(any_of(taken))
         def _():
-            take_field(tests, where_ref[1], plain)
+            take_field(taken, where_now[1], plain)
             source_of(lambda h: lags_ref[first + h], rt, cour, across, down, plain, shifted, turned, sums.at[t])
 
-        return carry
-
-    lax.fori_loop(0, ITERS, step, 0)
+        return tuple(after)
+
+    lax.fori_loop(0, ITERS, step, tuple(jnp.int32(0) for _ in groups))
 
 
 def steps_kernel(
-    choose, where_ref, owners_ref, lags_ref, rt, cour, across, down, kept_ref, given_ref, sums,
+    groups, where_now, owners_ref, lags_ref, rt, cour, across, down, kept_ref, given_ref, sums,
     plain, shifted, turned, wave_a, wave_b,
 ):
     sums_kernel(
-        choose, where_ref, owners_ref, lags_ref, rt, cour, across, down, sums, plain, shifted, turned
+        groups, where_now, owners_ref, lags_ref, rt, cour, across, down, sums, plain, shifted, turned
     )
     depth, rows, _ = cour.shape
     half = depth // 2
@@ -260,7 +258,7 @@
     if ITERS % 2 == 0:
         grow(ITERS - 1, wave_a, wave_b)
         last = wave_b
-    core = where_ref[1]
+    core = where_now[1]
     kept_ref[...] = last[pl.ds(core * half, half)]
     given_ref[...] = last[pl.ds((1 - core) * half, half)]
 
@@ -272,12 +270,6 @@
 def flip(x, bits):
     count = lax.axis_size("off")
     return lax.ppermute(x, "off", [(i, i ^ bits) for i in range(count)])
-
-
-def cross(x):
-    count = lax.axis_size("off")
-    pairs = [(2 * i + c, 2 * (i ^ (2 - c)) + c) for i in range(count) for c in range(2)]
-    return lax.ppermute(x, ("off", "dep"), pairs)
 
 
 def core_pair(snapshots, reflect, courant, lags, owners):
@@ -303,7 +295,6 @@
     smem = pl.BlockSpec(memory_space=pltpu.SMEM)
     anyspace = pl.BlockSpec(memory_space=pl.ANY)
     vmem = pl.BlockSpec(memory_space=pltpu.VMEM)
-    where = jnp.stack([lax.axis_index("off"), core]).astype(jnp.int32)
     tables = [
         jax.ShapeDtypeStruct((mine, blocks, columns, 128), BF16),
         jax.ShapeDtypeStruct((depth, rows, columns), F32),
@@ -313,12 +304,12 @@
     prepare = pl.pallas_call(
         prepare_kernel,
         out_shape=tables,
-        in_specs=[smem] + [vmem] * 4,
+        in_specs=[vmem] * 4,
         out_specs=[vmem] * 4,
-        compiler_params=pltpu.CompilerParams(vmem_limit_bytes=8 << 20),
+        compiler_params=pltpu.CompilerParams(vmem_limit_bytes=6 << 20),
         cost_estimate=pl.CostEstimate(flops=10**7, bytes_accessed=6 << 20, transcendentals=0),
     )
-    prepared = prepare(where[1:], own_reflect, far_reflect, own_courant, far_courant)
+    prepared = prepare(own_reflect, far_reflect, own_courant, far_courant)
     z_shape = jax.ShapeDtypeStruct((lines - 1, half, rows, columns), BF16)
     small = pl.CostEstimate(flops=0, bytes_accessed=1 << 20, transcendentals=0)
     join = pl.pallas_call(
@@ -326,21 +317,13 @@
         out_shape=z_shape,
         in_specs=[vmem] * (lines - 1),
         out_specs=vmem,
-        compiler_params=pltpu.CompilerParams(vmem_limit_bytes=4 << 20),
-        cost_estimate=small,
-    )
-    pick = pl.pallas_call(
-        pick_kernel,
-        out_shape=z_shape,
-        in_specs=[smem, vmem, vmem],
-        out_specs=vmem,
-        compiler_params=pltpu.CompilerParams(vmem_limit_bytes=4 << 20),
+        compiler_params=pltpu.CompilerParams(vmem_limit_bytes=2 << 20),
         cost_estimate=small,
     )
     z_all = join(*z_parts)
     z_x, z_y = flip(z_all, 1), flip(z_all, 2)
-    picked = pick(where[1:], z_x, z_y)
-    diagonal = cross(picked)
+    d_parts = [flip(o_d, wing * j) for j in range(1, lines)]
+    d_all = join(*d_parts)
 
     scratch = [
         pltpu.VMEM((depth, rows, columns), F32),
@@ -348,7 +331,7 @@
         pltpu.VMEM((blocks, columns, 128), F32),
     ]
     waves = [pltpu.VMEM((depth, rows, columns), F32)] * 2
-    params = pltpu.CompilerParams(vmem_limit_bytes=12 << 20)
+    params = pltpu.CompilerParams(vmem_limit_bytes=6 << 20)
     cost = pl.CostEstimate(flops=10**9, bytes_accessed=10 << 20, transcendentals=0)
     sums_shape = jax.ShapeDtypeStruct((ITERS, depth, rows, columns), F32)
 
@@ -374,29 +357,42 @@
 
         return choose
 
-    def run(body, banks, own_parts, extra, out_shape, more_scratch=()):
-        far_parts = [swapped(v) for v in own_parts]
-        n = len(own_parts)
-
-        def kernel(where_ref, owners_ref, lags_ref, *refs):
-            rest = refs[2 * n : 2 * n + 4] + refs[2 * n + 4 + len(extra) :]
-            body(banks(refs[:n], refs[n : 2 * n]), where_ref, owners_ref, lags_ref, *rest)
+    def both_halves(own_parts):
+        return own_parts, [swapped(v) for v in own_parts]
+
+    def run(body, groups, extra, out_shape, more_scratch=()):
+        arrays = [v for (owns, fars), *_ in groups for v in [*owns, *fars]]
+        n = len(arrays)
+
+        def kernel(owners_ref, lags_ref, *refs):
+            where_now = lax.axis_index("off"), lax.axis_index("dep")
+            given, chosen = list(refs[:n]), []
+            for (owns, fars), banks, low, high in groups:
+                own_refs = [given.pop(0) for _ in owns]
+                far_refs = [given.pop(0) for _ in fars]
+                chosen.append((banks(own_refs, far_refs), low, high))
+            rest = refs[n : n + 4] + refs[n + 4 + len(extra) :]
+            body(chosen, where_now, owners_ref, lags_ref, *rest)
 
         return pl.pallas_call(
             kernel,
-            in_specs=[smem] * 3 + [vmem] * (2 * n + 4 + len(extra)),
+            in_specs=[smem] * 2 + [vmem] * (n + 4 + len(extra)),
             out_shape=out_shape,
             out_specs=[vmem] * len(out_shape),
             scratch_shapes=scratch + list(more_scratch),
-            input_output_aliases={3 + 2 * n + 4: len(out_shape) - 1} if extra else {},
+            input_output_aliases={2 + n + 4: len(out_shape) - 1} if extra else {},
             compiler_params=params,
             cost_estimate=cost,
-        )(where, owners, lags, *own_parts, *far_parts, *prepared, *extra)
+        )(owners, lags, *arrays, *prepared, *extra)
 
     out_half = jax.ShapeDtypeStruct((half, rows, columns), F32)
-    sums = run(sums_kernel, near_banks, [snapshots, o_x, o_y, o_d, z_all], [], [sums_shape])
-    sums = run(sums_kernel, side_banks, [z_x, z_y], sums, [sums_shape])
-    kept, given, _ = run(steps_kernel, far_banks, [diagonal], sums, [out_half, out_half, sums_shape], waves)
+    near = both_halves([snapshots, o_x, o_y, o_d, z_all])
+    side = both_halves([z_x, z_y])
+    far = both_halves([d_all])
+    sums = run(sums_kernel, [(near, near_banks, 0, ITERS)], [], [sums_shape])
+    sums = run(sums_kernel, [(side, side_banks, 0, ITERS)], sums, [sums_shape])
+    groups = [(far, far_banks, 0, ITERS)]
+    kept, given, _ = run(steps_kernel, groups, sums, [out_half, out_half, sums_shape], waves)
 
     total = kept + swapped(given)
     pieces = total.reshape(count, half * rows // count, columns)

time: 95.7 us -> 87.1 us (0.910)
  local copies, waits for them, and re-layouts: 10.1 us -> 2.24 us
  waiting for transfers between devices: 18.3 us -> 23.3 us
  blocking collectives: 30 us -> 27.1 us
  Pallas kernels: 17.7 us -> 15.7 us
    unnamed x27 -> x7, local copies, waits for them, and re-layouts: 8.58 us -> 0.71 us
    ppermute x8 -> x11, waiting for transfers between devices: 17.2 us -> 21 us  [flip(): return lax.ppermute(x, 'off', [(i, i ^ bits) for i in range(count)])]
    all_to_all x1, blocking collectives: 17.2 us -> 14.3 us  [core_pair(): summed = lax.all_to_all(pieces, 'off', 0, 0).sum(0)]
    pallas_call x5, Pallas kernels: 17.7 us -> 15.7 us  [the longest x3 14.6 us: run(): pl.pallas_call(kernel, in_specs=[smem] * 2 + [vmem] * (n + 4 + len(extra)...]
    ppermute x11, waiting for transfers between devices: 1.19 us -> 2.29 us  [swapped(): return lax.ppermute(x, 'dep', [(0, 1), (1, 0)])]
    ppermute x8 -> x11, starting transfers between devices: 14.7 us -> 14.9 us  [flip(): return lax.ppermute(x, 'off', [(i, i ^ bits) for i in range(count)])]
  transfers between devices with their start and end apart: 20 -> 22, of which waited for: 6 -> 10; matrix products, arithmetic and copies ran while one was open for 3% -> 3% of each run, Pallas kernels for 12% -> 11%
where the time goes in v4:
time: 87.1 us; the launch traced here: 86.8 us
  blocking collectives  27.1 us (31%)
  waiting for transfers between devices  23.3 us (27%)
  starting transfers between devices  17.3 us (20%)
  Pallas kernels  15.7 us (18%)
  local copies, waits for them, and re-layouts  2.24 us (3%)
  other arithmetic  1.03 us (1%)
    ppermute x11, waiting for transfers between devices, flip(): return lax.ppermute(x, 'off', [(i, i ^ bits) for i in range(count)])  21 us
    ppermute x11, starting transfers between devices, flip(): return lax.ppermute(x, 'off', [(i, i ^ bits) for i in range(count)])  14.9 us
    pallas_call x3, Pallas kernels, run(): pl.pallas_call(kernel, in_specs=[smem] * 2 + [vmem] * (n + 4 + len(extra)...  14.6 us
    all_to_all x1, blocking collectives, core_pair(): summed = lax.all_to_all(pieces, 'off', 0, 0).sum(0)  14.3 us
    all_to_all x1, blocking collectives, core_pair(): return lax.all_to_all(spread, 'off', 0, 0).reshape(half, rows, columns)  12.8 us
    ppermute x11, starting transfers between devices, swapped(): return lax.ppermute(x, 'dep', [(0, 1), (1, 0)])  2.44 us
    ppermute x11, waiting for transfers between devices, swapped(): return lax.ppermute(x, 'dep', [(0, 1), (1, 0)])  2.29 us
  transfers between devices with their start and end apart: 22, of which 10 were waited for; matrix products, arithmetic and copies ran while one was open for 3% of the time, Pallas kernels for 11%

profile of v4, /device:TPU:0, one launch (start us, length us, event | category | flops | bytes accessed | tf_op | source)
XLA Modules:
  0.0 86.8 jit_solution(2155766385480390571)
XLA Ops:
  0.0 3.0 %collective-permute-start = (bf16[1,4,64,256]{3,2,1,0:T(8,128)(2,1)}, bf16[1,4,64,256]{3,2,1,0:T(8,128)(2,1)S(1)}, u32[]{:S(2)}, u32[]{:S(2)}) collective-permute-start(bf16[1,4,64,256]{3,2,1,0:T(8,128)(2,1)} %refs_0_.1), channel_id=1, source_target_pairs={{0,2},{2,0},{4,6},{6,4},{8,10},{10,8},{12,14},{14,12},{16,18},{18,... | collective-permute-start | bytes 393224 | tf_op jit(solution)/shard_map/ppermute | solution.py:272
  3.0 3.6 %collective-permute-start.10 = (bf16[1,4,64,256]{3,2,1,0:T(8,128)(2,1)}, bf16[1,4,64,256]{3,2,1,0:T(8,128)(2,1)S(1)}, u32[]{:S(2)}, u32[]{:S(2)}) collective-permute-start(bf16[1,4,64,256]{3,2,1,0:T(8,128)(2,1)} %refs_0_.1), channel_id=1, source_target_pairs={{0,24},{2,26},{4,28},{6,30},{8,16},{10,18},{12,20},{14,22},{16,8},... | collective-permute-start | bytes 393224 | tf_op jit(solution)/shard_map/ppermute | solution.py:272
  6.6 1.0 %broadcast_multiply_fusion.own_courant = f32[4,64,256]{2,1,0:T(8,128)S(1)} fusion(f32[4,64,256]{2,1,0:T(8,128)} %param.7), kind=kLoop, calls=%fused_computation | loop fusion | flops 65536 | bytes 524288 | tf_op jit(solution)/shard_map/mul | solution.py:292
  7.7 1.5 %constant_dynamic-slice_fusion = (bf16[6,4,64,256]{3,2,1,0:T(8,128)(2,1)S(1)}, bf16[6,4,64,256]{3,2,1,0:T(8,128)(2,1)S(1)}) fusion(bf16[12,4,64,256]{3,2,1,0:T(8,128)(2,1)} %param.6, s32[]{:T(128)S(6)} %select_n.7, s32[]{:T(128)S(6)} %select_n.6), kind=kLoop, calls=%fused_computation.1 | loop fusion | bytes 3145736 | tf_op jit(solution)/shard_map/dynamic_slice | solution.py:289
  9.2 0.6 collective-permute-start.6
  9.8 0.8 collective-permute-start.9
  10.6 0.9 collective-permute-done.10.refs_2_
  11.4 1.5 %collective-permute-start.15 = (bf16[1,4,64,256]{3,2,1,0:T(8,128)(2,1)}, bf16[1,4,64,256]{3,2,1,0:T(8,128)(2,1)S(1)}, u32[]{:S(2)}, u32[]{:S(2)}) collective-permute-start(bf16[1,4,64,256]{3,2,1,0:T(8,128)(2,1)} %refs_0_.1), channel_id=1, source_target_pairs={{0,4},{2,6},{4,0},{6,2},{8,12},{10,14},{12,8},{14,10},{16,20},{18,... | collective-permute-start | bytes 393224 | tf_op jit(solution)/shard_map/ppermute | solution.py:272
  12.9 0.6 collective-permute-done.8.refs_0_
  13.5 5.7 %collective-permute-done.9.refs_1_ = bf16[1,4,64,256]{3,2,1,0:T(8,128)(2,1)S(1)} collective-permute-done((bf16[1,4,64,256]{3,2,1,0:T(8,128)(2,1)}, bf16[1,4,64,256]{3,2,1,0:T(8,128)(2,1)S(1)}, u32[]{:S(2)}, u32[]{:S(2)}) %collective-permute-start.9) | collective-permute-done | bytes 131104 | tf_op jit(solution)/shard_map/ppermute | solution.py:272
  19.2 1.5 %collective-permute-start.1 = (bf16[1,4,64,256]{3,2,1,0:T(8,128)(2,1)S(1)}, bf16[1,4,64,256]{3,2,1,0:T(8,128)(2,1)S(1)}, u32[]{:S(2)}, u32[]{:S(2)}) collective-permute-start(bf16[1,4,64,256]{3,2,1,0:T(8,128)(2,1)S(1)} %collective-permute-done.refs_1_), channel_id=1, source_target_pairs={{0,4},{2,6},{4,0},{6,2},{8,12},{10,14},{12,8},{14,10},{16,20},{18,... | collective-permute-start | bytes 393224 | tf_op jit(solution)/shard_map/ppermute | solution.py:272
  20.7 0.6 collective-permute-start.11
  21.3 0.5 collective-permute-start.12
  21.9 3.7 %collective-permute-done.1.refs_3_ = bf16[1,4,64,256]{3,2,1,0:T(8,128)(2,1)S(1)} collective-permute-done((bf16[1,4,64,256]{3,2,1,0:T(8,128)(2,1)S(1)}, bf16[1,4,64,256]{3,2,1,0:T(8,128)(2,1)S(1)}, u32[]{:S(2)}, u32[]{:S(2)}) %collective-permute-start.1) | collective-permute-done | bytes 131104 | tf_op jit(solution)/shard_map/ppermute | solution.py:272
  25.6 2.3 %collective-permute-start.3 = (bf16[1,4,64,256]{3,2,1,0:T(8,128)(2,1)S(1)}, bf16[1,4,64,256]{3,2,1,0:T(8,128)(2,1)S(1)}, u32[]{:S(2)}, u32[]{:S(2)}) collective-permute-start(bf16[1,4,64,256]{3,2,1,0:T(8,128)(2,1)S(1)} %collective-permute-done.1.refs_3_), channel_id=1, source_target_pairs={{0,16},{2,18},{4,20},{6,22},{8,24},{10,26},{12,28},{14,30},{16,0},... | collective-permute-start | bytes 393224 | tf_op jit(solution)/shard_map/ppermute | solution.py:272
  27.8 4.5 %collective-permute-done.2.refs_0_ = bf16[1,4,64,256]{3,2,1,0:T(8,128)(2,1)S(1)} collective-permute-done((bf16[1,4,64,256]{3,2,1,0:T(8,128)(2,1)S(1)}, bf16[1,4,64,256]{3,2,1,0:T(8,128)(2,1)S(1)}, u32[]{:S(2)}, u32[]{:S(2)}) %collective-permute-start.2) | collective-permute-done | bytes 131104 | tf_op jit(solution)/shard_map/ppermute | solution.py:272
  32.3 1.0 %collective-permute-start.4 = (bf16[1,4,64,256]{3,2,1,0:T(8,128)(2,1)S(1)}, bf16[1,4,64,256]{3,2,1,0:T(8,128)(2,1)S(1)}, u32[]{:S(2)}, u32[]{:S(2)}) collective-permute-start(bf16[1,4,64,256]{3,2,1,0:T(8,128)(2,1)S(1)} %collective-permute-done.1.refs_3_), channel_id=1, source_target_pairs={{0,24},{2,26},{4,28},{6,30},{8,16},{10,18},{12,20},{14,22},{16,8},... | collective-permute-start | bytes 393224 | tf_op jit(solution)/shard_map/ppermute | solution.py:272
  33.3 2.0 %collective-permute-done.3.refs_1_ = bf16[1,4,64,256]{3,2,1,0:T(8,128)(2,1)S(1)} collective-permute-done((bf16[1,4,64,256]{3,2,1,0:T(8,128)(2,1)S(1)}, bf16[1,4,64,256]{3,2,1,0:T(8,128)(2,1)S(1)}, u32[]{:S(2)}, u32[]{:S(2)}) %collective-permute-start.3) | collective-permute-done | bytes 131104 | tf_op jit(solution)/shard_map/ppermute | solution.py:272
  35.3 3.8 %collective-permute-done.4.refs_2_ = bf16[1,4,64,256]{3,2,1,0:T(8,128)(2,1)S(1)} collective-permute-done((bf16[1,4,64,256]{3,2,1,0:T(8,128)(2,1)S(1)}, bf16[1,4,64,256]{3,2,1,0:T(8,128)(2,1)S(1)}, u32[]{:S(2)}, u32[]{:S(2)}) %collective-permute-start.4) | collective-permute-done | bytes 131104 | tf_op jit(solution)/shard_map/ppermute | solution.py:272
  39.1 0.5 collective-permute-start.13
  39.7 0.7 collective-permute-done.18.refs_7_
  40.6 0.4 collective-permute-start.19
  40.9 1.0 %shard_map.56 = (bf16[6,4,256,128]{3,2,1,0:T(8,128)(2,1)S(1)}, f32[8,64,256]{2,1,0:T(8,128)S(1)}, bf16[512,256]{1,0:T(8,128)(2,1)S(1)}, bf16[256,512]{1,0:T(8,128)(2,1)S(1)}) custom-call(bf16[6,4,64,256]{3,2,1,0:T(8,128)(2,1)S(1)} %get-tuple-element.18.own_reflect, bf16[6,4,64,256]{3,2,1,0:T(8,128)(2,1)S(1)} %collective-permute-done.6.far_reflect, ...), custom_call_target="tpu_custom_call" | custom-call | flops 10000000 | bytes 6291456 | tf_op jit(solution)/shard_map/pallas_call | solution.py:312
  42.0 0.4 collective-permute-done.19.refs_8_
  42.4 6.9 %shard_map.58.refs_8_ = f32[8,8,64,256]{3,2,1,0:T(8,128)S(1)} custom-call(s32[8]{0:T(128)S(1)} %copy-done.1, s32[12]{0:T(128)S(1)} %copy-done.2, bf16[1,4,64,256]{3,2,1,0:T(8,128)(2,1)S(1)} %copy-done, bf16[1,4,64,256]{3,2,1,0:T(8,128)(2,1)S(1)} %collective-permute-done.refs_1_, bf16[1,4,64,256]{3,2,1,0:T(8,128)(2,1)S(1)} %collective-permute-done.15.refs_2_, ...), custom_call_target="tpu_custom_call" | custom-call | flops 1000000000 | bytes 10485760 | tf_op jit(solution)/shard_map/pallas_call | solution.py:377
  49.3 1.8 %shard_map.59.refs_6_ = f32[8,8,64,256]{3,2,1,0:T(8,128)S(1)} custom-call(s32[8]{0:T(128)S(1)} %copy-done.1, s32[12]{0:T(128)S(1)} %copy-done.2, bf16[3,4,64,256]{3,2,1,0:T(8,128)(2,1)S(1)} %collective-permute-done.11.refs_0_, bf16[3,4,64,256]{3,2,1,0:T(8,128)(2,1)S(1)} %collective-permute-done.12.refs_1_, ...), custom_call_target="tpu_custom_call", output_to_operand_aliasing={{}: (10, {})} | custom-call | flops 1000000000 | bytes 10485760 | tf_op jit(solution)/shard_map/pallas_call | solution.py:377
  51.1 5.9 %shard_map.60 = (f32[4,64,256]{2,1,0:T(8,128)S(1)}, f32[4,64,256]{2,1,0:T(8,128)S(1)}, f32[8,8,64,256]{3,2,1,0:T(8,128)S(1)}) custom-call(s32[8]{0:T(128)S(1)} %copy-done.1, s32[12]{0:T(128)S(1)} %copy-done.2, bf16[3,4,64,256]{3,2,1,0:T(8,128)(2,1)S(1)} %shard_map.55.refs_0_, ...), custom_call_target="tpu_custom_call", output_to_operand_aliasing={{2}: (8, {})} | custom-call | flops 1000000000 | bytes 10485760 | tf_op jit(solution)/shard_map/pallas_call | solution.py:377
  57.0 0.7 collective-permute-start.21
  57.7 1.2 %collective-permute-done.21 = f32[4,64,256]{2,1,0:T(8,128)S(1)} collective-permute-done((f32[4,64,256]{2,1,0:T(8,128)S(1)}, f32[4,64,256]{2,1,0:T(8,128)S(1)}, u32[]{:S(2)}, u32[]{:S(2)}) %collective-permute-start.21) | collective-permute-done | bytes 262176 | tf_op jit(solution)/shard_map/ppermute | solution.py:267
  58.9 14.3 %all_to_all.10 = f32[16,16,256]{2,1,0:T(8,128)S(1)} all-to-all(f32[16,16,256]{2,1,0:T(8,128)S(1)} %bitcast.2), channel_id=1, replica_groups=mesh['off'=16,'dep'=2] {'off'}, dimensions={0} | all-to-all | bytes 524288 | tf_op jit(solution)/shard_map/all_to_all | solution.py:399
  73.3 12.8 %all_to_all.11 = f32[16,16,256]{2,1,0:T(8,128)S(1)} all-to-all(f32[16,16,256]{2,1,0:T(8,128)S(1)} %broadcast_in_dim.2), channel_id=1, replica_groups=mesh['off'=16,'dep'=2] {'off'}, dimensions={0} | all-to-all | bytes 524288 | tf_op jit(solution)/shard_map/all_to_all | solution.py:401
  86.1 0.7 copy.11
  (32 shorter events, 0.5 us)
Async XLA Ops:
  0.0 42.3 %copy-start = (bf16[1,4,64,256]{3,2,1,0:T(8,128)(2,1)S(1)}, bf16[1,4,64,256]{3,2,1,0:T(8,128)(2,1)}, u32[]{:S(2)}) copy-start(bf16[1,4,64,256]{3,2,1,0:T(8,128)(2,1)} %refs_0_.1) | copy-start | bytes 393220
  0.0 42.3 %copy-start.2 = (s32[12]{0:T(128)S(1)}, s32[12]{0:T(128)}, u32[]{:S(2)}) copy-start(s32[12]{0:T(128)} %lags_ref.5) | copy-start | bytes 148
  0.0 42.3 %copy-start.1 = (s32[8]{0:T(128)S(1)}, s32[8]{0:T(128)}, u32[]{:S(2)}) copy-start(s32[8]{0:T(128)} %owners_ref.5) | copy-start | bytes 100
  0.0 9.8 %collective-permute-start = (bf16[1,4,64,256]{3,2,1,0:T(8,128)(2,1)}, bf16[1,4,64,256]{3,2,1,0:T(8,128)(2,1)S(1)}, u32[]{:S(2)}, u32[]{:S(2)}) collective-permute-start(bf16[1,4,64,256]{3,2,1,0:T(8,128)(2,1)} %refs_0_.1), channel_id=1, source_target_pairs={{0,2},{2,0},{4,6},{6,4},{8,10},{10,8},{12,14},{14,12},{16,18},{18,... | collective-permute-start | bytes 393224 | tf_op jit(solution)/shard_map/ppermute | solution.py:272
  3.0 8.4 %collective-permute-start.10 = (bf16[1,4,64,256]{3,2,1,0:T(8,128)(2,1)}, bf16[1,4,64,256]{3,2,1,0:T(8,128)(2,1)S(1)}, u32[]{:S(2)}, u32[]{:S(2)}) collective-permute-start(bf16[1,4,64,256]{3,2,1,0:T(8,128)(2,1)} %refs_0_.1), channel_id=1, source_target_pairs={{0,24},{2,26},{4,28},{6,30},{8,16},{10,18},{12,20},{14,22},{16,8},... | collective-permute-start | bytes 393224 | tf_op jit(solution)/shard_map/ppermute | solution.py:272
  6.6 6.9 %collective-permute-start.8 = (bf16[1,4,64,256]{3,2,1,0:T(8,128)(2,1)}, bf16[1,4,64,256]{3,2,1,0:T(8,128)(2,1)S(1)}, u32[]{:S(2)}, u32[]{:S(2)}) collective-permute-start(bf16[1,4,64,256]{3,2,1,0:T(8,128)(2,1)} %refs_0_.1), channel_id=1, source_target_pairs={{0,8},{2,10},{4,12},{6,14},{8,0},{10,2},{12,4},{14,6},{16,24},{18,... | collective-permute-start | bytes 393224 | tf_op jit(solution)/shard_map/ppermute | solution.py:272
  7.6 14.2 %collective-permute-start.7 = (f32[4,64,256]{2,1,0:T(8,128)S(1)}, f32[4,64,256]{2,1,0:T(8,128)S(1)}, u32[]{:S(2)}, u32[]{:S(2)}) collective-permute-start(f32[4,64,256]{2,1,0:T(8,128)S(1)} %broadcast_multiply_fusion.own_courant), channel_id=1, source_target_pairs={{0,1},{1,0},{2,3},{3,2},{4,5},{5,4},{6,7},{7,6},{8,9},{9,8},{10,11... | collective-permute-start | bytes 786440 | tf_op jit(solution)/shard_map/ppermute | solution.py:267
  9.2 31.4 %collective-permute-start.6 = (bf16[6,4,64,256]{3,2,1,0:T(8,128)(2,1)S(1)}, bf16[6,4,64,256]{3,2,1,0:T(8,128)(2,1)S(1)}, u32[]{:S(2)}, u32[]{:S(2)}) collective-permute-start(bf16[6,4,64,256]{3,2,1,0:T(8,128)(2,1)S(1)} %get-tuple-element.17), channel_id=1, source_target_pairs={{0,1},{1,0},{2,3},{3,2},{4,5},{5,4},{6,7},{7,6},{8,9},{9,8},{10,11... | collective-permute-start | bytes 2359304 | tf_op jit(solution)/shard_map/ppermute | solution.py:267
  9.8 9.4 %collective-permute-start.9 = (bf16[1,4,64,256]{3,2,1,0:T(8,128)(2,1)}, bf16[1,4,64,256]{3,2,1,0:T(8,128)(2,1)S(1)}, u32[]{:S(2)}, u32[]{:S(2)}) collective-permute-start(bf16[1,4,64,256]{3,2,1,0:T(8,128)(2,1)} %refs_0_.1), channel_id=1, source_target_pairs={{0,16},{2,18},{4,20},{6,22},{8,24},{10,26},{12,28},{14,30},{16,0},... | collective-permute-start | bytes 393224 | tf_op jit(solution)/shard_map/ppermute | solution.py:272
  11.4 9.3 %collective-permute-start.15 = (bf16[1,4,64,256]{3,2,1,0:T(8,128)(2,1)}, bf16[1,4,64,256]{3,2,1,0:T(8,128)(2,1)S(1)}, u32[]{:S(2)}, u32[]{:S(2)}) collective-permute-start(bf16[1,4,64,256]{3,2,1,0:T(8,128)(2,1)} %refs_0_.1), channel_id=1, source_target_pairs={{0,4},{2,6},{4,0},{6,2},{8,12},{10,14},{12,8},{14,10},{16,20},{18,... | collective-permute-start | bytes 393224 | tf_op jit(solution)/shard_map/ppermute | solution.py:272
  13.5 7.8 %collective-permute-start.16 = (bf16[1,4,64,256]{3,2,1,0:T(8,128)(2,1)}, bf16[1,4,64,256]{3,2,1,0:T(8,128)(2,1)S(1)}, u32[]{:S(2)}, u32[]{:S(2)}) collective-permute-start(bf16[1,4,64,256]{3,2,1,0:T(8,128)(2,1)} %refs_0_.1), channel_id=1, source_target_pairs={{0,1},{1,0},{2,3},{3,2},{4,5},{5,4},{6,7},{7,6},{8,9},{9,8},{10,11... | collective-permute-start | bytes 393224 | tf_op jit(solution)/shard_map/ppermute | solution.py:267
  19.2 6.4 %collective-permute-start.1 = (bf16[1,4,64,256]{3,2,1,0:T(8,128)(2,1)S(1)}, bf16[1,4,64,256]{3,2,1,0:T(8,128)(2,1)S(1)}, u32[]{:S(2)}, u32[]{:S(2)}) collective-permute-start(bf16[1,4,64,256]{3,2,1,0:T(8,128)(2,1)S(1)} %collective-permute-done.refs_1_), channel_id=1, source_target_pairs={{0,4},{2,6},{4,0},{6,2},{8,12},{10,14},{12,8},{14,10},{16,20},{18,... | collective-permute-start | bytes 393224 | tf_op jit(solution)/shard_map/ppermute | solution.py:272
  20.7 18.3 %collective-permute-start.11 = (bf16[3,4,64,256]{3,2,1,0:T(8,128)(2,1)S(1)}, bf16[3,4,64,256]{3,2,1,0:T(8,128)(2,1)S(1)}, u32[]{:S(2)}, u32[]{:S(2)}) collective-permute-start(bf16[3,4,64,256]{3,2,1,0:T(8,128)(2,1)S(1)} %shard_map.57.refs_4_), channel_id=1, source_target_pairs={{0,2},{2,0},{4,6},{6,4},{8,10},{10,8},{12,14},{14,12},{16,18},{18,... | collective-permute-start | bytes 1179656 | tf_op jit(solution)/shard_map/ppermute | solution.py:272
  21.3 18.2 %collective-permute-start.12 = (bf16[3,4,64,256]{3,2,1,0:T(8,128)(2,1)S(1)}, bf16[3,4,64,256]{3,2,1,0:T(8,128)(2,1)S(1)}, u32[]{:S(2)}, u32[]{:S(2)}) collective-permute-start(bf16[3,4,64,256]{3,2,1,0:T(8,128)(2,1)S(1)} %shard_map.57.refs_4_), channel_id=1, source_target_pairs={{0,4},{2,6},{4,0},{6,2},{8,12},{10,14},{12,8},{14,10},{16,20},{18,... | collective-permute-start | bytes 1179656 | tf_op jit(solution)/shard_map/ppermute | solution.py:272
  21.9 3.7 %collective-permute-start.17 = (bf16[1,4,64,256]{3,2,1,0:T(8,128)(2,1)S(1)}, bf16[1,4,64,256]{3,2,1,0:T(8,128)(2,1)S(1)}, u32[]{:S(2)}, u32[]{:S(2)}) collective-permute-start(bf16[1,4,64,256]{3,2,1,0:T(8,128)(2,1)S(1)} %collective-permute-done.refs_1_), channel_id=1, source_target_pairs={{0,1},{1,0},{2,3},{3,2},{4,5},{5,4},{6,7},{7,6},{8,9},{9,8},{10,11... | collective-permute-start | bytes 393224 | tf_op jit(solution)/shard_map/ppermute | solution.py:267
  25.6 6.8 %collective-permute-start.2 = (bf16[1,4,64,256]{3,2,1,0:T(8,128)(2,1)S(1)}, bf16[1,4,64,256]{3,2,1,0:T(8,128)(2,1)S(1)}, u32[]{:S(2)}, u32[]{:S(2)}) collective-permute-start(bf16[1,4,64,256]{3,2,1,0:T(8,128)(2,1)S(1)} %collective-permute-done.1.refs_3_), channel_id=1, source_target_pairs={{0,8},{2,10},{4,12},{6,14},{8,0},{10,2},{12,4},{14,6},{16,24},{18,... | collective-permute-start | bytes 393224 | tf_op jit(solution)/shard_map/ppermute | solution.py:272
  25.6 9.7 %collective-permute-start.3 = (bf16[1,4,64,256]{3,2,1,0:T(8,128)(2,1)S(1)}, bf16[1,4,64,256]{3,2,1,0:T(8,128)(2,1)S(1)}, u32[]{:S(2)}, u32[]{:S(2)}) collective-permute-start(bf16[1,4,64,256]{3,2,1,0:T(8,128)(2,1)S(1)} %collective-permute-done.1.refs_3_), channel_id=1, source_target_pairs={{0,16},{2,18},{4,20},{6,22},{8,24},{10,26},{12,28},{14,30},{16,0},... | collective-permute-start | bytes 393224 | tf_op jit(solution)/shard_map/ppermute | solution.py:272
  32.3 6.8 %collective-permute-start.4 = (bf16[1,4,64,256]{3,2,1,0:T(8,128)(2,1)S(1)}, bf16[1,4,64,256]{3,2,1,0:T(8,128)(2,1)S(1)}, u32[]{:S(2)}, u32[]{:S(2)}) collective-permute-start(bf16[1,4,64,256]{3,2,1,0:T(8,128)(2,1)S(1)} %collective-permute-done.1.refs_3_), channel_id=1, source_target_pairs={{0,24},{2,26},{4,28},{6,30},{8,16},{10,18},{12,20},{14,22},{16,8},... | collective-permute-start | bytes 393224 | tf_op jit(solution)/shard_map/ppermute | solution.py:272
  35.3 7.1 %collective-permute-start.20 = (bf16[3,4,64,256]{3,2,1,0:T(8,128)(2,1)S(1)}, bf16[3,4,64,256]{3,2,1,0:T(8,128)(2,1)S(1)}, u32[]{:S(2)}, u32[]{:S(2)}) collective-permute-start(bf16[3,4,64,256]{3,2,1,0:T(8,128)(2,1)S(1)} %shard_map.57.refs_4_), channel_id=1, source_target_pairs={{0,1},{1,0},{2,3},{3,2},{4,5},{5,4},{6,7},{7,6},{8,9},{9,8},{10,11... | collective-permute-start | bytes 1179656 | tf_op jit(solution)/shard_map/ppermute | solution.py:267
  39.1 1.3 %collective-permute-start.18 = (bf16[1,4,64,256]{3,2,1,0:T(8,128)(2,1)S(1)}, bf16[1,4,64,256]{3,2,1,0:T(8,128)(2,1)S(1)}, u32[]{:S(2)}, u32[]{:S(2)}) collective-permute-start(bf16[1,4,64,256]{3,2,1,0:T(8,128)(2,1)S(1)} %collective-permute-done.15.refs_2_), channel_id=1, source_target_pairs={{0,1},{1,0},{2,3},{3,2},{4,5},{5,4},{6,7},{7,6},{8,9},{9,8},{10,11... | collective-permute-start | bytes 393224 | tf_op jit(solution)/shard_map/ppermute | solution.py:267
  39.1 10.2 %collective-permute-start.13 = (bf16[3,4,64,256]{3,2,1,0:T(8,128)(2,1)S(1)}, bf16[3,4,64,256]{3,2,1,0:T(8,128)(2,1)S(1)}, u32[]{:S(2)}, u32[]{:S(2)}) collective-permute-start(bf16[3,4,64,256]{3,2,1,0:T(8,128)(2,1)S(1)} %collective-permute-done.11.refs_0_), channel_id=1, source_target_pairs={{0,1},{1,0},{2,3},{3,2},{4,5},{5,4},{6,7},{7,6},{8,9},{9,8},{10,11... | collective-permute-start | bytes 1179656 | tf_op jit(solution)/shard_map/ppermute | solution.py:267
  39.6 9.7 %collective-permute-start.14 = (bf16[3,4,64,256]{3,2,1,0:T(8,128)(2,1)S(1)}, bf16[3,4,64,256]{3,2,1,0:T(8,128)(2,1)S(1)}, u32[]{:S(2)}, u32[]{:S(2)}) collective-permute-start(bf16[3,4,64,256]{3,2,1,0:T(8,128)(2,1)S(1)} %collective-permute-done.12.refs_1_), channel_id=1, source_target_pairs={{0,1},{1,0},{2,3},{3,2},{4,5},{5,4},{6,7},{7,6},{8,9},{9,8},{10,11... | collective-permute-start | bytes 1179656 | tf_op jit(solution)/shard_map/ppermute | solution.py:267
  40.4 10.7 %collective-permute-start.5 = (bf16[3,4,64,256]{3,2,1,0:T(8,128)(2,1)S(1)}, bf16[3,4,64,256]{3,2,1,0:T(8,128)(2,1)S(1)}, u32[]{:S(2)}, u32[]{:S(2)}) collective-permute-start(bf16[3,4,64,256]{3,2,1,0:T(8,128)(2,1)S(1)} %shard_map.55.refs_0_), channel_id=1, source_target_pairs={{0,1},{1,0},{2,3},{3,2},{4,5},{5,4},{6,7},{7,6},{8,9},{9,8},{10,11... | collective-permute-start | bytes 1179656 | tf_op jit(solution)/shard_map/ppermute | solution.py:267
  40.6 1.8 %collective-permute-start.19 = (bf16[1,4,64,256]{3,2,1,0:T(8,128)(2,1)S(1)}, bf16[1,4,64,256]{3,2,1,0:T(8,128)(2,1)S(1)}, u32[]{:S(2)}, u32[]{:S(2)}) collective-permute-start(bf16[1,4,64,256]{3,2,1,0:T(8,128)(2,1)S(1)} %collective-permute-done.1.refs_3_), channel_id=1, source_target_pairs={{0,1},{1,0},{2,3},{3,2},{4,5},{5,4},{6,7},{7,6},{8,9},{9,8},{10,11... | collective-permute-start | bytes 393224 | tf_op jit(solution)/shard_map/ppermute | solution.py:267
  57.0 1.9 %collective-permute-start.21 = (f32[4,64,256]{2,1,0:T(8,128)S(1)}, f32[4,64,256]{2,1,0:T(8,128)S(1)}, u32[]{:S(2)}, u32[]{:S(2)}) collective-permute-start(f32[4,64,256]{2,1,0:T(8,128)S(1)} %get-tuple-element.16), channel_id=1, source_target_pairs={{0,1},{1,0},{2,3},{3,2},{4,5},{5,4},{6,7},{7,6},{8,9},{9,8},{10,11... | collective-permute-start | bytes 786440 | tf_op jit(solution)/shard_map/ppermute | solution.py:267

commit v5 on v4

--- a/solution.py
+++ b/solution.py
@@ -97,7 +97,8 @@
 def band(rows, columns, block):
     i = lax.broadcasted_iota(jnp.int32, (rows, columns), 0)
     j = lax.broadcasted_iota(jnp.int32, (rows, columns), 1)
-    apart = jnp.where(i // block == j // block, jnp.abs(i - j), 0)
+    blocks_apart, cells_apart = jnp.abs(i // block - j // block), jnp.abs(i % block - j % block)
+    apart = jnp.where(blocks_apart == 0, cells_apart, jnp.where(cells_apart == 0, blocks_apart, 0))
     full = jnp.zeros((rows, columns), F32)
     for k in range(1, REACH + 1):
         full = jnp.where(apart == k, EXACT_WEIGHTS[k], full)
@@ -129,10 +130,10 @@
     lax.fori_loop(0, offsets, turn, 0)
 
 
-def vertical(plane_of, z, depth):
+def vertical(plane_of, z, depth, planes):
     total = EXACT_WEIGHTS[0] * plane_of(z)
     for k in range(1, REACH + 1):
-        near = [plane_of(n) for n in (z - k, z + k) if 0 <= n < depth]
+        near = [plane_of(n) for n in (z - k, z + k) if 0 <= n < depth and n // planes != z // planes]
         if near:
             total = total + EXACT_WEIGHTS[k] * functools.reduce(jnp.add, near)
     return total
@@ -159,7 +160,7 @@
             for i in range(stack):
                 p = b * stack + i
                 z = g * planes + p
-                upright = vertical(lambda n: plain[n], z, depth)
+                upright = vertical(lambda n: plain[n], z, depth, planes)
                 pieces.append(cour[z] * (both[p * rows : (p + 1) * rows] + upright))
             shifted[g * tiles + b, LAG : LAG + columns] = jnp.concatenate(pieces, 0).T
     chunk = 64
@@ -242,7 +243,7 @@
             both = sideways([high, low], across, down)
             for p in range(planes):
                 z = g * planes + p
-                laplace = both[p * rows : (p + 1) * rows] + vertical(lambda n: now[n], z, depth)
+                laplace = both[p * rows : (p + 1) * rows] + vertical(lambda n: now[n], z, depth, planes)
                 before[z] = (2.0 * now[z] - before[z]) + (cour[z] * laplace + sums[t, z])
 
     wave_a[...] = sums[0]

time: 87.1 us -> 86.4 us (level)
  no operation moved by 1% of the time
where the time goes in v5:
time: 86.4 us; the launch traced here: 86.1 us
  blocking collectives  27.1 us (31%)
  waiting for transfers between devices  23.2 us (27%)
  starting transfers between devices  17.3 us (20%)
  Pallas kernels  15.1 us (17%)
  local copies, waits for them, and re-layouts  2.24 us (3%)
  other arithmetic  1.03 us (1%)
    ppermute x11, waiting for transfers between devices, flip(): return lax.ppermute(x, 'off', [(i, i ^ bits) for i in range(count)])  21 us
    ppermute x11, starting transfers between devices, flip(): return lax.ppermute(x, 'off', [(i, i ^ bits) for i in range(count)])  14.9 us
    all_to_all x1, blocking collectives, core_pair(): summed = lax.all_to_all(pieces, 'off', 0, 0).sum(0)  14.4 us
    pallas_call x3, Pallas kernels, run(): pl.pallas_call(kernel, in_specs=[smem] * 2 + [vmem] * (n + 4 + len(extra)...  13.9 us
    all_to_all x1, blocking collectives, core_pair(): return lax.all_to_all(spread, 'off', 0, 0).reshape(half, rows, columns)  12.8 us
    ppermute x11, starting transfers between devices, swapped(): return lax.ppermute(x, 'dep', [(0, 1), (1, 0)])  2.41 us
    ppermute x11, waiting for transfers between devices, swapped(): return lax.ppermute(x, 'dep', [(0, 1), (1, 0)])  2.17 us
  transfers between devices with their start and end apart: 22, of which 10 were waited for; matrix products, arithmetic and copies ran while one was open for 3% of the time, Pallas kernels for 11%

profile of v5, /device:TPU:0, one launch (start us, length us, event | category | flops | bytes accessed | tf_op | source)
XLA Modules:
  0.0 86.1 jit_solution(3471037482812925981)
XLA Ops:
  0.0 3.0 %collective-permute-start = (bf16[1,4,64,256]{3,2,1,0:T(8,128)(2,1)}, bf16[1,4,64,256]{3,2,1,0:T(8,128)(2,1)S(1)}, u32[]{:S(2)}, u32[]{:S(2)}) collective-permute-start(bf16[1,4,64,256]{3,2,1,0:T(8,128)(2,1)} %refs_0_.1), channel_id=1, source_target_pairs={{0,2},{2,0},{4,6},{6,4},{8,10},{10,8},{12,14},{14,12},{16,18},{18,... | collective-permute-start | bytes 393224 | tf_op jit(solution)/shard_map/ppermute | solution.py:273
  3.0 3.6 %collective-permute-start.10 = (bf16[1,4,64,256]{3,2,1,0:T(8,128)(2,1)}, bf16[1,4,64,256]{3,2,1,0:T(8,128)(2,1)S(1)}, u32[]{:S(2)}, u32[]{:S(2)}) collective-permute-start(bf16[1,4,64,256]{3,2,1,0:T(8,128)(2,1)} %refs_0_.1), channel_id=1, source_target_pairs={{0,24},{2,26},{4,28},{6,30},{8,16},{10,18},{12,20},{14,22},{16,8},... | collective-permute-start | bytes 393224 | tf_op jit(solution)/shard_map/ppermute | solution.py:273
  6.6 1.0 %broadcast_multiply_fusion.own_courant = f32[4,64,256]{2,1,0:T(8,128)S(1)} fusion(f32[4,64,256]{2,1,0:T(8,128)} %param.7), kind=kLoop, calls=%fused_computation | loop fusion | flops 65536 | bytes 524288 | tf_op jit(solution)/shard_map/mul | solution.py:293
  7.7 1.5 %constant_dynamic-slice_fusion = (bf16[6,4,64,256]{3,2,1,0:T(8,128)(2,1)S(1)}, bf16[6,4,64,256]{3,2,1,0:T(8,128)(2,1)S(1)}) fusion(bf16[12,4,64,256]{3,2,1,0:T(8,128)(2,1)} %param.6, s32[]{:T(128)S(6)} %select_n.7, s32[]{:T(128)S(6)} %select_n.6), kind=kLoop, calls=%fused_computation.1 | loop fusion | bytes 3145736 | tf_op jit(solution)/shard_map/dynamic_slice | solution.py:290
  9.2 0.6 collective-permute-start.6
  9.8 0.8 collective-permute-start.9
  10.6 0.9 %collective-permute-done.10.refs_2_ = bf16[1,4,64,256]{3,2,1,0:T(8,128)(2,1)S(1)} collective-permute-done((bf16[1,4,64,256]{3,2,1,0:T(8,128)(2,1)}, bf16[1,4,64,256]{3,2,1,0:T(8,128)(2,1)S(1)}, u32[]{:S(2)}, u32[]{:S(2)}) %collective-permute-start.10) | collective-permute-done | bytes 131104 | tf_op jit(solution)/shard_map/ppermute | solution.py:273
  11.4 1.5 %collective-permute-start.15 = (bf16[1,4,64,256]{3,2,1,0:T(8,128)(2,1)}, bf16[1,4,64,256]{3,2,1,0:T(8,128)(2,1)S(1)}, u32[]{:S(2)}, u32[]{:S(2)}) collective-permute-start(bf16[1,4,64,256]{3,2,1,0:T(8,128)(2,1)} %refs_0_.1), channel_id=1, source_target_pairs={{0,4},{2,6},{4,0},{6,2},{8,12},{10,14},{12,8},{14,10},{16,20},{18,... | collective-permute-start | bytes 393224 | tf_op jit(solution)/shard_map/ppermute | solution.py:273
  12.9 0.6 collective-permute-done.8.refs_0_
  13.5 5.7 %collective-permute-done.9.refs_1_ = bf16[1,4,64,256]{3,2,1,0:T(8,128)(2,1)S(1)} collective-permute-done((bf16[1,4,64,256]{3,2,1,0:T(8,128)(2,1)}, bf16[1,4,64,256]{3,2,1,0:T(8,128)(2,1)S(1)}, u32[]{:S(2)}, u32[]{:S(2)}) %collective-permute-start.9) | collective-permute-done | bytes 131104 | tf_op jit(solution)/shard_map/ppermute | solution.py:273
  19.2 1.5 %collective-permute-start.1 = (bf16[1,4,64,256]{3,2,1,0:T(8,128)(2,1)S(1)}, bf16[1,4,64,256]{3,2,1,0:T(8,128)(2,1)S(1)}, u32[]{:S(2)}, u32[]{:S(2)}) collective-permute-start(bf16[1,4,64,256]{3,2,1,0:T(8,128)(2,1)S(1)} %collective-permute-done.refs_1_), channel_id=1, source_target_pairs={{0,4},{2,6},{4,0},{6,2},{8,12},{10,14},{12,8},{14,10},{16,20},{18,... | collective-permute-start | bytes 393224 | tf_op jit(solution)/shard_map/ppermute | solution.py:273
  20.7 0.6 collective-permute-start.11
  21.3 0.5 collective-permute-start.12
  21.9 3.7 %collective-permute-done.1.refs_3_ = bf16[1,4,64,256]{3,2,1,0:T(8,128)(2,1)S(1)} collective-permute-done((bf16[1,4,64,256]{3,2,1,0:T(8,128)(2,1)S(1)}, bf16[1,4,64,256]{3,2,1,0:T(8,128)(2,1)S(1)}, u32[]{:S(2)}, u32[]{:S(2)}) %collective-permute-start.1) | collective-permute-done | bytes 131104 | tf_op jit(solution)/shard_map/ppermute | solution.py:273
  25.6 2.3 %collective-permute-start.3 = (bf16[1,4,64,256]{3,2,1,0:T(8,128)(2,1)S(1)}, bf16[1,4,64,256]{3,2,1,0:T(8,128)(2,1)S(1)}, u32[]{:S(2)}, u32[]{:S(2)}) collective-permute-start(bf16[1,4,64,256]{3,2,1,0:T(8,128)(2,1)S(1)} %collective-permute-done.1.refs_3_), channel_id=1, source_target_pairs={{0,16},{2,18},{4,20},{6,22},{8,24},{10,26},{12,28},{14,30},{16,0},... | collective-permute-start | bytes 393224 | tf_op jit(solution)/shard_map/ppermute | solution.py:273
  27.8 4.5 %collective-permute-done.2.refs_0_ = bf16[1,4,64,256]{3,2,1,0:T(8,128)(2,1)S(1)} collective-permute-done((bf16[1,4,64,256]{3,2,1,0:T(8,128)(2,1)S(1)}, bf16[1,4,64,256]{3,2,1,0:T(8,128)(2,1)S(1)}, u32[]{:S(2)}, u32[]{:S(2)}) %collective-permute-start.2) | collective-permute-done | bytes 131104 | tf_op jit(solution)/shard_map/ppermute | solution.py:273
  32.3 1.0 %collective-permute-start.4 = (bf16[1,4,64,256]{3,2,1,0:T(8,128)(2,1)S(1)}, bf16[1,4,64,256]{3,2,1,0:T(8,128)(2,1)S(1)}, u32[]{:S(2)}, u32[]{:S(2)}) collective-permute-start(bf16[1,4,64,256]{3,2,1,0:T(8,128)(2,1)S(1)} %collective-permute-done.1.refs_3_), channel_id=1, source_target_pairs={{0,24},{2,26},{4,28},{6,30},{8,16},{10,18},{12,20},{14,22},{16,8},... | collective-permute-start | bytes 393224 | tf_op jit(solution)/shard_map/ppermute | solution.py:273
  33.3 2.0 %collective-permute-done.3.refs_1_ = bf16[1,4,64,256]{3,2,1,0:T(8,128)(2,1)S(1)} collective-permute-done((bf16[1,4,64,256]{3,2,1,0:T(8,128)(2,1)S(1)}, bf16[1,4,64,256]{3,2,1,0:T(8,128)(2,1)S(1)}, u32[]{:S(2)}, u32[]{:S(2)}) %collective-permute-start.3) | collective-permute-done | bytes 131104 | tf_op jit(solution)/shard_map/ppermute | solution.py:273
  35.3 3.8 %collective-permute-done.4.refs_2_ = bf16[1,4,64,256]{3,2,1,0:T(8,128)(2,1)S(1)} collective-permute-done((bf16[1,4,64,256]{3,2,1,0:T(8,128)(2,1)S(1)}, bf16[1,4,64,256]{3,2,1,0:T(8,128)(2,1)S(1)}, u32[]{:S(2)}, u32[]{:S(2)}) %collective-permute-start.4) | collective-permute-done | bytes 131104 | tf_op jit(solution)/shard_map/ppermute | solution.py:273
  39.1 0.5 collective-permute-start.13
  39.7 0.7 collective-permute-done.18.refs_7_
  40.6 0.4 collective-permute-start.19
  40.9 1.1 %shard_map.56 = (bf16[6,4,256,128]{3,2,1,0:T(8,128)(2,1)S(1)}, f32[8,64,256]{2,1,0:T(8,128)S(1)}, bf16[512,256]{1,0:T(8,128)(2,1)S(1)}, bf16[256,512]{1,0:T(8,128)(2,1)S(1)}) custom-call(bf16[6,4,64,256]{3,2,1,0:T(8,128)(2,1)S(1)} %get-tuple-element.18.own_reflect, bf16[6,4,64,256]{3,2,1,0:T(8,128)(2,1)S(1)} %collective-permute-done.6.far_reflect, ...), custom_call_target="tpu_custom_call" | custom-call | flops 10000000 | bytes 6291456 | tf_op jit(solution)/shard_map/pallas_call | solution.py:313
  42.1 0.3 collective-permute-done.19.refs_8_
  42.4 6.6 %shard_map.58.refs_8_ = f32[8,8,64,256]{3,2,1,0:T(8,128)S(1)} custom-call(s32[8]{0:T(128)S(1)} %copy-done.1, s32[12]{0:T(128)S(1)} %copy-done.2, bf16[1,4,64,256]{3,2,1,0:T(8,128)(2,1)S(1)} %copy-done, bf16[1,4,64,256]{3,2,1,0:T(8,128)(2,1)S(1)} %collective-permute-done.refs_1_, bf16[1,4,64,256]{3,2,1,0:T(8,128)(2,1)S(1)} %collective-permute-done.15.refs_2_, ...), custom_call_target="tpu_custom_call" | custom-call | flops 1000000000 | bytes 10485760 | tf_op jit(solution)/shard_map/pallas_call | solution.py:378
  49.0 1.7 %shard_map.59.refs_6_ = f32[8,8,64,256]{3,2,1,0:T(8,128)S(1)} custom-call(s32[8]{0:T(128)S(1)} %copy-done.1, s32[12]{0:T(128)S(1)} %copy-done.2, bf16[3,4,64,256]{3,2,1,0:T(8,128)(2,1)S(1)} %collective-permute-done.11.refs_0_, bf16[3,4,64,256]{3,2,1,0:T(8,128)(2,1)S(1)} %collective-permute-done.12.refs_1_, ...), custom_call_target="tpu_custom_call", output_to_operand_aliasing={{}: (10, {})} | custom-call | flops 1000000000 | bytes 10485760 | tf_op jit(solution)/shard_map/pallas_call | solution.py:378
  50.7 5.6 %shard_map.60 = (f32[4,64,256]{2,1,0:T(8,128)S(1)}, f32[4,64,256]{2,1,0:T(8,128)S(1)}, f32[8,8,64,256]{3,2,1,0:T(8,128)S(1)}) custom-call(s32[8]{0:T(128)S(1)} %copy-done.1, s32[12]{0:T(128)S(1)} %copy-done.2, bf16[3,4,64,256]{3,2,1,0:T(8,128)(2,1)S(1)} %shard_map.55.refs_0_, ...), custom_call_target="tpu_custom_call", output_to_operand_aliasing={{2}: (8, {})} | custom-call | flops 1000000000 | bytes 10485760 | tf_op jit(solution)/shard_map/pallas_call | solution.py:378
  56.3 0.7 collective-permute-start.21
  57.0 1.2 %collective-permute-done.21 = f32[4,64,256]{2,1,0:T(8,128)S(1)} collective-permute-done((f32[4,64,256]{2,1,0:T(8,128)S(1)}, f32[4,64,256]{2,1,0:T(8,128)S(1)}, u32[]{:S(2)}, u32[]{:S(2)}) %collective-permute-start.21) | collective-permute-done | bytes 262176 | tf_op jit(solution)/shard_map/ppermute | solution.py:268
  58.2 14.4 %all_to_all.10 = f32[16,16,256]{2,1,0:T(8,128)S(1)} all-to-all(f32[16,16,256]{2,1,0:T(8,128)S(1)} %bitcast.2), channel_id=1, replica_groups=mesh['off'=16,'dep'=2] {'off'}, dimensions={0} | all-to-all | bytes 524288 | tf_op jit(solution)/shard_map/all_to_all | solution.py:400
  72.6 12.8 %all_to_all.11 = f32[16,16,256]{2,1,0:T(8,128)S(1)} all-to-all(f32[16,16,256]{2,1,0:T(8,128)S(1)} %broadcast_in_dim.2), channel_id=1, replica_groups=mesh['off'=16,'dep'=2] {'off'}, dimensions={0} | all-to-all | bytes 524288 | tf_op jit(solution)/shard_map/all_to_all | solution.py:402
  85.4 0.7 copy.11
  (32 shorter events, 0.5 us)
Async XLA Ops:
  0.0 42.3 %copy-start = (bf16[1,4,64,256]{3,2,1,0:T(8,128)(2,1)S(1)}, bf16[1,4,64,256]{3,2,1,0:T(8,128)(2,1)}, u32[]{:S(2)}) copy-start(bf16[1,4,64,256]{3,2,1,0:T(8,128)(2,1)} %refs_0_.1) | copy-start | bytes 393220
  0.0 42.3 %copy-start.2 = (s32[12]{0:T(128)S(1)}, s32[12]{0:T(128)}, u32[]{:S(2)}) copy-start(s32[12]{0:T(128)} %lags_ref.5) | copy-start | bytes 148
  0.0 42.3 %copy-start.1 = (s32[8]{0:T(128)S(1)}, s32[8]{0:T(128)}, u32[]{:S(2)}) copy-start(s32[8]{0:T(128)} %owners_ref.5) | copy-start | bytes 100
  0.0 9.8 %collective-permute-start = (bf16[1,4,64,256]{3,2,1,0:T(8,128)(2,1)}, bf16[1,4,64,256]{3,2,1,0:T(8,128)(2,1)S(1)}, u32[]{:S(2)}, u32[]{:S(2)}) collective-permute-start(bf16[1,4,64,256]{3,2,1,0:T(8,128)(2,1)} %refs_0_.1), channel_id=1, source_target_pairs={{0,2},{2,0},{4,6},{6,4},{8,10},{10,8},{12,14},{14,12},{16,18},{18,... | collective-permute-start | bytes 393224 | tf_op jit(solution)/shard_map/ppermute | solution.py:273
  3.0 8.4 %collective-permute-start.10 = (bf16[1,4,64,256]{3,2,1,0:T(8,128)(2,1)}, bf16[1,4,64,256]{3,2,1,0:T(8,128)(2,1)S(1)}, u32[]{:S(2)}, u32[]{:S(2)}) collective-permute-start(bf16[1,4,64,256]{3,2,1,0:T(8,128)(2,1)} %refs_0_.1), channel_id=1, source_target_pairs={{0,24},{2,26},{4,28},{6,30},{8,16},{10,18},{12,20},{14,22},{16,8},... | collective-permute-start | bytes 393224 | tf_op jit(solution)/shard_map/ppermute | solution.py:273
  6.6 6.9 %collective-permute-start.8 = (bf16[1,4,64,256]{3,2,1,0:T(8,128)(2,1)}, bf16[1,4,64,256]{3,2,1,0:T(8,128)(2,1)S(1)}, u32[]{:S(2)}, u32[]{:S(2)}) collective-permute-start(bf16[1,4,64,256]{3,2,1,0:T(8,128)(2,1)} %refs_0_.1), channel_id=1, source_target_pairs={{0,8},{2,10},{4,12},{6,14},{8,0},{10,2},{12,4},{14,6},{16,24},{18,... | collective-permute-start | bytes 393224 | tf_op jit(solution)/shard_map/ppermute | solution.py:273
  7.6 14.2 %collective-permute-start.7 = (f32[4,64,256]{2,1,0:T(8,128)S(1)}, f32[4,64,256]{2,1,0:T(8,128)S(1)}, u32[]{:S(2)}, u32[]{:S(2)}) collective-permute-start(f32[4,64,256]{2,1,0:T(8,128)S(1)} %broadcast_multiply_fusion.own_courant), channel_id=1, source_target_pairs={{0,1},{1,0},{2,3},{3,2},{4,5},{5,4},{6,7},{7,6},{8,9},{9,8},{10,11... | collective-permute-start | bytes 786440 | tf_op jit(solution)/shard_map/ppermute | solution.py:268
  9.2 31.4 %collective-permute-start.6 = (bf16[6,4,64,256]{3,2,1,0:T(8,128)(2,1)S(1)}, bf16[6,4,64,256]{3,2,1,0:T(8,128)(2,1)S(1)}, u32[]{:S(2)}, u32[]{:S(2)}) collective-permute-start(bf16[6,4,64,256]{3,2,1,0:T(8,128)(2,1)S(1)} %get-tuple-element.17), channel_id=1, source_target_pairs={{0,1},{1,0},{2,3},{3,2},{4,5},{5,4},{6,7},{7,6},{8,9},{9,8},{10,11... | collective-permute-start | bytes 2359304 | tf_op jit(solution)/shard_map/ppermute | solution.py:268
  9.8 9.4 %collective-permute-start.9 = (bf16[1,4,64,256]{3,2,1,0:T(8,128)(2,1)}, bf16[1,4,64,256]{3,2,1,0:T(8,128)(2,1)S(1)}, u32[]{:S(2)}, u32[]{:S(2)}) collective-permute-start(bf16[1,4,64,256]{3,2,1,0:T(8,128)(2,1)} %refs_0_.1), channel_id=1, source_target_pairs={{0,16},{2,18},{4,20},{6,22},{8,24},{10,26},{12,28},{14,30},{16,0},... | collective-permute-start | bytes 393224 | tf_op jit(solution)/shard_map/ppermute | solution.py:273
  11.4 9.3 %collective-permute-start.15 = (bf16[1,4,64,256]{3,2,1,0:T(8,128)(2,1)}, bf16[1,4,64,256]{3,2,1,0:T(8,128)(2,1)S(1)}, u32[]{:S(2)}, u32[]{:S(2)}) collective-permute-start(bf16[1,4,64,256]{3,2,1,0:T(8,128)(2,1)} %refs_0_.1), channel_id=1, source_target_pairs={{0,4},{2,6},{4,0},{6,2},{8,12},{10,14},{12,8},{14,10},{16,20},{18,... | collective-permute-start | bytes 393224 | tf_op jit(solution)/shard_map/ppermute | solution.py:273
  13.5 7.8 %collective-permute-start.16 = (bf16[1,4,64,256]{3,2,1,0:T(8,128)(2,1)}, bf16[1,4,64,256]{3,2,1,0:T(8,128)(2,1)S(1)}, u32[]{:S(2)}, u32[]{:S(2)}) collective-permute-start(bf16[1,4,64,256]{3,2,1,0:T(8,128)(2,1)} %refs_0_.1), channel_id=1, source_target_pairs={{0,1},{1,0},{2,3},{3,2},{4,5},{5,4},{6,7},{7,6},{8,9},{9,8},{10,11... | collective-permute-start | bytes 393224 | tf_op jit(solution)/shard_map/ppermute | solution.py:268
  19.2 6.4 %collective-permute-start.1 = (bf16[1,4,64,256]{3,2,1,0:T(8,128)(2,1)S(1)}, bf16[1,4,64,256]{3,2,1,0:T(8,128)(2,1)S(1)}, u32[]{:S(2)}, u32[]{:S(2)}) collective-permute-start(bf16[1,4,64,256]{3,2,1,0:T(8,128)(2,1)S(1)} %collective-permute-done.refs_1_), channel_id=1, source_target_pairs={{0,4},{2,6},{4,0},{6,2},{8,12},{10,14},{12,8},{14,10},{16,20},{18,... | collective-permute-start | bytes 393224 | tf_op jit(solution)/shard_map/ppermute | solution.py:273
  20.7 18.3 %collective-permute-start.11 = (bf16[3,4,64,256]{3,2,1,0:T(8,128)(2,1)S(1)}, bf16[3,4,64,256]{3,2,1,0:T(8,128)(2,1)S(1)}, u32[]{:S(2)}, u32[]{:S(2)}) collective-permute-start(bf16[3,4,64,256]{3,2,1,0:T(8,128)(2,1)S(1)} %shard_map.57.refs_4_), channel_id=1, source_target_pairs={{0,2},{2,0},{4,6},{6,4},{8,10},{10,8},{12,14},{14,12},{16,18},{18,... | collective-permute-start | bytes 1179656 | tf_op jit(solution)/shard_map/ppermute | solution.py:273
  21.3 18.2 %collective-permute-start.12 = (bf16[3,4,64,256]{3,2,1,0:T(8,128)(2,1)S(1)}, bf16[3,4,64,256]{3,2,1,0:T(8,128)(2,1)S(1)}, u32[]{:S(2)}, u32[]{:S(2)}) collective-permute-start(bf16[3,4,64,256]{3,2,1,0:T(8,128)(2,1)S(1)} %shard_map.57.refs_4_), channel_id=1, source_target_pairs={{0,4},{2,6},{4,0},{6,2},{8,12},{10,14},{12,8},{14,10},{16,20},{18,... | collective-permute-start | bytes 1179656 | tf_op jit(solution)/shard_map/ppermute | solution.py:273
  21.9 3.7 %collective-permute-start.17 = (bf16[1,4,64,256]{3,2,1,0:T(8,128)(2,1)S(1)}, bf16[1,4,64,256]{3,2,1,0:T(8,128)(2,1)S(1)}, u32[]{:S(2)}, u32[]{:S(2)}) collective-permute-start(bf16[1,4,64,256]{3,2,1,0:T(8,128)(2,1)S(1)} %collective-permute-done.refs_1_), channel_id=1, source_target_pairs={{0,1},{1,0},{2,3},{3,2},{4,5},{5,4},{6,7},{7,6},{8,9},{9,8},{10,11... | collective-permute-start | bytes 393224 | tf_op jit(solution)/shard_map/ppermute | solution.py:268
  25.6 6.8 %collective-permute-start.2 = (bf16[1,4,64,256]{3,2,1,0:T(8,128)(2,1)S(1)}, bf16[1,4,64,256]{3,2,1,0:T(8,128)(2,1)S(1)}, u32[]{:S(2)}, u32[]{:S(2)}) collective-permute-start(bf16[1,4,64,256]{3,2,1,0:T(8,128)(2,1)S(1)} %collective-permute-done.1.refs_3_), channel_id=1, source_target_pairs={{0,8},{2,10},{4,12},{6,14},{8,0},{10,2},{12,4},{14,6},{16,24},{18,... | collective-permute-start | bytes 393224 | tf_op jit(solution)/shard_map/ppermute | solution.py:273
  25.6 9.7 %collective-permute-start.3 = (bf16[1,4,64,256]{3,2,1,0:T(8,128)(2,1)S(1)}, bf16[1,4,64,256]{3,2,1,0:T(8,128)(2,1)S(1)}, u32[]{:S(2)}, u32[]{:S(2)}) collective-permute-start(bf16[1,4,64,256]{3,2,1,0:T(8,128)(2,1)S(1)} %collective-permute-done.1.refs_3_), channel_id=1, source_target_pairs={{0,16},{2,18},{4,20},{6,22},{8,24},{10,26},{12,28},{14,30},{16,0},... | collective-permute-start | bytes 393224 | tf_op jit(solution)/shard_map/ppermute | solution.py:273
  32.3 6.8 %collective-permute-start.4 = (bf16[1,4,64,256]{3,2,1,0:T(8,128)(2,1)S(1)}, bf16[1,4,64,256]{3,2,1,0:T(8,128)(2,1)S(1)}, u32[]{:S(2)}, u32[]{:S(2)}) collective-permute-start(bf16[1,4,64,256]{3,2,1,0:T(8,128)(2,1)S(1)} %collective-permute-done.1.refs_3_), channel_id=1, source_target_pairs={{0,24},{2,26},{4,28},{6,30},{8,16},{10,18},{12,20},{14,22},{16,8},... | collective-permute-start | bytes 393224 | tf_op jit(solution)/shard_map/ppermute | solution.py:273
  35.3 7.1 %collective-permute-start.20 = (bf16[3,4,64,256]{3,2,1,0:T(8,128)(2,1)S(1)}, bf16[3,4,64,256]{3,2,1,0:T(8,128)(2,1)S(1)}, u32[]{:S(2)}, u32[]{:S(2)}) collective-permute-start(bf16[3,4,64,256]{3,2,1,0:T(8,128)(2,1)S(1)} %shard_map.57.refs_4_), channel_id=1, source_target_pairs={{0,1},{1,0},{2,3},{3,2},{4,5},{5,4},{6,7},{7,6},{8,9},{9,8},{10,11... | collective-permute-start | bytes 1179656 | tf_op jit(solution)/shard_map/ppermute | solution.py:268
  39.1 1.3 %collective-permute-start.18 = (bf16[1,4,64,256]{3,2,1,0:T(8,128)(2,1)S(1)}, bf16[1,4,64,256]{3,2,1,0:T(8,128)(2,1)S(1)}, u32[]{:S(2)}, u32[]{:S(2)}) collective-permute-start(bf16[1,4,64,256]{3,2,1,0:T(8,128)(2,1)S(1)} %collective-permute-done.15.refs_2_), channel_id=1, source_target_pairs={{0,1},{1,0},{2,3},{3,2},{4,5},{5,4},{6,7},{7,6},{8,9},{9,8},{10,11... | collective-permute-start | bytes 393224 | tf_op jit(solution)/shard_map/ppermute | solution.py:268
  39.1 9.9 %collective-permute-start.13 = (bf16[3,4,64,256]{3,2,1,0:T(8,128)(2,1)S(1)}, bf16[3,4,64,256]{3,2,1,0:T(8,128)(2,1)S(1)}, u32[]{:S(2)}, u32[]{:S(2)}) collective-permute-start(bf16[3,4,64,256]{3,2,1,0:T(8,128)(2,1)S(1)} %collective-permute-done.11.refs_0_), channel_id=1, source_target_pairs={{0,1},{1,0},{2,3},{3,2},{4,5},{5,4},{6,7},{7,6},{8,9},{9,8},{10,11... | collective-permute-start | bytes 1179656 | tf_op jit(solution)/shard_map/ppermute | solution.py:268
  39.6 9.4 %collective-permute-start.14 = (bf16[3,4,64,256]{3,2,1,0:T(8,128)(2,1)S(1)}, bf16[3,4,64,256]{3,2,1,0:T(8,128)(2,1)S(1)}, u32[]{:S(2)}, u32[]{:S(2)}) collective-permute-start(bf16[3,4,64,256]{3,2,1,0:T(8,128)(2,1)S(1)} %collective-permute-done.12.refs_1_), channel_id=1, source_target_pairs={{0,1},{1,0},{2,3},{3,2},{4,5},{5,4},{6,7},{7,6},{8,9},{9,8},{10,11... | collective-permute-start | bytes 1179656 | tf_op jit(solution)/shard_map/ppermute | solution.py:268
  40.4 10.3 %collective-permute-start.5 = (bf16[3,4,64,256]{3,2,1,0:T(8,128)(2,1)S(1)}, bf16[3,4,64,256]{3,2,1,0:T(8,128)(2,1)S(1)}, u32[]{:S(2)}, u32[]{:S(2)}) collective-permute-start(bf16[3,4,64,256]{3,2,1,0:T(8,128)(2,1)S(1)} %shard_map.55.refs_0_), channel_id=1, source_target_pairs={{0,1},{1,0},{2,3},{3,2},{4,5},{5,4},{6,7},{7,6},{8,9},{9,8},{10,11... | collective-permute-start | bytes 1179656 | tf_op jit(solution)/shard_map/ppermute | solution.py:268
  40.6 1.8 %collective-permute-start.19 = (bf16[1,4,64,256]{3,2,1,0:T(8,128)(2,1)S(1)}, bf16[1,4,64,256]{3,2,1,0:T(8,128)(2,1)S(1)}, u32[]{:S(2)}, u32[]{:S(2)}) collective-permute-start(bf16[1,4,64,256]{3,2,1,0:T(8,128)(2,1)S(1)} %collective-permute-done.1.refs_3_), channel_id=1, source_target_pairs={{0,1},{1,0},{2,3},{3,2},{4,5},{5,4},{6,7},{7,6},{8,9},{9,8},{10,11... | collective-permute-start | bytes 393224 | tf_op jit(solution)/shard_map/ppermute | solution.py:268
  56.3 1.9 %collective-permute-start.21 = (f32[4,64,256]{2,1,0:T(8,128)S(1)}, f32[4,64,256]{2,1,0:T(8,128)S(1)}, u32[]{:S(2)}, u32[]{:S(2)}) collective-permute-start(f32[4,64,256]{2,1,0:T(8,128)S(1)} %get-tuple-element.16), channel_id=1, source_target_pairs={{0,1},{1,0},{2,3},{3,2},{4,5},{5,4},{6,7},{7,6},{8,9},{9,8},{10,11... | collective-permute-start | bytes 786440 | tf_op jit(solution)/shard_map/ppermute | solution.py:268

commit v6 on v5

--- a/solution.py
+++ b/solution.py
@@ -200,6 +200,13 @@
                 plain[(1 - core) * half + z] = far[at, z].astype(F32)
 
 
+def first_with_owner(owners_ref, t):
+    first = t
+    for s in reversed(range(ITERS)):
+        first = jnp.where((s < t) & (owners_ref[s] == owners_ref[t]), s, first)
+    return first
+
+
 def sums_kernel(groups, where_now, owners_ref, lags_ref, rt, cour, across, down, sums, plain, shifted, turned):
     first = where_now[1] * rt.shape[0]
     clear_rims(shifted, cour.shape[2])
@@ -209,9 +216,10 @@
 
     def step(t, counts):
         taken, after = [], []
+        fresh = first_with_owner(owners_ref, t) == t
         for (choose, low, high), count in zip(groups, counts, strict=True):
             tests = choose(owners_ref[t] ^ where_now[0])
-            due = (count >= low) & (count < high)
+            due = fresh & (count >= low) & (count < high)
             taken += [(test & due, *bank) for test, *bank in tests]
             after.append(count + any_of(tests).astype(jnp.int32))
 
@@ -238,13 +246,14 @@
     planes = group // rows
 
     def grow(t, now, before):
+        served = first_with_owner(owners_ref, t)
         for g in range(depth // planes):
             high, low = split(jnp.concatenate([now[g * planes + p] for p in range(planes)], 0))
             both = sideways([high, low], across, down)
             for p in range(planes):
                 z = g * planes + p
                 laplace = both[p * rows : (p + 1) * rows] + vertical(lambda n: now[n], z, depth, planes)
-                before[z] = (2.0 * now[z] - before[z]) + (cour[z] * laplace + sums[t, z])
+                before[z] = (2.0 * now[z] - before[z]) + (cour[z] * laplace + sums[served, z])
 
     wave_a[...] = sums[0]
     wave_b[...] = jnp.zeros(wave_b.shape, F32)

time: 86.4 us -> 84.5 us (0.978)
  Pallas kernels: 15.1 us -> 13.4 us
    pallas_call x3, Pallas kernels: 13.9 us -> 12.2 us  [run(): pl.pallas_call(kernel, in_specs=[smem] * 2 + [vmem] * (n + 4 + len(extra)...]
  transfers between devices with their start and end apart: 22 -> 22, of which waited for: 10 -> 10; matrix products, arithmetic and copies ran while one was open for 3% -> 3% of each run, Pallas kernels for 11% -> 9%
where the time goes in v6:
time: 84.5 us; the launch traced here: 84.2 us
  blocking collectives  27.1 us (32%)
  waiting for transfers between devices  23.2 us (27%)
  starting transfers between devices  17.2 us (20%)
  Pallas kernels  13.4 us (16%)
  local copies, waits for them, and re-layouts  2.24 us (3%)
  other arithmetic  1.03 us (1%)
    ppermute x11, waiting for transfers between devices, flip(): return lax.ppermute(x, 'off', [(i, i ^ bits) for i in range(count)])  21 us
    ppermute x11, starting transfers between devices, flip(): return lax.ppermute(x, 'off', [(i, i ^ bits) for i in range(count)])  14.9 us
    all_to_all x1, blocking collectives, core_pair(): summed = lax.all_to_all(pieces, 'off', 0, 0).sum(0)  14.3 us
    all_to_all x1, blocking collectives, core_pair(): return lax.all_to_all(spread, 'off', 0, 0).reshape(half, rows, columns)  12.8 us
    pallas_call x3, Pallas kernels, run(): pl.pallas_call(kernel, in_specs=[smem] * 2 + [vmem] * (n + 4 + len(extra)...  12.2 us
    ppermute x11, starting transfers between devices, swapped(): return lax.ppermute(x, 'dep', [(0, 1), (1, 0)])  2.33 us
    ppermute x11, waiting for transfers between devices, swapped(): return lax.ppermute(x, 'dep', [(0, 1), (1, 0)])  2.17 us
  transfers between devices with their start and end apart: 22, of which 10 were waited for; matrix products, arithmetic and copies ran while one was open for 3% of the time, Pallas kernels for 9%

profile of v6, /device:TPU:0, one launch (start us, length us, event | category | flops | bytes accessed | tf_op | source)
XLA Modules:
  0.0 84.2 jit_solution(5849205099824593538)
XLA Ops:
  0.0 3.0 %collective-permute-start = (bf16[1,4,64,256]{3,2,1,0:T(8,128)(2,1)}, bf16[1,4,64,256]{3,2,1,0:T(8,128)(2,1)S(1)}, u32[]{:S(2)}, u32[]{:S(2)}) collective-permute-start(bf16[1,4,64,256]{3,2,1,0:T(8,128)(2,1)} %refs_0_.1), channel_id=1, source_target_pairs={{0,2},{2,0},{4,6},{6,4},{8,10},{10,8},{12,14},{14,12},{16,18},{18,... | collective-permute-start | bytes 393224 | tf_op jit(solution)/shard_map/ppermute | solution.py:282
  3.0 3.6 %collective-permute-start.10 = (bf16[1,4,64,256]{3,2,1,0:T(8,128)(2,1)}, bf16[1,4,64,256]{3,2,1,0:T(8,128)(2,1)S(1)}, u32[]{:S(2)}, u32[]{:S(2)}) collective-permute-start(bf16[1,4,64,256]{3,2,1,0:T(8,128)(2,1)} %refs_0_.1), channel_id=1, source_target_pairs={{0,24},{2,26},{4,28},{6,30},{8,16},{10,18},{12,20},{14,22},{16,8},... | collective-permute-start | bytes 393224 | tf_op jit(solution)/shard_map/ppermute | solution.py:282
  6.6 1.0 %broadcast_multiply_fusion.own_courant = f32[4,64,256]{2,1,0:T(8,128)S(1)} fusion(f32[4,64,256]{2,1,0:T(8,128)} %param.7), kind=kLoop, calls=%fused_computation | loop fusion | flops 65536 | bytes 524288 | tf_op jit(solution)/shard_map/mul | solution.py:302
  7.7 1.5 %constant_dynamic-slice_fusion = (bf16[6,4,64,256]{3,2,1,0:T(8,128)(2,1)S(1)}, bf16[6,4,64,256]{3,2,1,0:T(8,128)(2,1)S(1)}) fusion(bf16[12,4,64,256]{3,2,1,0:T(8,128)(2,1)} %param.6, s32[]{:T(128)S(6)} %select_n.7, s32[]{:T(128)S(6)} %select_n.6), kind=kLoop, calls=%fused_computation.1 | loop fusion | bytes 3145736 | tf_op jit(solution)/shard_map/dynamic_slice | solution.py:299
  9.2 0.6 collective-permute-start.6
  9.8 0.8 collective-permute-start.9
  10.6 0.9 %collective-permute-done.10.refs_2_ = bf16[1,4,64,256]{3,2,1,0:T(8,128)(2,1)S(1)} collective-permute-done((bf16[1,4,64,256]{3,2,1,0:T(8,128)(2,1)}, bf16[1,4,64,256]{3,2,1,0:T(8,128)(2,1)S(1)}, u32[]{:S(2)}, u32[]{:S(2)}) %collective-permute-start.10) | collective-permute-done | bytes 131104 | tf_op jit(solution)/shard_map/ppermute | solution.py:282
  11.4 1.5 %collective-permute-start.15 = (bf16[1,4,64,256]{3,2,1,0:T(8,128)(2,1)}, bf16[1,4,64,256]{3,2,1,0:T(8,128)(2,1)S(1)}, u32[]{:S(2)}, u32[]{:S(2)}) collective-permute-start(bf16[1,4,64,256]{3,2,1,0:T(8,128)(2,1)} %refs_0_.1), channel_id=1, source_target_pairs={{0,4},{2,6},{4,0},{6,2},{8,12},{10,14},{12,8},{14,10},{16,20},{18,... | collective-permute-start | bytes 393224 | tf_op jit(solution)/shard_map/ppermute | solution.py:282
  12.9 0.6 collective-permute-done.8.refs_0_
  13.5 5.7 %collective-permute-done.9.refs_1_ = bf16[1,4,64,256]{3,2,1,0:T(8,128)(2,1)S(1)} collective-permute-done((bf16[1,4,64,256]{3,2,1,0:T(8,128)(2,1)}, bf16[1,4,64,256]{3,2,1,0:T(8,128)(2,1)S(1)}, u32[]{:S(2)}, u32[]{:S(2)}) %collective-permute-start.9) | collective-permute-done | bytes 131104 | tf_op jit(solution)/shard_map/ppermute | solution.py:282
  19.2 1.5 %collective-permute-start.1 = (bf16[1,4,64,256]{3,2,1,0:T(8,128)(2,1)S(1)}, bf16[1,4,64,256]{3,2,1,0:T(8,128)(2,1)S(1)}, u32[]{:S(2)}, u32[]{:S(2)}) collective-permute-start(bf16[1,4,64,256]{3,2,1,0:T(8,128)(2,1)S(1)} %collective-permute-done.refs_1_), channel_id=1, source_target_pairs={{0,4},{2,6},{4,0},{6,2},{8,12},{10,14},{12,8},{14,10},{16,20},{18,... | collective-permute-start | bytes 393224 | tf_op jit(solution)/shard_map/ppermute | solution.py:282
  20.7 0.6 collective-permute-start.11
  21.3 0.5 collective-permute-start.12
  21.9 3.7 %collective-permute-done.1.refs_3_ = bf16[1,4,64,256]{3,2,1,0:T(8,128)(2,1)S(1)} collective-permute-done((bf16[1,4,64,256]{3,2,1,0:T(8,128)(2,1)S(1)}, bf16[1,4,64,256]{3,2,1,0:T(8,128)(2,1)S(1)}, u32[]{:S(2)}, u32[]{:S(2)}) %collective-permute-start.1) | collective-permute-done | bytes 131104 | tf_op jit(solution)/shard_map/ppermute | solution.py:282
  25.6 2.3 %collective-permute-start.3 = (bf16[1,4,64,256]{3,2,1,0:T(8,128)(2,1)S(1)}, bf16[1,4,64,256]{3,2,1,0:T(8,128)(2,1)S(1)}, u32[]{:S(2)}, u32[]{:S(2)}) collective-permute-start(bf16[1,4,64,256]{3,2,1,0:T(8,128)(2,1)S(1)} %collective-permute-done.1.refs_3_), channel_id=1, source_target_pairs={{0,16},{2,18},{4,20},{6,22},{8,24},{10,26},{12,28},{14,30},{16,0},... | collective-permute-start | bytes 393224 | tf_op jit(solution)/shard_map/ppermute | solution.py:282
  27.8 4.5 %collective-permute-done.2.refs_0_ = bf16[1,4,64,256]{3,2,1,0:T(8,128)(2,1)S(1)} collective-permute-done((bf16[1,4,64,256]{3,2,1,0:T(8,128)(2,1)S(1)}, bf16[1,4,64,256]{3,2,1,0:T(8,128)(2,1)S(1)}, u32[]{:S(2)}, u32[]{:S(2)}) %collective-permute-start.2) | collective-permute-done | bytes 131104 | tf_op jit(solution)/shard_map/ppermute | solution.py:282
  32.3 1.0 %collective-permute-start.4 = (bf16[1,4,64,256]{3,2,1,0:T(8,128)(2,1)S(1)}, bf16[1,4,64,256]{3,2,1,0:T(8,128)(2,1)S(1)}, u32[]{:S(2)}, u32[]{:S(2)}) collective-permute-start(bf16[1,4,64,256]{3,2,1,0:T(8,128)(2,1)S(1)} %collective-permute-done.1.refs_3_), channel_id=1, source_target_pairs={{0,24},{2,26},{4,28},{6,30},{8,16},{10,18},{12,20},{14,22},{16,8},... | collective-permute-start | bytes 393224 | tf_op jit(solution)/shard_map/ppermute | solution.py:282
  33.3 2.0 %collective-permute-done.3.refs_1_ = bf16[1,4,64,256]{3,2,1,0:T(8,128)(2,1)S(1)} collective-permute-done((bf16[1,4,64,256]{3,2,1,0:T(8,128)(2,1)S(1)}, bf16[1,4,64,256]{3,2,1,0:T(8,128)(2,1)S(1)}, u32[]{:S(2)}, u32[]{:S(2)}) %collective-permute-start.3) | collective-permute-done | bytes 131104 | tf_op jit(solution)/shard_map/ppermute | solution.py:282
  35.3 3.8 %collective-permute-done.4.refs_2_ = bf16[1,4,64,256]{3,2,1,0:T(8,128)(2,1)S(1)} collective-permute-done((bf16[1,4,64,256]{3,2,1,0:T(8,128)(2,1)S(1)}, bf16[1,4,64,256]{3,2,1,0:T(8,128)(2,1)S(1)}, u32[]{:S(2)}, u32[]{:S(2)}) %collective-permute-start.4) | collective-permute-done | bytes 131104 | tf_op jit(solution)/shard_map/ppermute | solution.py:282
  39.1 0.5 collective-permute-start.13
  39.7 0.7 collective-permute-done.18.refs_7_
  40.6 0.4 collective-permute-start.19
  40.9 1.1 %shard_map.56 = (bf16[6,4,256,128]{3,2,1,0:T(8,128)(2,1)S(1)}, f32[8,64,256]{2,1,0:T(8,128)S(1)}, bf16[512,256]{1,0:T(8,128)(2,1)S(1)}, bf16[256,512]{1,0:T(8,128)(2,1)S(1)}) custom-call(bf16[6,4,64,256]{3,2,1,0:T(8,128)(2,1)S(1)} %get-tuple-element.18.own_reflect, bf16[6,4,64,256]{3,2,1,0:T(8,128)(2,1)S(1)} %collective-permute-done.6.far_reflect, ...), custom_call_target="tpu_custom_call" | custom-call | flops 10000000 | bytes 6291456 | tf_op jit(solution)/shard_map/pallas_call | solution.py:322
  42.1 0.3 collective-permute-done.19.refs_8_
  42.4 4.8 %shard_map.58.refs_8_ = f32[8,8,64,256]{3,2,1,0:T(8,128)S(1)} custom-call(s32[8]{0:T(128)S(1)} %copy-done.1, s32[12]{0:T(128)S(1)} %copy-done.2, bf16[1,4,64,256]{3,2,1,0:T(8,128)(2,1)S(1)} %copy-done, bf16[1,4,64,256]{3,2,1,0:T(8,128)(2,1)S(1)} %collective-permute-done.refs_1_, bf16[1,4,64,256]{3,2,1,0:T(8,128)(2,1)S(1)} %collective-permute-done.15.refs_2_, ...), custom_call_target="tpu_custom_call" | custom-call | flops 1000000000 | bytes 10485760 | tf_op jit(solution)/shard_map/pallas_call | solution.py:387
  47.1 1.8 %shard_map.59.refs_6_ = f32[8,8,64,256]{3,2,1,0:T(8,128)S(1)} custom-call(s32[8]{0:T(128)S(1)} %copy-done.1, s32[12]{0:T(128)S(1)} %copy-done.2, bf16[3,4,64,256]{3,2,1,0:T(8,128)(2,1)S(1)} %collective-permute-done.11.refs_0_, bf16[3,4,64,256]{3,2,1,0:T(8,128)(2,1)S(1)} %collective-permute-done.12.refs_1_, ...), custom_call_target="tpu_custom_call", output_to_operand_aliasing={{}: (10, {})} | custom-call | flops 1000000000 | bytes 10485760 | tf_op jit(solution)/shard_map/pallas_call | solution.py:387
  49.0 5.6 %shard_map.60 = (f32[4,64,256]{2,1,0:T(8,128)S(1)}, f32[4,64,256]{2,1,0:T(8,128)S(1)}, f32[8,8,64,256]{3,2,1,0:T(8,128)S(1)}) custom-call(s32[8]{0:T(128)S(1)} %copy-done.1, s32[12]{0:T(128)S(1)} %copy-done.2, bf16[3,4,64,256]{3,2,1,0:T(8,128)(2,1)S(1)} %shard_map.55.refs_0_, ...), custom_call_target="tpu_custom_call", output_to_operand_aliasing={{2}: (8, {})} | custom-call | flops 1000000000 | bytes 10485760 | tf_op jit(solution)/shard_map/pallas_call | solution.py:387
  54.6 0.6 collective-permute-start.21
  55.2 1.2 %collective-permute-done.21 = f32[4,64,256]{2,1,0:T(8,128)S(1)} collective-permute-done((f32[4,64,256]{2,1,0:T(8,128)S(1)}, f32[4,64,256]{2,1,0:T(8,128)S(1)}, u32[]{:S(2)}, u32[]{:S(2)}) %collective-permute-start.21) | collective-permute-done | bytes 262176 | tf_op jit(solution)/shard_map/ppermute | solution.py:277
  56.4 14.3 %all_to_all.10 = f32[16,16,256]{2,1,0:T(8,128)S(1)} all-to-all(f32[16,16,256]{2,1,0:T(8,128)S(1)} %bitcast.2), channel_id=1, replica_groups=mesh['off'=16,'dep'=2] {'off'}, dimensions={0} | all-to-all | bytes 524288 | tf_op jit(solution)/shard_map/all_to_all | solution.py:409
  70.8 12.8 %all_to_all.11 = f32[16,16,256]{2,1,0:T(8,128)S(1)} all-to-all(f32[16,16,256]{2,1,0:T(8,128)S(1)} %broadcast_in_dim.2), channel_id=1, replica_groups=mesh['off'=16,'dep'=2] {'off'}, dimensions={0} | all-to-all | bytes 524288 | tf_op jit(solution)/shard_map/all_to_all | solution.py:411
  83.5 0.7 copy.11
  (32 shorter events, 0.5 us)
Async XLA Ops:
  0.0 42.3 %copy-start = (bf16[1,4,64,256]{3,2,1,0:T(8,128)(2,1)S(1)}, bf16[1,4,64,256]{3,2,1,0:T(8,128)(2,1)}, u32[]{:S(2)}) copy-start(bf16[1,4,64,256]{3,2,1,0:T(8,128)(2,1)} %refs_0_.1) | copy-start | bytes 393220
  0.0 42.3 %copy-start.2 = (s32[12]{0:T(128)S(1)}, s32[12]{0:T(128)}, u32[]{:S(2)}) copy-start(s32[12]{0:T(128)} %lags_ref.5) | copy-start | bytes 148
  0.0 42.3 %copy-start.1 = (s32[8]{0:T(128)S(1)}, s32[8]{0:T(128)}, u32[]{:S(2)}) copy-start(s32[8]{0:T(128)} %owners_ref.5) | copy-start | bytes 100
  0.0 9.8 %collective-permute-start = (bf16[1,4,64,256]{3,2,1,0:T(8,128)(2,1)}, bf16[1,4,64,256]{3,2,1,0:T(8,128)(2,1)S(1)}, u32[]{:S(2)}, u32[]{:S(2)}) collective-permute-start(bf16[1,4,64,256]{3,2,1,0:T(8,128)(2,1)} %refs_0_.1), channel_id=1, source_target_pairs={{0,2},{2,0},{4,6},{6,4},{8,10},{10,8},{12,14},{14,12},{16,18},{18,... | collective-permute-start | bytes 393224 | tf_op jit(solution)/shard_map/ppermute | solution.py:282
  3.0 8.4 %collective-permute-start.10 = (bf16[1,4,64,256]{3,2,1,0:T(8,128)(2,1)}, bf16[1,4,64,256]{3,2,1,0:T(8,128)(2,1)S(1)}, u32[]{:S(2)}, u32[]{:S(2)}) collective-permute-start(bf16[1,4,64,256]{3,2,1,0:T(8,128)(2,1)} %refs_0_.1), channel_id=1, source_target_pairs={{0,24},{2,26},{4,28},{6,30},{8,16},{10,18},{12,20},{14,22},{16,8},... | collective-permute-start | bytes 393224 | tf_op jit(solution)/shard_map/ppermute | solution.py:282
  6.6 6.9 %collective-permute-start.8 = (bf16[1,4,64,256]{3,2,1,0:T(8,128)(2,1)}, bf16[1,4,64,256]{3,2,1,0:T(8,128)(2,1)S(1)}, u32[]{:S(2)}, u32[]{:S(2)}) collective-permute-start(bf16[1,4,64,256]{3,2,1,0:T(8,128)(2,1)} %refs_0_.1), channel_id=1, source_target_pairs={{0,8},{2,10},{4,12},{6,14},{8,0},{10,2},{12,4},{14,6},{16,24},{18,... | collective-permute-start | bytes 393224 | tf_op jit(solution)/shard_map/ppermute | solution.py:282
  7.6 14.2 %collective-permute-start.7 = (f32[4,64,256]{2,1,0:T(8,128)S(1)}, f32[4,64,256]{2,1,0:T(8,128)S(1)}, u32[]{:S(2)}, u32[]{:S(2)}) collective-permute-start(f32[4,64,256]{2,1,0:T(8,128)S(1)} %broadcast_multiply_fusion.own_courant), channel_id=1, source_target_pairs={{0,1},{1,0},{2,3},{3,2},{4,5},{5,4},{6,7},{7,6},{8,9},{9,8},{10,11... | collective-permute-start | bytes 786440 | tf_op jit(solution)/shard_map/ppermute | solution.py:277
  9.2 31.4 %collective-permute-start.6 = (bf16[6,4,64,256]{3,2,1,0:T(8,128)(2,1)S(1)}, bf16[6,4,64,256]{3,2,1,0:T(8,128)(2,1)S(1)}, u32[]{:S(2)}, u32[]{:S(2)}) collective-permute-start(bf16[6,4,64,256]{3,2,1,0:T(8,128)(2,1)S(1)} %get-tuple-element.17), channel_id=1, source_target_pairs={{0,1},{1,0},{2,3},{3,2},{4,5},{5,4},{6,7},{7,6},{8,9},{9,8},{10,11... | collective-permute-start | bytes 2359304 | tf_op jit(solution)/shard_map/ppermute | solution.py:277
  9.8 9.4 %collective-permute-start.9 = (bf16[1,4,64,256]{3,2,1,0:T(8,128)(2,1)}, bf16[1,4,64,256]{3,2,1,0:T(8,128)(2,1)S(1)}, u32[]{:S(2)}, u32[]{:S(2)}) collective-permute-start(bf16[1,4,64,256]{3,2,1,0:T(8,128)(2,1)} %refs_0_.1), channel_id=1, source_target_pairs={{0,16},{2,18},{4,20},{6,22},{8,24},{10,26},{12,28},{14,30},{16,0},... | collective-permute-start | bytes 393224 | tf_op jit(solution)/shard_map/ppermute | solution.py:282
  11.4 9.3 %collective-permute-start.15 = (bf16[1,4,64,256]{3,2,1,0:T(8,128)(2,1)}, bf16[1,4,64,256]{3,2,1,0:T(8,128)(2,1)S(1)}, u32[]{:S(2)}, u32[]{:S(2)}) collective-permute-start(bf16[1,4,64,256]{3,2,1,0:T(8,128)(2,1)} %refs_0_.1), channel_id=1, source_target_pairs={{0,4},{2,6},{4,0},{6,2},{8,12},{10,14},{12,8},{14,10},{16,20},{18,... | collective-permute-start | bytes 393224 | tf_op jit(solution)/shard_map/ppermute | solution.py:282
  13.5 7.8 %collective-permute-start.16 = (bf16[1,4,64,256]{3,2,1,0:T(8,128)(2,1)}, bf16[1,4,64,256]{3,2,1,0:T(8,128)(2,1)S(1)}, u32[]{:S(2)}, u32[]{:S(2)}) collective-permute-start(bf16[1,4,64,256]{3,2,1,0:T(8,128)(2,1)} %refs_0_.1), channel_id=1, source_target_pairs={{0,1},{1,0},{2,3},{3,2},{4,5},{5,4},{6,7},{7,6},{8,9},{9,8},{10,11... | collective-permute-start | bytes 393224 | tf_op jit(solution)/shard_map/ppermute | solution.py:277
  19.2 6.4 %collective-permute-start.1 = (bf16[1,4,64,256]{3,2,1,0:T(8,128)(2,1)S(1)}, bf16[1,4,64,256]{3,2,1,0:T(8,128)(2,1)S(1)}, u32[]{:S(2)}, u32[]{:S(2)}) collective-permute-start(bf16[1,4,64,256]{3,2,1,0:T(8,128)(2,1)S(1)} %collective-permute-done.refs_1_), channel_id=1, source_target_pairs={{0,4},{2,6},{4,0},{6,2},{8,12},{10,14},{12,8},{14,10},{16,20},{18,... | collective-permute-start | bytes 393224 | tf_op jit(solution)/shard_map/ppermute | solution.py:282
  20.7 18.3 %collective-permute-start.11 = (bf16[3,4,64,256]{3,2,1,0:T(8,128)(2,1)S(1)}, bf16[3,4,64,256]{3,2,1,0:T(8,128)(2,1)S(1)}, u32[]{:S(2)}, u32[]{:S(2)}) collective-permute-start(bf16[3,4,64,256]{3,2,1,0:T(8,128)(2,1)S(1)} %shard_map.57.refs_4_), channel_id=1, source_target_pairs={{0,2},{2,0},{4,6},{6,4},{8,10},{10,8},{12,14},{14,12},{16,18},{18,... | collective-permute-start | bytes 1179656 | tf_op jit(solution)/shard_map/ppermute | solution.py:282
  21.3 18.2 %collective-permute-start.12 = (bf16[3,4,64,256]{3,2,1,0:T(8,128)(2,1)S(1)}, bf16[3,4,64,256]{3,2,1,0:T(8,128)(2,1)S(1)}, u32[]{:S(2)}, u32[]{:S(2)}) collective-permute-start(bf16[3,4,64,256]{3,2,1,0:T(8,128)(2,1)S(1)} %shard_map.57.refs_4_), channel_id=1, source_target_pairs={{0,4},{2,6},{4,0},{6,2},{8,12},{10,14},{12,8},{14,10},{16,20},{18,... | collective-permute-start | bytes 1179656 | tf_op jit(solution)/shard_map/ppermute | solution.py:282
  21.9 3.7 %collective-permute-start.17 = (bf16[1,4,64,256]{3,2,1,0:T(8,128)(2,1)S(1)}, bf16[1,4,64,256]{3,2,1,0:T(8,128)(2,1)S(1)}, u32[]{:S(2)}, u32[]{:S(2)}) collective-permute-start(bf16[1,4,64,256]{3,2,1,0:T(8,128)(2,1)S(1)} %collective-permute-done.refs_1_), channel_id=1, source_target_pairs={{0,1},{1,0},{2,3},{3,2},{4,5},{5,4},{6,7},{7,6},{8,9},{9,8},{10,11... | collective-permute-start | bytes 393224 | tf_op jit(solution)/shard_map/ppermute | solution.py:277
  25.6 6.8 %collective-permute-start.2 = (bf16[1,4,64,256]{3,2,1,0:T(8,128)(2,1)S(1)}, bf16[1,4,64,256]{3,2,1,0:T(8,128)(2,1)S(1)}, u32[]{:S(2)}, u32[]{:S(2)}) collective-permute-start(bf16[1,4,64,256]{3,2,1,0:T(8,128)(2,1)S(1)} %collective-permute-done.1.refs_3_), channel_id=1, source_target_pairs={{0,8},{2,10},{4,12},{6,14},{8,0},{10,2},{12,4},{14,6},{16,24},{18,... | collective-permute-start | bytes 393224 | tf_op jit(solution)/shard_map/ppermute | solution.py:282
  25.6 9.7 %collective-permute-start.3 = (bf16[1,4,64,256]{3,2,1,0:T(8,128)(2,1)S(1)}, bf16[1,4,64,256]{3,2,1,0:T(8,128)(2,1)S(1)}, u32[]{:S(2)}, u32[]{:S(2)}) collective-permute-start(bf16[1,4,64,256]{3,2,1,0:T(8,128)(2,1)S(1)} %collective-permute-done.1.refs_3_), channel_id=1, source_target_pairs={{0,16},{2,18},{4,20},{6,22},{8,24},{10,26},{12,28},{14,30},{16,0},... | collective-permute-start | bytes 393224 | tf_op jit(solution)/shard_map/ppermute | solution.py:282
  32.3 6.8 %collective-permute-start.4 = (bf16[1,4,64,256]{3,2,1,0:T(8,128)(2,1)S(1)}, bf16[1,4,64,256]{3,2,1,0:T(8,128)(2,1)S(1)}, u32[]{:S(2)}, u32[]{:S(2)}) collective-permute-start(bf16[1,4,64,256]{3,2,1,0:T(8,128)(2,1)S(1)} %collective-permute-done.1.refs_3_), channel_id=1, source_target_pairs={{0,24},{2,26},{4,28},{6,30},{8,16},{10,18},{12,20},{14,22},{16,8},... | collective-permute-start | bytes 393224 | tf_op jit(solution)/shard_map/ppermute | solution.py:282
  35.3 7.1 %collective-permute-start.20 = (bf16[3,4,64,256]{3,2,1,0:T(8,128)(2,1)S(1)}, bf16[3,4,64,256]{3,2,1,0:T(8,128)(2,1)S(1)}, u32[]{:S(2)}, u32[]{:S(2)}) collective-permute-start(bf16[3,4,64,256]{3,2,1,0:T(8,128)(2,1)S(1)} %shard_map.57.refs_4_), channel_id=1, source_target_pairs={{0,1},{1,0},{2,3},{3,2},{4,5},{5,4},{6,7},{7,6},{8,9},{9,8},{10,11... | collective-permute-start | bytes 1179656 | tf_op jit(solution)/shard_map/ppermute | solution.py:277
  39.1 1.3 %collective-permute-start.18 = (bf16[1,4,64,256]{3,2,1,0:T(8,128)(2,1)S(1)}, bf16[1,4,64,256]{3,2,1,0:T(8,128)(2,1)S(1)}, u32[]{:S(2)}, u32[]{:S(2)}) collective-permute-start(bf16[1,4,64,256]{3,2,1,0:T(8,128)(2,1)S(1)} %collective-permute-done.15.refs_2_), channel_id=1, source_target_pairs={{0,1},{1,0},{2,3},{3,2},{4,5},{5,4},{6,7},{7,6},{8,9},{9,8},{10,11... | collective-permute-start | bytes 393224 | tf_op jit(solution)/shard_map/ppermute | solution.py:277
  39.1 8.0 %collective-permute-start.13 = (bf16[3,4,64,256]{3,2,1,0:T(8,128)(2,1)S(1)}, bf16[3,4,64,256]{3,2,1,0:T(8,128)(2,1)S(1)}, u32[]{:S(2)}, u32[]{:S(2)}) collective-permute-start(bf16[3,4,64,256]{3,2,1,0:T(8,128)(2,1)S(1)} %collective-permute-done.11.refs_0_), channel_id=1, source_target_pairs={{0,1},{1,0},{2,3},{3,2},{4,5},{5,4},{6,7},{7,6},{8,9},{9,8},{10,11... | collective-permute-start | bytes 1179656 | tf_op jit(solution)/shard_map/ppermute | solution.py:277
  39.6 7.5 %collective-permute-start.14 = (bf16[3,4,64,256]{3,2,1,0:T(8,128)(2,1)S(1)}, bf16[3,4,64,256]{3,2,1,0:T(8,128)(2,1)S(1)}, u32[]{:S(2)}, u32[]{:S(2)}) collective-permute-start(bf16[3,4,64,256]{3,2,1,0:T(8,128)(2,1)S(1)} %collective-permute-done.12.refs_1_), channel_id=1, source_target_pairs={{0,1},{1,0},{2,3},{3,2},{4,5},{5,4},{6,7},{7,6},{8,9},{9,8},{10,11... | collective-permute-start | bytes 1179656 | tf_op jit(solution)/shard_map/ppermute | solution.py:277
  40.4 8.5 %collective-permute-start.5 = (bf16[3,4,64,256]{3,2,1,0:T(8,128)(2,1)S(1)}, bf16[3,4,64,256]{3,2,1,0:T(8,128)(2,1)S(1)}, u32[]{:S(2)}, u32[]{:S(2)}) collective-permute-start(bf16[3,4,64,256]{3,2,1,0:T(8,128)(2,1)S(1)} %shard_map.55.refs_0_), channel_id=1, source_target_pairs={{0,1},{1,0},{2,3},{3,2},{4,5},{5,4},{6,7},{7,6},{8,9},{9,8},{10,11... | collective-permute-start | bytes 1179656 | tf_op jit(solution)/shard_map/ppermute | solution.py:277
  40.6 1.8 %collective-permute-start.19 = (bf16[1,4,64,256]{3,2,1,0:T(8,128)(2,1)S(1)}, bf16[1,4,64,256]{3,2,1,0:T(8,128)(2,1)S(1)}, u32[]{:S(2)}, u32[]{:S(2)}) collective-permute-start(bf16[1,4,64,256]{3,2,1,0:T(8,128)(2,1)S(1)} %collective-permute-done.1.refs_3_), channel_id=1, source_target_pairs={{0,1},{1,0},{2,3},{3,2},{4,5},{5,4},{6,7},{7,6},{8,9},{9,8},{10,11... | collective-permute-start | bytes 393224 | tf_op jit(solution)/shard_map/ppermute | solution.py:277
  54.6 1.8 %collective-permute-start.21 = (f32[4,64,256]{2,1,0:T(8,128)S(1)}, f32[4,64,256]{2,1,0:T(8,128)S(1)}, u32[]{:S(2)}, u32[]{:S(2)}) collective-permute-start(f32[4,64,256]{2,1,0:T(8,128)S(1)} %get-tuple-element.16), channel_id=1, source_target_pairs={{0,1},{1,0},{2,3},{3,2},{4,5},{5,4},{6,7},{7,6},{8,9},{9,8},{10,11... | collective-permute-start | bytes 786440 | tf_op jit(solution)/shard_map/ppermute | solution.py:277

commit v7 on v6

--- a/solution.py
+++ b/solution.py
@@ -333,7 +333,6 @@
     z_all = join(*z_parts)
     z_x, z_y = flip(z_all, 1), flip(z_all, 2)
     d_parts = [flip(o_d, wing * j) for j in range(1, lines)]
-    d_all = join(*d_parts)
 
     scratch = [
         pltpu.VMEM((depth, rows, columns), F32),
@@ -363,7 +362,7 @@
     def far_banks(owns, fars):
         def choose(apart):
             low, line = apart % wing, apart // wing
-            return [((low == 3) & (line > 0), line - 1, owns[0], fars[0])]
+            return [((low == 3) & (line == 1 + i), 0, owns[i], fars[i]) for i in range(lines - 1)]
 
         return choose
 
@@ -398,7 +397,7 @@
     out_half = jax.ShapeDtypeStruct((half, rows, columns), F32)
     near = both_halves([snapshots, o_x, o_y, o_d, z_all])
     side = both_halves([z_x, z_y])
-    far = both_halves([d_all])
+    far = both_halves(d_parts)
     sums = run(sums_kernel, [(near, near_banks, 0, ITERS)], [], [sums_shape])
     sums = run(sums_kernel, [(side, side_banks, 0, ITERS)], sums, [sums_shape])
     groups = [(far, far_banks, 0, ITERS)]

time: 84.5 us -> 98 us (1.16)
  waiting for transfers between devices: 23.2 us -> 30.8 us
  starting transfers between devices: 17.2 us -> 20.9 us
  blocking collectives: 27.1 us -> 29.2 us
    ppermute x11, waiting for transfers between devices: 21 us -> 28.8 us  [flip(): return lax.ppermute(x, 'off', [(i, i ^ bits) for i in range(count)])]
    ppermute x11, starting transfers between devices: 14.9 us -> 17.7 us  [flip(): return lax.ppermute(x, 'off', [(i, i ^ bits) for i in range(count)])]
    all_to_all x1, blocking collectives: 14.3 us -> 16.5 us  [core_pair(): summed = lax.all_to_all(pieces, 'off', 0, 0).sum(0)]
    ppermute x11 -> x13, starting transfers between devices: 2.33 us -> 3.17 us  [swapped(): return lax.ppermute(x, 'dep', [(0, 1), (1, 0)])]
    ppermute x11 -> x13, waiting for transfers between devices: 2.17 us -> 2.02 us  [swapped(): return lax.ppermute(x, 'dep', [(0, 1), (1, 0)])]
  transfers between devices with their start and end apart: 22 -> 24, of which waited for: 10 -> 6; matrix products, arithmetic and copies ran while one was open for 3% -> 3% of each run, Pallas kernels for 9% -> 8%
where the time goes in v7:
time: 98 us; the launch traced here: 97.7 us
  waiting for transfers between devices  30.8 us (31%)
  blocking collectives  29.2 us (30%)
  starting transfers between devices  20.9 us (21%)
  Pallas kernels  13.4 us (14%)
  local copies, waits for them, and re-layouts  2.27 us (2%)
  other arithmetic  1.04 us (1%)
    ppermute x11, waiting for transfers between devices, flip(): return lax.ppermute(x, 'off', [(i, i ^ bits) for i in range(count)])  28.8 us
    ppermute x11, starting transfers between devices, flip(): return lax.ppermute(x, 'off', [(i, i ^ bits) for i in range(count)])  17.7 us
    all_to_all x1, blocking collectives, core_pair(): summed = lax.all_to_all(pieces, 'off', 0, 0).sum(0)  16.5 us
    all_to_all x1, blocking collectives, core_pair(): return lax.all_to_all(spread, 'off', 0, 0).reshape(half, rows, columns)  12.8 us
    pallas_call x3, Pallas kernels, run(): pl.pallas_call(kernel, in_specs=[smem] * 2 + [vmem] * (n + 4 + len(extra)...  12.2 us
    ppermute x13, starting transfers between devices, swapped(): return lax.ppermute(x, 'dep', [(0, 1), (1, 0)])  3.17 us
    ppermute x13, waiting for transfers between devices, swapped(): return lax.ppermute(x, 'dep', [(0, 1), (1, 0)])  2.02 us
  transfers between devices with their start and end apart: 24, of which 6 were waited for; matrix products, arithmetic and copies ran while one was open for 3% of the time, Pallas kernels for 8%

profile of v7, /device:TPU:0, one launch (start us, length us, event | category | flops | bytes accessed | tf_op | source)
XLA Modules:
  0.0 97.7 jit_solution(14483402523253113302)
XLA Ops:
  0.0 3.0 %collective-permute-start = (bf16[1,4,64,256]{3,2,1,0:T(8,128)(2,1)}, bf16[1,4,64,256]{3,2,1,0:T(8,128)(2,1)S(1)}, u32[]{:S(2)}, u32[]{:S(2)}) collective-permute-start(bf16[1,4,64,256]{3,2,1,0:T(8,128)(2,1)} %refs_0_.1), channel_id=1, source_target_pairs={{0,2},{2,0},{4,6},{6,4},{8,10},{10,8},{12,14},{14,12},{16,18},{18,... | collective-permute-start | bytes 393224 | tf_op jit(solution)/shard_map/ppermute | solution.py:282
  3.0 1.6 %collective-permute-start.10 = (bf16[1,4,64,256]{3,2,1,0:T(8,128)(2,1)}, bf16[1,4,64,256]{3,2,1,0:T(8,128)(2,1)S(1)}, u32[]{:S(2)}, u32[]{:S(2)}) collective-permute-start(bf16[1,4,64,256]{3,2,1,0:T(8,128)(2,1)} %refs_0_.1), channel_id=1, source_target_pairs={{0,8},{2,10},{4,12},{6,14},{8,0},{10,2},{12,4},{14,6},{16,24},{18,... | collective-permute-start | bytes 393224 | tf_op jit(solution)/shard_map/ppermute | solution.py:282
  4.6 2.6 %collective-permute-start.11 = (bf16[1,4,64,256]{3,2,1,0:T(8,128)(2,1)}, bf16[1,4,64,256]{3,2,1,0:T(8,128)(2,1)S(1)}, u32[]{:S(2)}, u32[]{:S(2)}) collective-permute-start(bf16[1,4,64,256]{3,2,1,0:T(8,128)(2,1)} %refs_0_.1), channel_id=1, source_target_pairs={{0,16},{2,18},{4,20},{6,22},{8,24},{10,26},{12,28},{14,30},{16,0},... | collective-permute-start | bytes 393224 | tf_op jit(solution)/shard_map/ppermute | solution.py:282
  7.2 0.2 collective-permute-start.12
  7.4 1.5 %collective-permute-start.17 = (bf16[1,4,64,256]{3,2,1,0:T(8,128)(2,1)}, bf16[1,4,64,256]{3,2,1,0:T(8,128)(2,1)S(1)}, u32[]{:S(2)}, u32[]{:S(2)}) collective-permute-start(bf16[1,4,64,256]{3,2,1,0:T(8,128)(2,1)} %refs_0_.1), channel_id=1, source_target_pairs={{0,4},{2,6},{4,0},{6,2},{8,12},{10,14},{12,8},{14,10},{16,20},{18,... | collective-permute-start | bytes 393224 | tf_op jit(solution)/shard_map/ppermute | solution.py:282
  9.0 1.5 %constant_dynamic-slice_fusion = (bf16[6,4,64,256]{3,2,1,0:T(8,128)(2,1)S(1)}, bf16[6,4,64,256]{3,2,1,0:T(8,128)(2,1)S(1)}) fusion(bf16[12,4,64,256]{3,2,1,0:T(8,128)(2,1)} %param.6, s32[]{:T(128)S(6)} %select_n.7, s32[]{:T(128)S(6)} %select_n.6), kind=kLoop, calls=%fused_computation.1 | loop fusion | bytes 3145736 | tf_op jit(solution)/shard_map/dynamic_slice | solution.py:299
  10.6 1.0 broadcast_multiply_fusion.own_courant
  11.6 5.9 %collective-permute-done.11.refs_1_ = bf16[1,4,64,256]{3,2,1,0:T(8,128)(2,1)S(1)} collective-permute-done((bf16[1,4,64,256]{3,2,1,0:T(8,128)(2,1)}, bf16[1,4,64,256]{3,2,1,0:T(8,128)(2,1)S(1)}, u32[]{:S(2)}, u32[]{:S(2)}) %collective-permute-start.11) | collective-permute-done | bytes 131104 | tf_op jit(solution)/shard_map/ppermute | solution.py:282
  17.5 0.5 collective-permute-start.18
  18.0 0.6 collective-permute-start.13
  18.6 1.5 %collective-permute-start.14 = (bf16[3,4,64,256]{3,2,1,0:T(8,128)(2,1)S(1)}, bf16[3,4,64,256]{3,2,1,0:T(8,128)(2,1)S(1)}, u32[]{:S(2)}, u32[]{:S(2)}) collective-permute-start(bf16[3,4,64,256]{3,2,1,0:T(8,128)(2,1)S(1)} %shard_map.56.refs_4_), channel_id=1, source_target_pairs={{0,4},{2,6},{4,0},{6,2},{8,12},{10,14},{12,8},{14,10},{16,20},{18,... | collective-permute-start | bytes 1179656 | tf_op jit(solution)/shard_map/ppermute | solution.py:282
  20.2 0.6 collective-permute-start.1
  20.8 11.4 %collective-permute-done.1.refs_3_ = bf16[1,4,64,256]{3,2,1,0:T(8,128)(2,1)S(1)} collective-permute-done((bf16[1,4,64,256]{3,2,1,0:T(8,128)(2,1)S(1)}, bf16[1,4,64,256]{3,2,1,0:T(8,128)(2,1)S(1)}, u32[]{:S(2)}, u32[]{:S(2)}) %collective-permute-start.1) | collective-permute-done | bytes 131104 | tf_op jit(solution)/shard_map/ppermute | solution.py:282
  32.2 0.5 collective-permute-start.21
  32.7 0.8 collective-permute-done.20.refs_7_
  33.7 0.4 collective-permute-start.15
  34.1 0.1 collective-permute-start.16
  34.2 2.0 %collective-permute-start.2 = (bf16[1,4,64,256]{3,2,1,0:T(8,128)(2,1)S(1)}, bf16[1,4,64,256]{3,2,1,0:T(8,128)(2,1)S(1)}, u32[]{:S(2)}, u32[]{:S(2)}) collective-permute-start(bf16[1,4,64,256]{3,2,1,0:T(8,128)(2,1)S(1)} %collective-permute-done.1.refs_3_), channel_id=1, source_target_pairs={{0,8},{2,10},{4,12},{6,14},{8,0},{10,2},{12,4},{14,6},{16,24},{18,... | collective-permute-start | bytes 393224 | tf_op jit(solution)/shard_map/ppermute | solution.py:282
  36.2 4.0 %collective-permute-done.2.refs_0_ = bf16[1,4,64,256]{3,2,1,0:T(8,128)(2,1)S(1)} collective-permute-done((bf16[1,4,64,256]{3,2,1,0:T(8,128)(2,1)S(1)}, bf16[1,4,64,256]{3,2,1,0:T(8,128)(2,1)S(1)}, u32[]{:S(2)}, u32[]{:S(2)}) %collective-permute-start.2) | collective-permute-done | bytes 131104 | tf_op jit(solution)/shard_map/ppermute | solution.py:282
  40.2 2.7 %collective-permute-start.3 = (bf16[1,4,64,256]{3,2,1,0:T(8,128)(2,1)S(1)}, bf16[1,4,64,256]{3,2,1,0:T(8,128)(2,1)S(1)}, u32[]{:S(2)}, u32[]{:S(2)}) collective-permute-start(bf16[1,4,64,256]{3,2,1,0:T(8,128)(2,1)S(1)} %collective-permute-done.1.refs_3_), channel_id=1, source_target_pairs={{0,16},{2,18},{4,20},{6,22},{8,24},{10,26},{12,28},{14,30},{16,0},... | collective-permute-start | bytes 393224 | tf_op jit(solution)/shard_map/ppermute | solution.py:282
  42.9 1.4 %collective-permute-start.4 = (bf16[1,4,64,256]{3,2,1,0:T(8,128)(2,1)S(1)}, bf16[1,4,64,256]{3,2,1,0:T(8,128)(2,1)S(1)}, u32[]{:S(2)}, u32[]{:S(2)}) collective-permute-start(bf16[1,4,64,256]{3,2,1,0:T(8,128)(2,1)S(1)} %collective-permute-done.1.refs_3_), channel_id=1, source_target_pairs={{0,24},{2,26},{4,28},{6,30},{8,16},{10,18},{12,20},{14,22},{16,8},... | collective-permute-start | bytes 393224 | tf_op jit(solution)/shard_map/ppermute | solution.py:282
  44.3 1.1 %shard_map.55 = (bf16[6,4,256,128]{3,2,1,0:T(8,128)(2,1)S(1)}, f32[8,64,256]{2,1,0:T(8,128)S(1)}, bf16[512,256]{1,0:T(8,128)(2,1)S(1)}, bf16[256,512]{1,0:T(8,128)(2,1)S(1)}) custom-call(bf16[6,4,64,256]{3,2,1,0:T(8,128)(2,1)S(1)} %get-tuple-element.18.own_reflect, bf16[6,4,64,256]{3,2,1,0:T(8,128)(2,1)S(1)} %collective-permute-done.8.far_reflect, ...), custom_call_target="tpu_custom_call" | custom-call | flops 10000000 | bytes 6291456 | tf_op jit(solution)/shard_map/pallas_call | solution.py:322
  45.5 7.4 %collective-permute-done.3.refs_1_ = bf16[1,4,64,256]{3,2,1,0:T(8,128)(2,1)S(1)} collective-permute-done((bf16[1,4,64,256]{3,2,1,0:T(8,128)(2,1)S(1)}, bf16[1,4,64,256]{3,2,1,0:T(8,128)(2,1)S(1)}, u32[]{:S(2)}, u32[]{:S(2)}) %collective-permute-start.3) | collective-permute-done | bytes 131104 | tf_op jit(solution)/shard_map/ppermute | solution.py:282
  52.9 0.5 collective-permute-start.6
  53.5 4.8 %shard_map.57.refs_8_ = f32[8,8,64,256]{3,2,1,0:T(8,128)S(1)} custom-call(s32[8]{0:T(128)S(1)} %copy-done.1, s32[12]{0:T(128)S(1)} %copy-done.2, bf16[1,4,64,256]{3,2,1,0:T(8,128)(2,1)S(1)} %copy-done, bf16[1,4,64,256]{3,2,1,0:T(8,128)(2,1)S(1)} %collective-permute-done.refs_1_, bf16[1,4,64,256]{3,2,1,0:T(8,128)(2,1)S(1)} %collective-permute-done.17.refs_2_, ...), custom_call_target="tpu_custom_call" | custom-call | flops 1000000000 | bytes 10485760 | tf_op jit(solution)/shard_map/pallas_call | solution.py:386
  58.3 1.8 %shard_map.58.refs_10_ = f32[8,8,64,256]{3,2,1,0:T(8,128)S(1)} custom-call(s32[8]{0:T(128)S(1)} %copy-done.1, s32[12]{0:T(128)S(1)} %copy-done.2, bf16[3,4,64,256]{3,2,1,0:T(8,128)(2,1)S(1)} %collective-permute-done.13.refs_0_, bf16[3,4,64,256]{3,2,1,0:T(8,128)(2,1)S(1)} %collective-permute-done.14.refs_1_, ...), custom_call_target="tpu_custom_call", output_to_operand_aliasing={{}: (10, {})} | custom-call | flops 1000000000 | bytes 10485760 | tf_op jit(solution)/shard_map/pallas_call | solution.py:386
  60.1 5.7 %shard_map.59 = (f32[4,64,256]{2,1,0:T(8,128)S(1)}, f32[4,64,256]{2,1,0:T(8,128)S(1)}, f32[8,8,64,256]{3,2,1,0:T(8,128)S(1)}) custom-call(s32[8]{0:T(128)S(1)} %copy-done.1, s32[12]{0:T(128)S(1)} %copy-done.2, bf16[1,4,64,256]{3,2,1,0:T(8,128)(2,1)S(1)} %collective-permute-done.2.refs_0_, ...), custom_call_target="tpu_custom_call", output_to_operand_aliasing={{2}: (12, {})} | custom-call | flops 1000000000 | bytes 10485760 | tf_op jit(solution)/shard_map/pallas_call | solution.py:386
  65.8 0.8 collective-permute-start.23
  66.6 1.2 %collective-permute-done.23 = f32[4,64,256]{2,1,0:T(8,128)S(1)} collective-permute-done((f32[4,64,256]{2,1,0:T(8,128)S(1)}, f32[4,64,256]{2,1,0:T(8,128)S(1)}, u32[]{:S(2)}, u32[]{:S(2)}) %collective-permute-start.23) | collective-permute-done | bytes 262176 | tf_op jit(solution)/shard_map/ppermute | solution.py:277
  67.8 16.5 %all_to_all.10 = f32[16,16,256]{2,1,0:T(8,128)S(1)} all-to-all(f32[16,16,256]{2,1,0:T(8,128)S(1)} %bitcast.2), channel_id=1, replica_groups=mesh['off'=16,'dep'=2] {'off'}, dimensions={0} | all-to-all | bytes 524288 | tf_op jit(solution)/shard_map/all_to_all | solution.py:408
  84.3 12.8 %all_to_all.11 = f32[16,16,256]{2,1,0:T(8,128)S(1)} all-to-all(f32[16,16,256]{2,1,0:T(8,128)S(1)} %broadcast_in_dim.2), channel_id=1, replica_groups=mesh['off'=16,'dep'=2] {'off'}, dimensions={0} | all-to-all | bytes 524288 | tf_op jit(solution)/shard_map/all_to_all | solution.py:410
  97.0 0.7 copy.11
  (35 shorter events, 0.5 us)
Async XLA Ops:
  0.0 53.5 %copy-start = (bf16[1,4,64,256]{3,2,1,0:T(8,128)(2,1)S(1)}, bf16[1,4,64,256]{3,2,1,0:T(8,128)(2,1)}, u32[]{:S(2)}) copy-start(bf16[1,4,64,256]{3,2,1,0:T(8,128)(2,1)} %refs_0_.1) | copy-start | bytes 393220
  0.0 53.5 %copy-start.2 = (s32[12]{0:T(128)S(1)}, s32[12]{0:T(128)}, u32[]{:S(2)}) copy-start(s32[12]{0:T(128)} %lags_ref.5) | copy-start | bytes 148
  0.0 53.5 %copy-start.1 = (s32[8]{0:T(128)S(1)}, s32[8]{0:T(128)}, u32[]{:S(2)}) copy-start(s32[8]{0:T(128)} %owners_ref.5) | copy-start | bytes 100
  0.0 18.0 %collective-permute-start = (bf16[1,4,64,256]{3,2,1,0:T(8,128)(2,1)}, bf16[1,4,64,256]{3,2,1,0:T(8,128)(2,1)S(1)}, u32[]{:S(2)}, u32[]{:S(2)}) collective-permute-start(bf16[1,4,64,256]{3,2,1,0:T(8,128)(2,1)} %refs_0_.1), channel_id=1, source_target_pairs={{0,2},{2,0},{4,6},{6,4},{8,10},{10,8},{12,14},{14,12},{16,18},{18,... | collective-permute-start | bytes 393224 | tf_op jit(solution)/shard_map/ppermute | solution.py:282
  3.0 7.5 %collective-permute-start.10 = (bf16[1,4,64,256]{3,2,1,0:T(8,128)(2,1)}, bf16[1,4,64,256]{3,2,1,0:T(8,128)(2,1)S(1)}, u32[]{:S(2)}, u32[]{:S(2)}) collective-permute-start(bf16[1,4,64,256]{3,2,1,0:T(8,128)(2,1)} %refs_0_.1), channel_id=1, source_target_pairs={{0,8},{2,10},{4,12},{6,14},{8,0},{10,2},{12,4},{14,6},{16,24},{18,... | collective-permute-start | bytes 393224 | tf_op jit(solution)/shard_map/ppermute | solution.py:282
  4.6 12.9 %collective-permute-start.11 = (bf16[1,4,64,256]{3,2,1,0:T(8,128)(2,1)}, bf16[1,4,64,256]{3,2,1,0:T(8,128)(2,1)S(1)}, u32[]{:S(2)}, u32[]{:S(2)}) collective-permute-start(bf16[1,4,64,256]{3,2,1,0:T(8,128)(2,1)} %refs_0_.1), channel_id=1, source_target_pairs={{0,16},{2,18},{4,20},{6,22},{8,24},{10,26},{12,28},{14,30},{16,0},... | collective-permute-start | bytes 393224 | tf_op jit(solution)/shard_map/ppermute | solution.py:282
  7.2 10.3 %collective-permute-start.12 = (bf16[1,4,64,256]{3,2,1,0:T(8,128)(2,1)}, bf16[1,4,64,256]{3,2,1,0:T(8,128)(2,1)S(1)}, u32[]{:S(2)}, u32[]{:S(2)}) collective-permute-start(bf16[1,4,64,256]{3,2,1,0:T(8,128)(2,1)} %refs_0_.1), channel_id=1, source_target_pairs={{0,24},{2,26},{4,28},{6,30},{8,16},{10,18},{12,20},{14,22},{16,8},... | collective-permute-start | bytes 393224 | tf_op jit(solution)/shard_map/ppermute | solution.py:282
  7.4 11.2 %collective-permute-start.17 = (bf16[1,4,64,256]{3,2,1,0:T(8,128)(2,1)}, bf16[1,4,64,256]{3,2,1,0:T(8,128)(2,1)S(1)}, u32[]{:S(2)}, u32[]{:S(2)}) collective-permute-start(bf16[1,4,64,256]{3,2,1,0:T(8,128)(2,1)} %refs_0_.1), channel_id=1, source_target_pairs={{0,4},{2,6},{4,0},{6,2},{8,12},{10,14},{12,8},{14,10},{16,20},{18,... | collective-permute-start | bytes 393224 | tf_op jit(solution)/shard_map/ppermute | solution.py:282
  10.5 32.4 %collective-permute-start.8 = (bf16[6,4,64,256]{3,2,1,0:T(8,128)(2,1)S(1)}, bf16[6,4,64,256]{3,2,1,0:T(8,128)(2,1)S(1)}, u32[]{:S(2)}, u32[]{:S(2)}) collective-permute-start(bf16[6,4,64,256]{3,2,1,0:T(8,128)(2,1)S(1)} %get-tuple-element.17), channel_id=1, source_target_pairs={{0,1},{1,0},{2,3},{3,2},{4,5},{5,4},{6,7},{7,6},{8,9},{9,8},{10,11... | collective-permute-start | bytes 2359304 | tf_op jit(solution)/shard_map/ppermute | solution.py:277
  17.5 3.2 %collective-permute-start.9 = (f32[4,64,256]{2,1,0:T(8,128)S(1)}, f32[4,64,256]{2,1,0:T(8,128)S(1)}, u32[]{:S(2)}, u32[]{:S(2)}) collective-permute-start(f32[4,64,256]{2,1,0:T(8,128)S(1)} %broadcast_multiply_fusion.own_courant), channel_id=1, source_target_pairs={{0,1},{1,0},{2,3},{3,2},{4,5},{5,4},{6,7},{7,6},{8,9},{9,8},{10,11... | collective-permute-start | bytes 786440 | tf_op jit(solution)/shard_map/ppermute | solution.py:277
  17.5 2.7 %collective-permute-start.18 = (bf16[1,4,64,256]{3,2,1,0:T(8,128)(2,1)}, bf16[1,4,64,256]{3,2,1,0:T(8,128)(2,1)S(1)}, u32[]{:S(2)}, u32[]{:S(2)}) collective-permute-start(bf16[1,4,64,256]{3,2,1,0:T(8,128)(2,1)} %refs_0_.1), channel_id=1, source_target_pairs={{0,1},{1,0},{2,3},{3,2},{4,5},{5,4},{6,7},{7,6},{8,9},{9,8},{10,11... | collective-permute-start | bytes 393224 | tf_op jit(solution)/shard_map/ppermute | solution.py:277
  18.0 15.7 %collective-permute-start.13 = (bf16[3,4,64,256]{3,2,1,0:T(8,128)(2,1)S(1)}, bf16[3,4,64,256]{3,2,1,0:T(8,128)(2,1)S(1)}, u32[]{:S(2)}, u32[]{:S(2)}) collective-permute-start(bf16[3,4,64,256]{3,2,1,0:T(8,128)(2,1)S(1)} %shard_map.56.refs_4_), channel_id=1, source_target_pairs={{0,2},{2,0},{4,6},{6,4},{8,10},{10,8},{12,14},{14,12},{16,18},{18,... | collective-permute-start | bytes 1179656 | tf_op jit(solution)/shard_map/ppermute | solution.py:282
  18.6 15.4 %collective-permute-start.14 = (bf16[3,4,64,256]{3,2,1,0:T(8,128)(2,1)S(1)}, bf16[3,4,64,256]{3,2,1,0:T(8,128)(2,1)S(1)}, u32[]{:S(2)}, u32[]{:S(2)}) collective-permute-start(bf16[3,4,64,256]{3,2,1,0:T(8,128)(2,1)S(1)} %shard_map.56.refs_4_), channel_id=1, source_target_pairs={{0,4},{2,6},{4,0},{6,2},{8,12},{10,14},{12,8},{14,10},{16,20},{18,... | collective-permute-start | bytes 1179656 | tf_op jit(solution)/shard_map/ppermute | solution.py:282
  20.2 12.0 %collective-permute-start.1 = (bf16[1,4,64,256]{3,2,1,0:T(8,128)(2,1)S(1)}, bf16[1,4,64,256]{3,2,1,0:T(8,128)(2,1)S(1)}, u32[]{:S(2)}, u32[]{:S(2)}) collective-permute-start(bf16[1,4,64,256]{3,2,1,0:T(8,128)(2,1)S(1)} %collective-permute-done.refs_1_), channel_id=1, source_target_pairs={{0,4},{2,6},{4,0},{6,2},{8,12},{10,14},{12,8},{14,10},{16,20},{18,... | collective-permute-start | bytes 393224 | tf_op jit(solution)/shard_map/ppermute | solution.py:282
  20.7 11.5 %collective-permute-start.19 = (bf16[1,4,64,256]{3,2,1,0:T(8,128)(2,1)S(1)}, bf16[1,4,64,256]{3,2,1,0:T(8,128)(2,1)S(1)}, u32[]{:S(2)}, u32[]{:S(2)}) collective-permute-start(bf16[1,4,64,256]{3,2,1,0:T(8,128)(2,1)S(1)} %collective-permute-done.refs_1_), channel_id=1, source_target_pairs={{0,1},{1,0},{2,3},{3,2},{4,5},{5,4},{6,7},{7,6},{8,9},{9,8},{10,11... | collective-permute-start | bytes 393224 | tf_op jit(solution)/shard_map/ppermute | solution.py:277
  32.2 1.3 %collective-permute-start.20 = (bf16[1,4,64,256]{3,2,1,0:T(8,128)(2,1)S(1)}, bf16[1,4,64,256]{3,2,1,0:T(8,128)(2,1)S(1)}, u32[]{:S(2)}, u32[]{:S(2)}) collective-permute-start(bf16[1,4,64,256]{3,2,1,0:T(8,128)(2,1)S(1)} %collective-permute-done.17.refs_2_), channel_id=1, source_target_pairs={{0,1},{1,0},{2,3},{3,2},{4,5},{5,4},{6,7},{7,6},{8,9},{9,8},{10,11... | collective-permute-start | bytes 393224 | tf_op jit(solution)/shard_map/ppermute | solution.py:277
  32.2 2.0 %collective-permute-start.21 = (bf16[1,4,64,256]{3,2,1,0:T(8,128)(2,1)S(1)}, bf16[1,4,64,256]{3,2,1,0:T(8,128)(2,1)S(1)}, u32[]{:S(2)}, u32[]{:S(2)}) collective-permute-start(bf16[1,4,64,256]{3,2,1,0:T(8,128)(2,1)S(1)} %collective-permute-done.1.refs_3_), channel_id=1, source_target_pairs={{0,1},{1,0},{2,3},{3,2},{4,5},{5,4},{6,7},{7,6},{8,9},{9,8},{10,11... | collective-permute-start | bytes 393224 | tf_op jit(solution)/shard_map/ppermute | solution.py:277
  33.5 19.9 %collective-permute-start.22 = (bf16[3,4,64,256]{3,2,1,0:T(8,128)(2,1)S(1)}, bf16[3,4,64,256]{3,2,1,0:T(8,128)(2,1)S(1)}, u32[]{:S(2)}, u32[]{:S(2)}) collective-permute-start(bf16[3,4,64,256]{3,2,1,0:T(8,128)(2,1)S(1)} %shard_map.56.refs_4_), channel_id=1, source_target_pairs={{0,1},{1,0},{2,3},{3,2},{4,5},{5,4},{6,7},{7,6},{8,9},{9,8},{10,11... | collective-permute-start | bytes 1179656 | tf_op jit(solution)/shard_map/ppermute | solution.py:277
  33.7 24.6 %collective-permute-start.15 = (bf16[3,4,64,256]{3,2,1,0:T(8,128)(2,1)S(1)}, bf16[3,4,64,256]{3,2,1,0:T(8,128)(2,1)S(1)}, u32[]{:S(2)}, u32[]{:S(2)}) collective-permute-start(bf16[3,4,64,256]{3,2,1,0:T(8,128)(2,1)S(1)} %collective-permute-done.13.refs_0_), channel_id=1, source_target_pairs={{0,1},{1,0},{2,3},{3,2},{4,5},{5,4},{6,7},{7,6},{8,9},{9,8},{10,11... | collective-permute-start | bytes 1179656 | tf_op jit(solution)/shard_map/ppermute | solution.py:277
  34.1 24.2 %collective-permute-start.16 = (bf16[3,4,64,256]{3,2,1,0:T(8,128)(2,1)S(1)}, bf16[3,4,64,256]{3,2,1,0:T(8,128)(2,1)S(1)}, u32[]{:S(2)}, u32[]{:S(2)}) collective-permute-start(bf16[3,4,64,256]{3,2,1,0:T(8,128)(2,1)S(1)} %collective-permute-done.14.refs_1_), channel_id=1, source_target_pairs={{0,1},{1,0},{2,3},{3,2},{4,5},{5,4},{6,7},{7,6},{8,9},{9,8},{10,11... | collective-permute-start | bytes 1179656 | tf_op jit(solution)/shard_map/ppermute | solution.py:277
  34.2 6.0 %collective-permute-start.2 = (bf16[1,4,64,256]{3,2,1,0:T(8,128)(2,1)S(1)}, bf16[1,4,64,256]{3,2,1,0:T(8,128)(2,1)S(1)}, u32[]{:S(2)}, u32[]{:S(2)}) collective-permute-start(bf16[1,4,64,256]{3,2,1,0:T(8,128)(2,1)S(1)} %collective-permute-done.1.refs_3_), channel_id=1, source_target_pairs={{0,8},{2,10},{4,12},{6,14},{8,0},{10,2},{12,4},{14,6},{16,24},{18,... | collective-permute-start | bytes 393224 | tf_op jit(solution)/shard_map/ppermute | solution.py:282
  40.2 12.7 %collective-permute-start.3 = (bf16[1,4,64,256]{3,2,1,0:T(8,128)(2,1)S(1)}, bf16[1,4,64,256]{3,2,1,0:T(8,128)(2,1)S(1)}, u32[]{:S(2)}, u32[]{:S(2)}) collective-permute-start(bf16[1,4,64,256]{3,2,1,0:T(8,128)(2,1)S(1)} %collective-permute-done.1.refs_3_), channel_id=1, source_target_pairs={{0,16},{2,18},{4,20},{6,22},{8,24},{10,26},{12,28},{14,30},{16,0},... | collective-permute-start | bytes 393224 | tf_op jit(solution)/shard_map/ppermute | solution.py:282
  42.9 10.0 %collective-permute-start.4 = (bf16[1,4,64,256]{3,2,1,0:T(8,128)(2,1)S(1)}, bf16[1,4,64,256]{3,2,1,0:T(8,128)(2,1)S(1)}, u32[]{:S(2)}, u32[]{:S(2)}) collective-permute-start(bf16[1,4,64,256]{3,2,1,0:T(8,128)(2,1)S(1)} %collective-permute-done.1.refs_3_), channel_id=1, source_target_pairs={{0,24},{2,26},{4,28},{6,30},{8,16},{10,18},{12,20},{14,22},{16,8},... | collective-permute-start | bytes 393224 | tf_op jit(solution)/shard_map/ppermute | solution.py:282
  52.9 7.2 %collective-permute-start.5 = (bf16[1,4,64,256]{3,2,1,0:T(8,128)(2,1)S(1)}, bf16[1,4,64,256]{3,2,1,0:T(8,128)(2,1)S(1)}, u32[]{:S(2)}, u32[]{:S(2)}) collective-permute-start(bf16[1,4,64,256]{3,2,1,0:T(8,128)(2,1)S(1)} %collective-permute-done.2.refs_0_), channel_id=1, source_target_pairs={{0,1},{1,0},{2,3},{3,2},{4,5},{5,4},{6,7},{7,6},{8,9},{9,8},{10,11... | collective-permute-start | bytes 393224 | tf_op jit(solution)/shard_map/ppermute | solution.py:277
  52.9 7.2 %collective-permute-start.6 = (bf16[1,4,64,256]{3,2,1,0:T(8,128)(2,1)S(1)}, bf16[1,4,64,256]{3,2,1,0:T(8,128)(2,1)S(1)}, u32[]{:S(2)}, u32[]{:S(2)}) collective-permute-start(bf16[1,4,64,256]{3,2,1,0:T(8,128)(2,1)S(1)} %collective-permute-done.3.refs_1_), channel_id=1, source_target_pairs={{0,1},{1,0},{2,3},{3,2},{4,5},{5,4},{6,7},{7,6},{8,9},{9,8},{10,11... | collective-permute-start | bytes 393224 | tf_op jit(solution)/shard_map/ppermute | solution.py:277
  53.4 6.7 %collective-permute-start.7 = (bf16[1,4,64,256]{3,2,1,0:T(8,128)(2,1)S(1)}, bf16[1,4,64,256]{3,2,1,0:T(8,128)(2,1)S(1)}, u32[]{:S(2)}, u32[]{:S(2)}) collective-permute-start(bf16[1,4,64,256]{3,2,1,0:T(8,128)(2,1)S(1)} %collective-permute-done.4.refs_2_), channel_id=1, source_target_pairs={{0,1},{1,0},{2,3},{3,2},{4,5},{5,4},{6,7},{7,6},{8,9},{9,8},{10,11... | collective-permute-start | bytes 393224 | tf_op jit(solution)/shard_map/ppermute | solution.py:277
  65.8 1.9 %collective-permute-start.23 = (f32[4,64,256]{2,1,0:T(8,128)S(1)}, f32[4,64,256]{2,1,0:T(8,128)S(1)}, u32[]{:S(2)}, u32[]{:S(2)}) collective-permute-start(f32[4,64,256]{2,1,0:T(8,128)S(1)} %get-tuple-element.16), channel_id=1, source_target_pairs={{0,1},{1,0},{2,3},{3,2},{4,5},{5,4},{6,7},{7,6},{8,9},{9,8},{10,11... | collective-permute-start | bytes 786440 | tf_op jit(solution)/shard_map/ppermute | solution.py:277
